TPU v7x, 128 devices: a whole 4x4x4 slice. The times are simulated.
128 devices in a mesh: dp: 16 (over x, z_hi, core), head: 8 (over z_lo, y).
Axes of the slice: x: 4, y: 4, z: 4 (z_hi: 2, z_lo: 2; z = z_hi * 2 + z_lo), core: 2. Of those that a mesh axis runs over, the one named last changes fastest.
Arguments:
- latent: bfloat16 [16384, 512], P(('dp', 'head')), may hold values from -32 to 32
- out_grad: bfloat16 [16384, 16, 8, 256], P('dp', None, 'head'), may hold values from -6 to 6
- weight: float32 [512, 16, 8, 256], P(None, 'dp', 'head'), may hold values from -0.25 to 0.25
- moment_one: float32 [512, 16, 8, 256], P(None, 'dp', 'head'), may hold values from -4 to 4
- moment_two: float32 [512, 16, 8, 256], P(None, 'dp', 'head'), may hold values from 0.1 to 2
Outputs:
- latent_grad: bfloat16 [16384, 512], P(('dp', 'head'))
- new_weight: float32 [512, 16, 8, 256], P(None, 'dp', 'head')
- new_moment_one: float32 [512, 16, 8, 256], P(None, 'dp', 'head')
- new_moment_two: float32 [512, 16, 8, 256], P(None, 'dp', 'head')
All inputs are finite; a program needn't handle non-finite values.
Results may differ from a plain program's by a relative error of at most 0.014.
Values may be sent and summed in bfloat16 or wider, within the bound.
No kernel may reach another device: no remote copies, remote signals or barrier semaphores. Data moves between devices by JAX's collectives and lax.ppermute only.
A program may use at most 128 MiB of HBM per device.

v0:
```python
import math

import jax
import jax.numpy as jnp
from jax import lax
from jax.sharding import PartitionSpec as P


def sent_to_all(x, axis):
    peers = lax.axis_size(axis)
    return lax.all_to_all(jnp.broadcast_to(x[None], (peers, *x.shape)), axis, 0, 0, tiled=True)


def laid_out(tiles, dim):
    tiles = jnp.moveaxis(tiles, 0, dim)
    dims = tiles.shape
    return tiles.reshape(*dims[:dim], dims[dim] * dims[dim + 1], *dims[dim + 2 :])


def gathered_copies(x, axis, dim):
    tiles = sent_to_all(x, axis)
    return laid_out(tiles, dim)


def in_blocks(x, dim, peers):
    dims = x.shape
    tiles = x.reshape(*dims[:dim], peers, dims[dim] // peers, *dims[dim + 1 :])
    return jnp.moveaxis(tiles, dim, 0)


def summed_on_arrival(x, axis, dim):
    tiles = in_blocks(x, dim, lax.axis_size(axis))
    arrived = lax.all_to_all(tiles, axis, split_axis=0, concat_axis=0, tiled=True)
    return arrived.astype(jnp.float32).sum(axis=0)


def hadamard(length):
    row_index = jnp.arange(length, dtype=jnp.int32)[:, None]
    col_index = jnp.arange(length, dtype=jnp.int32)[None, :]
    common = jnp.bitwise_and(row_index, col_index)
    parity = jnp.zeros((length, length), jnp.int32)
    for position in range(length.bit_length()):
        parity = parity + jnp.bitwise_and(jnp.right_shift(common, position), 1)
    sign_table = 1.0 - 2.0 * jnp.bitwise_and(parity, 1).astype(jnp.float32)
    return sign_table / math.sqrt(length)


def local(latent, out_grad, weight, moment_one, moment_two):
    dp_count = lax.axis_size("dp")
    latent_width = latent.shape[1]
    rotation = hadamard(latent_width)
    gathered = gathered_copies(latent, "head", 0)
    tokens_all = gathered.shape[0] * dp_count
    weight_half = weight.astype(jnp.bfloat16)
    grads_block = out_grad
    partial_value = jnp.einsum(
        "tahc,lahc->tl",
        grads_block,
        lax.all_gather(weight_half, "dp", axis=1, tiled=True),
        preferred_element_type=jnp.float32,
    )
    latent_grad = summed_on_arrival(partial_value.astype(jnp.bfloat16), "head", 0).astype(
        jnp.bfloat16
    )
    grads_block = out_grad
    partial_value = jnp.einsum(
        "tl,tahc->alc", gathered, grads_block, preferred_element_type=jnp.float32
    )
    rotated = jnp.einsum("ml,alc->amc", rotation, partial_value)
    spread = jnp.sqrt(jnp.mean(rotated * rotated, axis=1, keepdims=True) + 1e-06)
    outgoing = jnp.clip(rotated, -2.0 * spread, 2.0 * spread).astype(jnp.bfloat16)
    received = lax.all_to_all(outgoing, "dp", split_axis=0, concat_axis=0, tiled=True)
    summed = jnp.sum(received.astype(jnp.float32), axis=0)
    gradient = jnp.dot(rotation, summed) * tokens_all ** (-0.5)
    gradient = gradient.reshape(weight.shape)
    new_moment_one = 0.9 * moment_one + 0.1 * gradient
    new_moment_two = 0.95 * moment_two + 0.05 * gradient * gradient
    update = (
        new_moment_one / (1.0 - 0.9**10) / (jnp.sqrt(new_moment_two / (1.0 - 0.95**10)) + 1e-08)
    )
    new_weight = weight - 0.001 * (update + 0.1 * weight)
    return (latent_grad, new_weight, new_moment_one, new_moment_two)


def solution(mesh):
    placed = (
        P(("dp", "head"), None),
        P("dp", None, "head", None),
        P(None, "dp", "head", None),
        P(None, "dp", "head", None),
        P(None, "dp", "head", None),
    )
    return jax.shard_map(
        local,
        mesh=mesh,
        in_specs=placed,
        out_specs=(
            P(("dp", "head"), None),
            P(None, "dp", "head", None),
            P(None, "dp", "head", None),
            P(None, "dp", "head", None),
        ),
        check_vma=False,
    )
```

profile of v0, /device:TPU:1, one launch (start us, length us, event | category | flops | bytes accessed | tf_op | source)
XLA Modules:
  0.0 149.6 jit_solution(12734567798015555913)
XLA Ops:
  7.2 0.0 all-gather.2.cloned.1.call-start
  7.2 1.8 %copy.36 = bf16[512,1,1,256]{3,0,2,1:T(8,128)(2,1)} copy(f32[512,1,1,256]{3,2,1,0:T(1,128)} %param.7) | data formatting | bytes 786432 | tf_op args[2]
  9.0 0.0 all-gather.2.cloned.1.call-update
  9.0 2.0 %broadcast_in_dim.2 = bf16[8,128,512]{2,1,0:T(8,128)(2,1)} broadcast(bf16[128,512]{1,0:T(8,128)(2,1)} %param.5), dimensions={1,2} | broadcast | bytes 1179648 | tf_op jit(solution)/shard_map/broadcast_in_dim | solution.py:11
  11.0 6.4 %all-to-all-start.1 = ((bf16[8,128,512]{2,1,0:T(8,128)(2,1)}), bf16[8,128,512]{2,1,0:T(8,128)(2,1)S(1)}, u32[]{:S(2)}, u32[]{:S(2)}) async-start(bf16[8,128,512]{2,1,0:T(8,128)(2,1)} %broadcast_in_dim.2), calls=%async_computation.1 | async-start | bytes 2097152 | tf_op jit(solution)/shard_map/all_to_all | solution.py:11
  17.4 12.3 %copy.27 = bf16[1024,16,256]{0,2,1:T(8,128)(2,1)} copy(bf16[1024,16,256]{2,1,0:T(8,128)(2,1)} %bitcast.34) | data formatting | bytes 16777216 | tf_op jit(solution)/shard_map/reshape.1
  29.7 3.7 %all-to-all-done.1 = bf16[8,128,512]{2,1,0:T(8,128)(2,1)S(1)} async-done(((bf16[8,128,512]{2,1,0:T(8,128)(2,1)}), bf16[8,128,512]{2,1,0:T(8,128)(2,1)S(1)}, u32[]{:S(2)}, u32[]{:S(2)}) %all-to-all-start.1) | async-done | bytes 1048608 | tf_op jit(solution)/shard_map/all_to_all | solution.py:11
  33.4 12.4 %multiply_reduce_fusion = (f32[16,256]{1,0:T(8,128)S(1)}, bf16[16,256,512]{2,1,0:T(8,128)(2,1)}) fusion(bf16[1024,16,256]{0,2,1:T(8,128)(2,1)} %copy.27, bf16[1024,512,1]{1,0,2:T(8,128)(2,1)S(1)} %bitcast.35), kind=kOutput, calls=%fused_computation.4 | convolution fusion | flops 6457913344 | bytes 13647872 | tf_op jit(solution)/shard_map/ml,alc->amc/dot_general | solution.py:69
  45.8 4.2 %fusion.2 = bf16[16,512,256]{1,2,0:T(8,128)(2,1)} fusion(bf16[16,256,512]{2,1,0:T(8,128)(2,1)} %get-tuple-element.18, bf16[16,256]{1,0:T(8,128)(2,1)S(1)} %get-tuple-element.16, bf16[16,256]{1,0:T(8,128)(2,1)S(1)} %get-tuple-element.15), kind=kLoop, calls=%fused_computation.5 | loop fusion | flops 4194304 | bytes 8404992 | tf_op jit(solution)/shard_map/convert_element_type | solution.py:71
  49.9 8.2 %all-to-all-start.2 = ((bf16[16,512,256]{1,2,0:T(8,128)(2,1)}), bf16[16,512,256]{1,2,0:T(8,128)(2,1)}, u32[]{:S(2)}, u32[]{:S(2)}) async-start(bf16[16,512,256]{1,2,0:T(8,128)(2,1)} %fusion.2), calls=%async_computation.2 | async-start | bytes 8388608 | tf_op jit(solution)/shard_map/all_to_all | solution.py:72
  58.1 43.2 %all-gather.2.cloned.1.call-done = bf16[512,16,1,256]{3,0,2,1:T(8,128)(2,1)} async-done(((bf16[512,1,1,256]{3,0,2,1:T(8,128)(2,1)}), bf16[512,16,1,256]{3,0,2,1:T(8,128)(2,1)}) %all-gather.2.cloned.1.call-update) | async-done | bytes 4194320 | tf_op jit(solution)/shard_map/all_gather | solution.py:59
  101.3 10.1 %bitcast_convert_fusion = bf16[1024,512]{1,0:T(8,128)(2,1)} fusion(bf16[1024,16,256]{0,2,1:T(8,128)(2,1)} %copy.27, bf16[512,16,1,256]{3,0,2,1:T(8,128)(2,1)} %all-gather.2.cloned.1.call-done), kind=kOutput, calls=%fused_computation.8 | convolution fusion | flops 4295491584 | bytes 13631488 | tf_op jit(solution)/shard_map/tahc,lahc->tl/dot_general | solution.py:56
  111.4 0.0 copy-start
  111.4 0.0 copy-start.1
  111.4 0.0 copy-start.2
  111.4 4.1 %all-to-all-done.2 = bf16[16,512,256]{1,2,0:T(8,128)(2,1)} async-done(((bf16[16,512,256]{1,2,0:T(8,128)(2,1)}), bf16[16,512,256]{1,2,0:T(8,128)(2,1)}, u32[]{:S(2)}, u32[]{:S(2)}) %all-to-all-start.2) | async-done | bytes 4194336 | tf_op jit(solution)/shard_map/all_to_all | solution.py:72
  115.5 10.6 %all-to-all-start = ((bf16[8,128,512]{2,1,0:T(8,128)(2,1)}), bf16[8,128,512]{2,1,0:T(8,128)(2,1)S(1)}, u32[]{:S(2)}, u32[]{:S(2)}) async-start(bf16[8,128,512]{2,1,0:T(8,128)(2,1)} %bitcast.3), calls=%async_computation | async-start | bytes 2097152 | tf_op jit(solution)/shard_map/all_to_all | solution.py:33
  126.0 2.7 %convert_reduce_fusion = bf16[512,256]{0,1:T(8,128)(2,1)S(1)} fusion(bf16[16,512,256]{1,2,0:T(8,128)(2,1)} %all-to-all-done.2), kind=kLoop, calls=%fused_computation.2 | loop fusion | flops 4063232 | bytes 4456448 | tf_op jit(solution)/shard_map/reduce_sum | solution.py:73
  128.8 0.0 copy-done
  128.8 0.0 copy-done.1
  128.8 0.0 copy-done.2
  128.8 1.7 %multiply_subtract_fusion = (f32[512,1,1,256]{3,0,2,1:T(8,128)S(1)}, f32[512,1,1,256]{3,0,2,1:T(8,128)S(1)}, f32[512,1,1,256]{3,0,2,1:T(8,128)S(1)}) fusion(f32[512,1,1,256]{3,2,1,0:T(1,128)S(1)} %copy-done, f32[512,1,1,256]{3,2,1,0:T(1,128)S(1)} %copy-done.1, f32[512,1,1,256]{3,2,1,0:T(1,128)S(1)} %copy-done.2, bf16[512,256]{0,1:T(8,128)(2,1)S(1)} %convert_reduce_fusion), kind=kOutput, calls=%fused_computation.16 | convolution fusion | flops 145489920 | bytes 3407872 | tf_op jit(solution)/shard_map/dot_general | solution.py:74
  130.5 1.3 copy.24
  131.9 1.3 copy.25
  133.2 1.3 copy.26
  134.5 7.4 %all-to-all-done = bf16[8,128,512]{2,1,0:T(8,128)(2,1)S(1)} async-done(((bf16[8,128,512]{2,1,0:T(8,128)(2,1)}), bf16[8,128,512]{2,1,0:T(8,128)(2,1)S(1)}, u32[]{:S(2)}, u32[]{:S(2)}) %all-to-all-start) | async-done | bytes 1048608 | tf_op jit(solution)/shard_map/all_to_all | solution.py:33
  141.9 0.8 reduce_sum.34
  (1 shorter events, 0.0 us)
Async XLA Ops:
  7.2 94.1 %all-gather.2.cloned.1.call-start = ((), (), s32[]{:S(2)}) async-start(), calls=%async_computation.3 | async-start | bytes 4456448 | tf_op jit(solution)/shard_map/all_gather | solution.py:59
  11.0 22.3 %all-to-all-start.1 = ((bf16[8,128,512]{2,1,0:T(8,128)(2,1)}), bf16[8,128,512]{2,1,0:T(8,128)(2,1)S(1)}, u32[]{:S(2)}, u32[]{:S(2)}) async-start(bf16[8,128,512]{2,1,0:T(8,128)(2,1)} %broadcast_in_dim.2), calls=%async_computation.1 | async-start | bytes 2097152 | tf_op jit(solution)/shard_map/all_to_all | solution.py:11
  49.9 65.5 %all-to-all-start.2 = ((bf16[16,512,256]{1,2,0:T(8,128)(2,1)}), bf16[16,512,256]{1,2,0:T(8,128)(2,1)}, u32[]{:S(2)}, u32[]{:S(2)}) async-start(bf16[16,512,256]{1,2,0:T(8,128)(2,1)} %fusion.2), calls=%async_computation.2 | async-start | bytes 8388608 | tf_op jit(solution)/shard_map/all_to_all | solution.py:72
  111.4 17.4 %copy-start = (f32[512,1,1,256]{3,2,1,0:T(1,128)S(1)}, f32[512,1,1,256]{3,2,1,0:T(1,128)}, u32[]{:S(2)}) copy-start(f32[512,1,1,256]{3,2,1,0:T(1,128)} %param.7) | copy-start | bytes 1572868
  111.4 17.4 %copy-start.1 = (f32[512,1,1,256]{3,2,1,0:T(1,128)S(1)}, f32[512,1,1,256]{3,2,1,0:T(1,128)}, u32[]{:S(2)}) copy-start(f32[512,1,1,256]{3,2,1,0:T(1,128)} %param.8) | copy-start | bytes 1572868
  111.4 17.4 %copy-start.2 = (f32[512,1,1,256]{3,2,1,0:T(1,128)S(1)}, f32[512,1,1,256]{3,2,1,0:T(1,128)}, u32[]{:S(2)}) copy-start(f32[512,1,1,256]{3,2,1,0:T(1,128)} %param.9) | copy-start | bytes 1572868
  115.5 26.4 %all-to-all-start = ((bf16[8,128,512]{2,1,0:T(8,128)(2,1)}), bf16[8,128,512]{2,1,0:T(8,128)(2,1)S(1)}, u32[]{:S(2)}, u32[]{:S(2)}) async-start(bf16[8,128,512]{2,1,0:T(8,128)(2,1)} %bitcast.3), calls=%async_computation | async-start | bytes 2097152 | tf_op jit(solution)/shard_map/all_to_all | solution.py:33
Sparse Core Ops, SparseCore 0:
  10.9 90.3 all-gather.1
where the time goes:
time: 150 us
  waiting for transfers between devices  58.3 us (39%)
  starting transfers between devices  25.1 us (17%)
  matrix products  24.1 us (16%)
  local copies, waits for them, and re-layouts  20.1 us (13%)
  between operations  14.1 us (9%)
  other arithmetic  7.77 us (5%)
    all_gather x1, waiting for transfers between devices, local(): lax.all_gather(weight_half, 'dp', axis=1, tiled=True)  43.2 us
    dot_general x1, matrix products, local(): rotated = jnp.einsum('ml,alc->amc', rotation, partial_value)  12.4 us
    another operation x1, local copies, waits for them, and re-layouts  12.3 us
    all_to_all x1, starting transfers between devices, summed_on_arrival(): lax.all_to_all(tiles, axis, split_axis=0, concat_axis=0, tiled=True)  10.6 us
    dot_general x1, matrix products, local(): jnp.einsum('tahc,lahc->tl', grads_block, lax.all_gather(weight_half, 'dp'...  10.1 us
    all_to_all x1, starting transfers between devices, local(): lax.all_to_all(outgoing, 'dp', split_axis=0, concat_axis=0, tiled=True)  8.16 us
    all_to_all x1, waiting for transfers between devices, summed_on_arrival(): lax.all_to_all(tiles, axis, split_axis=0, concat_axis=0, tiled=True)  7.4 us
    all_to_all x1, starting transfers between devices, sent_to_all(): lax.all_to_all(jnp.broadcast_to(x[None], (peers, *x.shape)), axis, 0, 0,...  6.36 us
  transfers between devices with their start and end apart: 4, of which 4 were waited for; matrix products, arithmetic and copies ran while one was open for 33% of the time, Pallas kernels for 0%

commit v1 on v0

v1 whole, which is shorter than its diff:
```python
import math

import jax
import jax.numpy as jnp
import numpy as np
from jax import lax
from jax.experimental import pallas as pl
from jax.experimental.pallas import tpu as pltpu
from jax.sharding import PartitionSpec as P


LATENT = 512
COLS = 256
NX, NZH, NC = 4, 2, 2
NZL, NY = 2, 4
TOK = 1024
TOKENS = 16384
BF = jnp.bfloat16
F32 = jnp.float32
VM = pl.BlockSpec(memory_space=pltpu.VMEM)
AXES = ("dp", "head")
EARLY = ((1, 1), (3, 1), (2, 1))
LATE = ((1, 0), (3, 0), (2, 0), (0, 1), (0, 0))
ORDER = ((0, 0), (1, 0), (3, 0), (2, 0), (0, 1), (1, 1), (3, 1), (2, 1))


def signs(length):
    i = np.arange(length)
    common = i[:, None] & i[None, :]
    parity = np.zeros_like(common)
    for position in range(length.bit_length()):
        parity += (common >> position) & 1
    return jnp.asarray(1 - 2 * (parity & 1), BF)


def shifted(value, dx=0, dz=0, dc=0, dl=0, dy=0):
    sizes = (NX, NZH, NC, NZL, NY)
    steps = (dx, dz, dc, dl, dy)
    pairs = []
    for source, place in enumerate(np.ndindex(*sizes)):
        target = [(p + d) % n for p, d, n in zip(place, steps, sizes)]
        pairs.append((source, int(np.ravel_multi_index(target, sizes))))
    return lax.ppermute(value, AXES, pairs)


def kernel(body, outs, count, grid=None, in_specs=None, limit=16, home=False):
    shape_of = jax.ShapeDtypeStruct if home else pltpu.VMEM
    return pl.pallas_call(
        body,
        grid=grid or (),
        in_specs=in_specs or [VM] * count,
        out_specs=[VM] * len(outs),
        out_shape=[shape_of(shape, dtype) for shape, dtype in outs],
        compiler_params=pltpu.CompilerParams(vmem_limit_bytes=limit << 20),
    )


def group_of(dx, dz, dc):
    me = lax.axis_index("dp")
    x, zh, c = me // (NZH * NC), lax.rem(me // NC, NZH), lax.rem(me, NC)
    return (lax.rem(x + dx, NX) * NZH + lax.rem(zh + dz, NZH)) * NC + lax.rem(c + dc, NC)


def halve_body(w_ref, o_ref):
    for half in range(2):
        rows = w_ref[pl.ds(half, LATENT, stride=2), :]
        o_ref[:, half * 128 : half * 128 + 128] = rows.astype(BF)


def swap_body(g_ref, o_ref):
    tile = g_ref.shape[0]
    at = pl.multiple_of(pl.program_id(0) * tile, tile)
    o_ref[:, pl.ds(at, tile), :] = jnp.swapaxes(g_ref[...], 0, 1)


def rotate_body(h_ref, l_ref, o_ref):
    rows = l_ref[...].reshape(TOK, LATENT)
    turned = lax.dot_general(h_ref[...], rows, (((1,), (1,)), ((), ())), preferred_element_type=F32)
    o_ref[...] = (turned * (1.0 / math.sqrt(LATENT))).astype(BF)


def turned_block(l_ref, g_ref, block):
    value = jnp.dot(l_ref[...], g_ref[block], preferred_element_type=F32)
    spread = 2.0 * jnp.sqrt(jnp.mean(value * value, axis=0, keepdims=True) + 1e-06)
    return jnp.clip(value, -spread, spread).astype(BF)


def give_body(places):
    def body(g_ref, l_ref, o_ref):
        for at, (dx, dz) in enumerate(places):
            o_ref[at] = turned_block(l_ref, g_ref, group_of(dx, dz, 1))

    return body


def keep_body(places):
    def body(g_ref, l_ref, r_ref, *o_refs):
        for at, ((dx, dz), o_ref) in enumerate(zip(places, o_refs)):
            mine = turned_block(l_ref, g_ref, group_of(dx, dz, 0)).astype(F32)
            o_ref[...] = (mine + r_ref[at].astype(F32)).astype(o_ref.dtype)

    return body


def latent_body(g_ref, *refs):
    w_refs, o_ref = refs[:16], refs[16]
    for part in range(2):
        total = None
        for at, (dx, dz) in enumerate(ORDER):
            for dc in range(2):
                term = lax.dot_general(
                    g_ref[group_of(dx, dz, dc), part * 512 : part * 512 + 512],
                    w_refs[2 * at + dc][...],
                    (((1,), (1,)), ((), ())),
                    preferred_element_type=F32,
                )
                total = term if total is None else total + term
        o_ref[part * 4 : part * 4 + 4] = total.astype(BF).reshape(4, 128, LATENT)


def update_body(h_ref, own, d_up, d_down, over, far, w_ref, a_ref, b_ref, nw_ref, na_ref, nb_ref):
    summed = own[...] + d_up[...].astype(F32) + d_down[...].astype(F32)
    summed = summed + over[...].astype(F32) + far[...].astype(F32)
    high = summed.astype(BF)
    low = (summed - high.astype(F32)).astype(BF)
    h = h_ref[...]
    grad = jnp.dot(h, high, preferred_element_type=F32) + jnp.dot(h, low, preferred_element_type=F32)
    grad = grad * (TOKENS ** (-0.5) / math.sqrt(LATENT))
    for half in range(2):
        rows = pl.ds(half, LATENT, stride=2)
        g = grad[:, half * 128 : half * 128 + 128]
        one = 0.9 * a_ref[rows, :] + 0.1 * g
        two = 0.95 * b_ref[rows, :] + 0.05 * g * g
        step = one / (1.0 - 0.9**10) / (jnp.sqrt(two / (1.0 - 0.95**10)) + 1e-08)
        w = w_ref[rows, :]
        na_ref[rows, :] = one
        nb_ref[rows, :] = two
        nw_ref[rows, :] = w - 0.001 * (step + 0.1 * w)


def join_body(*refs):
    total = refs[0][...].astype(F32)
    for r in refs[1:-1]:
        total = total + r[...].astype(F32)
    refs[-1][...] = total.astype(BF)


def run(body, outs, *operands, **more):
    return kernel(body, outs, len(operands), **more)(*operands)


def send(value, **steps):
    return shifted(value, **steps)


def step(latent, out_grad, weight, moment_one, moment_two):
    h = signs(LATENT)
    flat = (1024, 128)
    block = (LATENT, COLS)
    one = [(block, BF)]
    peers = NZL * NY

    rows = jnp.broadcast_to(latent[None], (peers, *latent.shape))
    rows = lax.all_to_all(rows, "head", 0, 0, tiled=True)

    (w0,) = run(halve_body, one, weight.reshape(flat))
    w = {(0, 0): w0}
    w[0, 1] = send(w0, dz=1)
    w[2, 0] = send(w0, dx=2)
    w[3, 0] = send(w0, dx=1)
    w[1, 0] = send(w0, dx=-1)
    w[3, 1] = send(w[0, 1], dx=1)
    w[1, 1] = send(w[0, 1], dx=-1)
    w[2, 1] = send(w[2, 0], dz=1)
    ws = []
    for place in ORDER:
        ws += [w[place], send(w[place], dc=1)]

    tile = 128
    (grads,) = run(
        swap_body,
        [((16, TOK, COLS), BF)],
        out_grad[:, :, 0, :],
        grid=(TOK // tile,),
        in_specs=[pl.BlockSpec((tile, 16, COLS), lambda i: (i, 0, 0))],
        limit=24,
    )

    (turn,) = run(rotate_body, [((LATENT, TOK), BF)], h, rows)
    (give,) = run(give_body(EARLY), [((3, *block), BF)], grads, turn)
    got_early = send(give, dc=1)
    (give,) = run(give_body(LATE), [((5, *block), BF)], grads, turn)
    got_late = send(give, dc=1)
    up, down, other = run(keep_body(EARLY), one * 3, grads, turn, got_early)
    up = send(up, dx=1)
    down = send(down, dx=-1)
    other = send(other, dz=1)
    d_up, d_down, far, over, own = run(
        keep_body(LATE), one * 2 + [(block, F32)] * 3, grads, turn, got_late
    )
    d_up = send(d_up, dx=1)
    d_down = send(d_down, dx=-1)
    (over,) = run(join_body, one, over, up, down)
    over = send(over, dz=1)
    (far,) = run(join_body, one, far, other)
    far = send(far, dx=2)

    (partial,) = run(latent_body, [((peers, 128, LATENT), BF)], grads, *ws)
    arrived = lax.all_to_all(partial, "head", 0, 0, tiled=True)
    latent_grad = arrived.astype(F32).sum(axis=0).astype(BF)

    states = [s.reshape(flat) for s in (weight, moment_one, moment_two)]
    new = run(
        update_body, [(flat, F32)] * 3, h, own, d_up, d_down, over, far, *states,
        limit=24, home=True,
    )
    new = [n.reshape(weight.shape) for n in new]
    return (latent_grad, *new)


def solution(mesh):
    state = P(None, "dp", "head", None)
    return jax.shard_map(
        step,
        mesh=mesh,
        in_specs=(P(("dp", "head"), None), P("dp", None, "head", None), state, state, state),
        out_specs=(P(("dp", "head"), None), state, state, state),
        check_vma=False,
    )
```

time: 150 us -> 106 us (0.71)
  waiting for transfers between devices: 58.3 us -> 12.3 us
  matrix products: 24.1 us -> 0 us
  starting transfers between devices: 25.1 us -> 48.6 us
  Pallas kernels: 0 us -> 23.1 us
  between operations: 14.1 us -> 0.79 us
  other arithmetic: 7.77 us -> 2.06 us
  local copies, waits for them, and re-layouts: 20.1 us -> 18.3 us
    all_gather x1 -> x0, waiting for transfers between devices: 43.2 us -> none  [local(): lax.all_gather(weight_half, 'dp', axis=1, tiled=True)]
    ppermute x0 -> x24, starting transfers between devices: none -> 37.4 us  [shifted(): return lax.ppermute(value, AXES, pairs)]
    dot_general x3 -> x0, matrix products: 24.1 us -> none  [the longest x1 12.4 us: local(): rotated = jnp.einsum('ml,alc->amc', rotation, partial_value)]
    pallas_call x0 -> x11, Pallas kernels: none -> 23.1 us  [run(): return kernel(body, outs, len(operands), **more)(*operands)]
    all_to_all x3 -> x2, waiting for transfers between devices: 15.1 us -> 0.01 us  [the longest x1 0.01 us: step(): rows = lax.all_to_all(rows, 'head', 0, 0, tiled=True)]
    all_to_all x3 -> x2, starting transfers between devices: 25.1 us -> 11.2 us  [the longest x1 6.36 us: step(): rows = lax.all_to_all(rows, 'head', 0, 0, tiled=True)]
    ppermute x0 -> x24, waiting for transfers between devices: none -> 12.3 us  [shifted(): return lax.ppermute(value, AXES, pairs)]
    another operation x1 -> x0, local copies, waits for them, and re-layouts: 12.3 us -> none
  transfers between devices with their start and end apart: 4 -> 26, of which waited for: 4 -> 6; matrix products, arithmetic and copies ran while one was open for 33% -> 2% of each run, Pallas kernels for 0% -> 20%
where the time goes in v1:
time: 106 us; the launch traced here: 105 us
  starting transfers between devices  48.6 us (46%)
  Pallas kernels  23.1 us (22%)
  local copies, waits for them, and re-layouts  18.3 us (17%)
  waiting for transfers between devices  12.3 us (12%)
  other arithmetic  2.06 us (2%)
    ppermute x24, starting transfers between devices, shifted(): return lax.ppermute(value, AXES, pairs)  37.4 us
    pallas_call x11, Pallas kernels, run(): return kernel(body, outs, len(operands), **more)(*operands)  23.1 us
    unnamed x22, local copies, waits for them, and re-layouts  16.3 us
    ppermute x24, waiting for transfers between devices, shifted(): return lax.ppermute(value, AXES, pairs)  12.3 us
    all_to_all x1, starting transfers between devices, step(): rows = lax.all_to_all(rows, 'head', 0, 0, tiled=True)  6.36 us
    all_to_all x1, starting transfers between devices, step(): arrived = lax.all_to_all(partial, 'head', 0, 0, tiled=True)  4.8 us
  transfers between devices with their start and end apart: 26, of which 6 were waited for; matrix products, arithmetic and copies ran while one was open for 2% of the time, Pallas kernels for 20%

profile of v1, /device:TPU:1, one launch (start us, length us, event | category | flops | bytes accessed | tf_op | source)
XLA Modules:
  0.0 105.2 jit_solution(1127259379863353020)
XLA Ops:
  0.6 2.0 %broadcast_in_dim.2 = bf16[8,128,512]{2,1,0:T(8,128)(2,1)} broadcast(bf16[128,512]{1,0:T(8,128)(2,1)} %param.6), dimensions={1,2} | broadcast | bytes 1179648 | tf_op jit(solution)/shard_map/broadcast_in_dim | solution.py:163
  2.6 6.4 %all-to-all-start.1 = ((bf16[8,128,512]{2,1,0:T(8,128)(2,1)}), bf16[8,128,512]{2,1,0:T(8,128)(2,1)S(1)}, u32[]{:S(2)}, u32[]{:S(2)}) async-start(bf16[8,128,512]{2,1,0:T(8,128)(2,1)} %broadcast_in_dim.2), calls=%async_computation.1 | async-start | bytes 2097152 | tf_op jit(solution)/shard_map/all_to_all | solution.py:164
  9.0 1.0 copy-done.5
  10.1 2.5 %collective-permute-start.1 = (bf16[512,256]{1,0:T(8,128)(2,1)S(1)}, bf16[512,256]{1,0:T(8,128)(2,1)S(1)}, u32[]{:S(2)}, u32[]{:S(2)}) collective-permute-start(bf16[512,256]{1,0:T(8,128)(2,1)S(1)} %shard_map.94.refs_0_), channel_id=1, source_target_pairs={{0,96},{1,97},{2,98},{3,99},{4,100},{5,101},{6,102},{7,103},{8,104... | collective-permute-start | bytes 786440 | tf_op jit(solution)/shard_map/ppermute | solution.py:43
  12.6 0.0 collective-permute-start.3
  12.6 1.7 %collective-permute-start.5 = (bf16[512,256]{1,0:T(8,128)(2,1)S(1)}, bf16[512,256]{1,0:T(8,128)(2,1)}, u32[]{:S(2)}, u32[]{:S(2)}) collective-permute-start(bf16[512,256]{1,0:T(8,128)(2,1)S(1)} %shard_map.94.refs_0_), channel_id=1, source_target_pairs={{0,64},{1,65},{2,66},{3,67},{4,68},{5,69},{6,70},{7,71},{8,72},{9,... | collective-permute-start | bytes 786440 | tf_op jit(solution)/shard_map/ppermute | solution.py:43
  14.4 1.8 %collective-permute-start = (bf16[512,256]{1,0:T(8,128)(2,1)S(1)}, bf16[512,256]{1,0:T(8,128)(2,1)}, u32[]{:S(2)}, u32[]{:S(2)}) collective-permute-start(bf16[512,256]{1,0:T(8,128)(2,1)S(1)} %shard_map.94.refs_0_), channel_id=1, source_target_pairs={{0,8},{1,9},{2,10},{3,11},{4,12},{5,13},{6,14},{7,15},{8,0},{9,1},... | collective-permute-start | bytes 786440 | tf_op jit(solution)/shard_map/ppermute | solution.py:43
  16.1 3.3 %collective-permute-start.7 = (bf16[512,256]{1,0:T(8,128)(2,1)S(1)}, bf16[512,256]{1,0:T(8,128)(2,1)}, u32[]{:S(2)}, u32[]{:S(2)}) collective-permute-start(bf16[512,256]{1,0:T(8,128)(2,1)S(1)} %shard_map.94.refs_0_), channel_id=1, source_target_pairs={{0,16},{1,17},{2,18},{3,19},{4,20},{5,21},{6,22},{7,23},{8,24},{9,... | collective-permute-start | bytes 786440 | tf_op jit(solution)/shard_map/ppermute | solution.py:43
  19.5 0.0 collective-permute-done.1.refs_2_
  19.5 5.3 %collective-permute-start.2 = (bf16[512,256]{1,0:T(8,128)(2,1)S(1)}, bf16[512,256]{1,0:T(8,128)(2,1)}, u32[]{:S(2)}, u32[]{:S(2)}) collective-permute-start(bf16[512,256]{1,0:T(8,128)(2,1)S(1)} %collective-permute-done.1.refs_2_), channel_id=1, source_target_pairs={{0,8},{1,9},{2,10},{3,11},{4,12},{5,13},{6,14},{7,15},{8,0},{9,1},... | collective-permute-start | bytes 786440 | tf_op jit(solution)/shard_map/ppermute | solution.py:43
  24.8 3.4 %collective-permute-start.4 = (bf16[512,256]{1,0:T(8,128)(2,1)S(1)}, bf16[512,256]{1,0:T(8,128)(2,1)}, u32[]{:S(2)}, u32[]{:S(2)}) collective-permute-start(bf16[512,256]{1,0:T(8,128)(2,1)S(1)} %collective-permute-done.3.refs_4_), channel_id=1, source_target_pairs={{0,8},{1,9},{2,10},{3,11},{4,12},{5,13},{6,14},{7,15},{8,0},{9,1},... | collective-permute-start | bytes 786440 | tf_op jit(solution)/shard_map/ppermute | solution.py:43
  28.2 0.0 collective-permute-start.6
  28.2 3.4 %copy-done.3 = bf16[1024,16,1,256]{3,1,2,0:T(8,128)(2,1)S(1)} copy-done((bf16[1024,16,1,256]{3,1,2,0:T(8,128)(2,1)S(1)}, bf16[1024,16,1,256]{3,1,2,0:T(8,128)(2,1)}, u32[]{:S(2)}) %copy-start.3) | copy-done | bytes 8388632
  31.6 2.2 %shard_map.93.g_ref = bf16[16,1024,256]{2,1,0:T(8,128)(2,1)S(1)} custom-call(bf16[1024,16,256]{2,1,0:T(8,128)(2,1)S(1)} %bitcast.7), custom_call_target="tpu_custom_call" | custom-call | tf_op jit(solution)/shard_map/pallas_call | solution.py:149
  33.8 3.3 %copy-done = bf16[16,1024,256]{2,1,0:T(8,128)(2,1)} copy-done((bf16[16,1024,256]{2,1,0:T(8,128)(2,1)}, bf16[16,1024,256]{2,1,0:T(8,128)(2,1)S(1)}, u32[]{:S(2)}) %copy-start) | copy-done | bytes 8388632
  37.1 0.0 all-to-all-done.1.l_ref
  37.1 0.7 shard_map.96.l_ref
  37.8 3.4 %copy-done.1 = bf16[16,1024,256]{2,1,0:T(8,128)(2,1)S(1)} copy-done((bf16[16,1024,256]{2,1,0:T(8,128)(2,1)S(1)}, bf16[16,1024,256]{2,1,0:T(8,128)(2,1)}, u32[]{:S(2)}) %copy-start.1) | copy-done | bytes 8388632
  41.2 3.0 %shard_map.97 = bf16[5,512,256]{2,1,0:T(8,128)(2,1)} custom-call(bf16[16,1024,256]{2,1,0:T(8,128)(2,1)S(1)} %copy-done.1, bf16[512,1024]{1,0:T(8,128)(2,1)S(1)} %shard_map.96.l_ref), custom_call_target="tpu_custom_call" | custom-call | tf_op jit(solution)/shard_map/pallas_call | solution.py:149
  44.2 0.5 collective-permute-start.15
  44.7 0.0 collective-permute-done.7.refs_8_
  44.7 0.1 collective-permute-start.8
  44.8 0.0 collective-permute-done.2.refs_3_
  44.8 0.4 collective-permute-start.9
  45.2 1.0 collective-permute-start.11
  46.3 3.3 %collective-permute-start.13 = (bf16[512,256]{1,0:T(8,128)(2,1)}, bf16[512,256]{1,0:T(8,128)(2,1)S(1)}, u32[]{:S(2)}, u32[]{:S(2)}) collective-permute-start(bf16[512,256]{1,0:T(8,128)(2,1)} %collective-permute-done.5.refs_6_), channel_id=1, source_target_pairs={{0,16},{1,17},{2,18},{3,19},{4,20},{5,21},{6,22},{7,23},{8,24},{9,... | collective-permute-start | bytes 786440 | tf_op jit(solution)/shard_map/ppermute | solution.py:43
  49.6 2.1 %shard_map.99 = bf16[3,512,256]{2,1,0:T(8,128)(2,1)} custom-call(bf16[16,1024,256]{2,1,0:T(8,128)(2,1)S(1)} %copy-done.1, bf16[512,1024]{1,0:T(8,128)(2,1)S(1)} %shard_map.96.l_ref), custom_call_target="tpu_custom_call" | custom-call | tf_op jit(solution)/shard_map/pallas_call | solution.py:149
  51.7 1.3 %collective-permute-start.18 = (bf16[3,512,256]{2,1,0:T(8,128)(2,1)}, bf16[3,512,256]{2,1,0:T(8,128)(2,1)S(1)}, u32[]{:S(2)}, u32[]{:S(2)}) collective-permute-start(bf16[3,512,256]{2,1,0:T(8,128)(2,1)} %shard_map.99), channel_id=1, source_target_pairs={{0,8},{1,9},{2,10},{3,11},{4,12},{5,13},{6,14},{7,15},{8,0},{9,1},... | collective-permute-start | bytes 2359304 | tf_op jit(solution)/shard_map/ppermute | solution.py:43
  53.0 0.8 collective-permute-start.10
  53.7 0.4 collective-permute-done.11.refs_12_
  54.2 1.2 %collective-permute-start.12 = (bf16[512,256]{1,0:T(8,128)(2,1)S(1)}, bf16[512,256]{1,0:T(8,128)(2,1)S(1)}, u32[]{:S(2)}, u32[]{:S(2)}) collective-permute-start(bf16[512,256]{1,0:T(8,128)(2,1)S(1)} %collective-permute-done.11.refs_12_), channel_id=1, source_target_pairs={{0,8},{1,9},{2,10},{3,11},{4,12},{5,13},{6,14},{7,15},{8,0},{9,1},... | collective-permute-start | bytes 786440 | tf_op jit(solution)/shard_map/ppermute | solution.py:43
  55.4 0.1 collective-permute-done.13.refs_14_
  55.5 1.6 %collective-permute-start.14 = (bf16[512,256]{1,0:T(8,128)(2,1)S(1)}, bf16[512,256]{1,0:T(8,128)(2,1)S(1)}, u32[]{:S(2)}, u32[]{:S(2)}) collective-permute-start(bf16[512,256]{1,0:T(8,128)(2,1)S(1)} %collective-permute-done.13.refs_14_), channel_id=1, source_target_pairs={{0,8},{1,9},{2,10},{3,11},{4,12},{5,13},{6,14},{7,15},{8,0},{9,1},... | collective-permute-start | bytes 786440 | tf_op jit(solution)/shard_map/ppermute | solution.py:43
  57.1 0.0 collective-permute-done.10.refs_11_
  57.1 0.0 collective-permute-done.12.refs_13_
  57.1 1.2 %collective-permute-done.14.refs_15_ = bf16[512,256]{1,0:T(8,128)(2,1)S(1)} collective-permute-done((bf16[512,256]{1,0:T(8,128)(2,1)S(1)}, bf16[512,256]{1,0:T(8,128)(2,1)S(1)}, u32[]{:S(2)}, u32[]{:S(2)}) %collective-permute-start.14) | collective-permute-done | bytes 262176 | tf_op jit(solution)/shard_map/ppermute | solution.py:43
  58.2 6.9 %shard_map.95 = bf16[8,128,512]{2,1,0:T(8,128)(2,1)} custom-call(bf16[16,1024,256]{2,1,0:T(8,128)(2,1)S(1)} %copy-done.1, bf16[512,256]{1,0:T(8,128)(2,1)S(1)} %shard_map.94.refs_0_, bf16[512,256]{1,0:T(8,128)(2,1)} %collective-permute-done.refs_1_, bf16[512,256]{1,0:T(8,128)(2,1)S(1)} %collective-permute-done.1.refs_2_, ...), custom_call_target="tpu_custom_call" | custom-call | tf_op jit(solution)/shard_map/pallas_call | solution.py:149
  65.1 4.8 %all-to-all-start = ((bf16[8,128,512]{2,1,0:T(8,128)(2,1)}), bf16[8,128,512]{2,1,0:T(8,128)(2,1)}, u32[]{:S(2)}, u32[]{:S(2)}) async-start(bf16[8,128,512]{2,1,0:T(8,128)(2,1)} %shard_map.95), calls=%async_computation | async-start | bytes 2097152 | tf_op jit(solution)/shard_map/all_to_all | solution.py:209
  69.9 0.0 collective-permute-done.18.r_ref
  69.9 3.4 %copy-done.2 = bf16[16,1024,256]{2,1,0:T(8,128)(2,1)S(1)} copy-done((bf16[16,1024,256]{2,1,0:T(8,128)(2,1)S(1)}, bf16[16,1024,256]{2,1,0:T(8,128)(2,1)}, u32[]{:S(2)}) %copy-start.2) | copy-done | bytes 8388632
  73.3 1.6 %shard_map.100 = (bf16[512,256]{1,0:T(8,128)(2,1)S(1)}, bf16[512,256]{1,0:T(8,128)(2,1)S(1)}, bf16[512,256]{1,0:T(8,128)(2,1)S(1)}) custom-call(bf16[16,1024,256]{2,1,0:T(8,128)(2,1)S(1)} %copy-done.2, bf16[512,1024]{1,0:T(8,128)(2,1)S(1)} %shard_map.96.l_ref, bf16[3,512,256]{2,1,0:T(8,128)(2,1)S(1)} %collective-permute-done.18.r_ref), custom_call_target="tpu_custom_call" | custom-call | tf_op jit(solution)/shard_map/pallas_call | solution.py:149
  74.9 0.0 copy-start.6
  74.9 0.0 copy-start.7
  74.9 0.0 copy-start.8
  74.9 0.1 collective-permute-start.19
  75.1 2.6 %collective-permute-start.20 = (bf16[512,256]{1,0:T(8,128)(2,1)S(1)}, bf16[512,256]{1,0:T(8,128)(2,1)S(1)}, u32[]{:S(2)}, u32[]{:S(2)}) collective-permute-start(bf16[512,256]{1,0:T(8,128)(2,1)S(1)} %get-tuple-element.20), channel_id=1, source_target_pairs={{0,96},{1,97},{2,98},{3,99},{4,100},{5,101},{6,102},{7,103},{8,104... | collective-permute-start | bytes 786440 | tf_op jit(solution)/shard_map/ppermute | solution.py:43
  77.7 3.3 %collective-permute-start.22 = (bf16[512,256]{1,0:T(8,128)(2,1)S(1)}, bf16[512,256]{1,0:T(8,128)(2,1)S(1)}, u32[]{:S(2)}, u32[]{:S(2)}) collective-permute-start(bf16[512,256]{1,0:T(8,128)(2,1)S(1)} %get-tuple-element.22), channel_id=1, source_target_pairs={{0,16},{1,17},{2,18},{3,19},{4,20},{5,21},{6,22},{7,23},{8,24},{9,... | collective-permute-start | bytes 786440 | tf_op jit(solution)/shard_map/ppermute | solution.py:43
  81.0 0.0 collective-permute-done.15.r_ref
  81.0 3.7 %shard_map.98 = (bf16[512,256]{1,0:T(8,128)(2,1)}, bf16[512,256]{1,0:T(8,128)(2,1)}, f32[512,256]{1,0:T(8,128)S(1)}, f32[512,256]{1,0:T(8,128)S(1)}, f32[512,256]{1,0:T(8,128)S(1)}) custom-call(bf16[16,1024,256]{2,1,0:T(8,128)(2,1)S(1)} %copy-done.2, bf16[512,1024]{1,0:T(8,128)(2,1)S(1)} %shard_map.96.l_ref, bf16[5,512,256]{2,1,0:T(8,128)(2,1)} %collective-permute-done.15.r_ref), custom_call_target="tpu_custom_call" | custom-call | tf_op jit(solution)/shard_map/pallas_call | solution.py:149
  84.7 0.0 copy-start.9
  84.7 0.8 copy-done.9
  85.5 2.7 %collective-permute-start.17 = (bf16[512,256]{1,0:T(8,128)(2,1)}, bf16[512,256]{1,0:T(8,128)(2,1)S(1)}, u32[]{:S(2)}, u32[]{:S(2)}) collective-permute-start(bf16[512,256]{1,0:T(8,128)(2,1)} %get-tuple-element.17), channel_id=1, source_target_pairs={{0,96},{1,97},{2,98},{3,99},{4,100},{5,101},{6,102},{7,103},{8,104... | collective-permute-start | bytes 786440 | tf_op jit(solution)/shard_map/ppermute | solution.py:43
  88.2 0.0 collective-permute-done.19.refs_1_
  88.2 0.1 shard_map.101
  88.3 0.1 collective-permute-start.21
  88.4 3.9 %collective-permute-done.22.refs_1_ = bf16[512,256]{1,0:T(8,128)(2,1)S(1)} collective-permute-done((bf16[512,256]{1,0:T(8,128)(2,1)S(1)}, bf16[512,256]{1,0:T(8,128)(2,1)S(1)}, u32[]{:S(2)}, u32[]{:S(2)}) %collective-permute-start.22) | collective-permute-done | bytes 262176 | tf_op jit(solution)/shard_map/ppermute | solution.py:43
  92.3 0.7 shard_map.102
  93.0 0.3 collective-permute-start.23
  93.4 2.1 %reduce_sum.12 = bf16[128,512]{1,0:T(8,128)(2,1)} reduce(bf16[8,128,512]{2,1,0:T(8,128)(2,1)} %all-to-all-done, bf16[]{:T(256)} %constant.4.clone.1), dimensions={0}, to_apply=%region_0.0 | reduce | flops 458752 | bytes 1179650 | tf_op jit(solution)/shard_map/reduce_sum | solution.py:210
  95.4 0.2 collective-permute-done.21.over
  95.7 6.5 %collective-permute-done.23.far = bf16[512,256]{1,0:T(8,128)(2,1)S(1)} collective-permute-done((bf16[512,256]{1,0:T(8,128)(2,1)}, bf16[512,256]{1,0:T(8,128)(2,1)S(1)}, u32[]{:S(2)}, u32[]{:S(2)}) %collective-permute-start.23) | collective-permute-done | bytes 262176 | tf_op jit(solution)/shard_map/ppermute | solution.py:43
  102.1 0.0 copy-start.10
  102.1 1.0 copy-done.10
  103.2 2.0 %shard_map.103 = (f32[1024,128]{1,0:T(8,128)}, f32[1024,128]{1,0:T(8,128)}, f32[1024,128]{1,0:T(8,128)}) custom-call(bf16[512,512]{1,0:T(8,128)(2,1)S(1)} %copy-done.4, f32[512,256]{1,0:T(8,128)S(1)} %copy-done.10, bf16[512,256]{1,0:T(8,128)(2,1)S(1)} %collective-permute-done.16.d_up, bf16[512,256]{1,0:T(8,128)(2,1)S(1)} %collective-permute-done.17.d_down, ...), custom_call_target="tpu_custom_call" | custom-call | tf_op jit(solution)/shard_map/pallas_call | solution.py:149
  (23 shorter events, 0.1 us)
Async XLA Ops:
  2.6 34.5 %all-to-all-start.1 = ((bf16[8,128,512]{2,1,0:T(8,128)(2,1)}), bf16[8,128,512]{2,1,0:T(8,128)(2,1)S(1)}, u32[]{:S(2)}, u32[]{:S(2)}) async-start(bf16[8,128,512]{2,1,0:T(8,128)(2,1)} %broadcast_in_dim.2), calls=%async_computation.1 | async-start | bytes 2097152 | tf_op jit(solution)/shard_map/all_to_all | solution.py:164
  9.0 1.0 copy-start.5
  10.1 9.4 %collective-permute-start.1 = (bf16[512,256]{1,0:T(8,128)(2,1)S(1)}, bf16[512,256]{1,0:T(8,128)(2,1)S(1)}, u32[]{:S(2)}, u32[]{:S(2)}) collective-permute-start(bf16[512,256]{1,0:T(8,128)(2,1)S(1)} %shard_map.94.refs_0_), channel_id=1, source_target_pairs={{0,96},{1,97},{2,98},{3,99},{4,100},{5,101},{6,102},{7,103},{8,104... | collective-permute-start | bytes 786440 | tf_op jit(solution)/shard_map/ppermute | solution.py:43
  12.6 12.2 %collective-permute-start.3 = (bf16[512,256]{1,0:T(8,128)(2,1)S(1)}, bf16[512,256]{1,0:T(8,128)(2,1)S(1)}, u32[]{:S(2)}, u32[]{:S(2)}) collective-permute-start(bf16[512,256]{1,0:T(8,128)(2,1)S(1)} %shard_map.94.refs_0_), channel_id=1, source_target_pairs={{0,32},{1,33},{2,34},{3,35},{4,36},{5,37},{6,38},{7,39},{8,40},{9,... | collective-permute-start | bytes 786440 | tf_op jit(solution)/shard_map/ppermute | solution.py:43
  12.6 15.6 %collective-permute-start.5 = (bf16[512,256]{1,0:T(8,128)(2,1)S(1)}, bf16[512,256]{1,0:T(8,128)(2,1)}, u32[]{:S(2)}, u32[]{:S(2)}) collective-permute-start(bf16[512,256]{1,0:T(8,128)(2,1)S(1)} %shard_map.94.refs_0_), channel_id=1, source_target_pairs={{0,64},{1,65},{2,66},{3,67},{4,68},{5,69},{6,70},{7,71},{8,72},{9,... | collective-permute-start | bytes 786440 | tf_op jit(solution)/shard_map/ppermute | solution.py:43
  14.4 29.9 %collective-permute-start = (bf16[512,256]{1,0:T(8,128)(2,1)S(1)}, bf16[512,256]{1,0:T(8,128)(2,1)}, u32[]{:S(2)}, u32[]{:S(2)}) collective-permute-start(bf16[512,256]{1,0:T(8,128)(2,1)S(1)} %shard_map.94.refs_0_), channel_id=1, source_target_pairs={{0,8},{1,9},{2,10},{3,11},{4,12},{5,13},{6,14},{7,15},{8,0},{9,1},... | collective-permute-start | bytes 786440 | tf_op jit(solution)/shard_map/ppermute | solution.py:43
  16.1 28.6 %collective-permute-start.7 = (bf16[512,256]{1,0:T(8,128)(2,1)S(1)}, bf16[512,256]{1,0:T(8,128)(2,1)}, u32[]{:S(2)}, u32[]{:S(2)}) collective-permute-start(bf16[512,256]{1,0:T(8,128)(2,1)S(1)} %shard_map.94.refs_0_), channel_id=1, source_target_pairs={{0,16},{1,17},{2,18},{3,19},{4,20},{5,21},{6,22},{7,23},{8,24},{9,... | collective-permute-start | bytes 786440 | tf_op jit(solution)/shard_map/ppermute | solution.py:43
  19.5 25.4 %collective-permute-start.2 = (bf16[512,256]{1,0:T(8,128)(2,1)S(1)}, bf16[512,256]{1,0:T(8,128)(2,1)}, u32[]{:S(2)}, u32[]{:S(2)}) collective-permute-start(bf16[512,256]{1,0:T(8,128)(2,1)S(1)} %collective-permute-done.1.refs_2_), channel_id=1, source_target_pairs={{0,8},{1,9},{2,10},{3,11},{4,12},{5,13},{6,14},{7,15},{8,0},{9,1},... | collective-permute-start | bytes 786440 | tf_op jit(solution)/shard_map/ppermute | solution.py:43
  24.8 20.4 %collective-permute-start.4 = (bf16[512,256]{1,0:T(8,128)(2,1)S(1)}, bf16[512,256]{1,0:T(8,128)(2,1)}, u32[]{:S(2)}, u32[]{:S(2)}) collective-permute-start(bf16[512,256]{1,0:T(8,128)(2,1)S(1)} %collective-permute-done.3.refs_4_), channel_id=1, source_target_pairs={{0,8},{1,9},{2,10},{3,11},{4,12},{5,13},{6,14},{7,15},{8,0},{9,1},... | collective-permute-start | bytes 786440 | tf_op jit(solution)/shard_map/ppermute | solution.py:43
  28.2 18.1 %collective-permute-start.6 = (bf16[512,256]{1,0:T(8,128)(2,1)}, bf16[512,256]{1,0:T(8,128)(2,1)}, u32[]{:S(2)}, u32[]{:S(2)}) collective-permute-start(bf16[512,256]{1,0:T(8,128)(2,1)} %collective-permute-done.5.refs_6_), channel_id=1, source_target_pairs={{0,8},{1,9},{2,10},{3,11},{4,12},{5,13},{6,14},{7,15},{8,0},{9,1},... | collective-permute-start | bytes 786440 | tf_op jit(solution)/shard_map/ppermute | solution.py:43
  28.2 3.4 %copy-start.3 = (bf16[1024,16,1,256]{3,1,2,0:T(8,128)(2,1)S(1)}, bf16[1024,16,1,256]{3,1,2,0:T(8,128)(2,1)}, u32[]{:S(2)}) copy-start(bf16[1024,16,1,256]{3,1,2,0:T(8,128)(2,1)} %param.7) | copy-start | bytes 25165828
  31.6 5.5 %copy-start.4 = (bf16[512,512]{1,0:T(8,128)(2,1)S(1)}, bf16[512,512]{1,0:T(8,128)(2,1)}, u32[]{:S(2)}) copy-start(bf16[512,512]{1,0:T(8,128)(2,1)} %constant.5.clone.h_ref) | copy-start | bytes 1572868
  33.8 3.3 %copy-start = (bf16[16,1024,256]{2,1,0:T(8,128)(2,1)}, bf16[16,1024,256]{2,1,0:T(8,128)(2,1)S(1)}, u32[]{:S(2)}) copy-start(bf16[16,1024,256]{2,1,0:T(8,128)(2,1)S(1)} %shard_map.93.g_ref) | copy-start | bytes 25165828
  37.8 3.4 %copy-start.1 = (bf16[16,1024,256]{2,1,0:T(8,128)(2,1)S(1)}, bf16[16,1024,256]{2,1,0:T(8,128)(2,1)}, u32[]{:S(2)}) copy-start(bf16[16,1024,256]{2,1,0:T(8,128)(2,1)} %copy-done) | copy-start | bytes 25165828
  44.2 36.7 %collective-permute-start.15 = (bf16[5,512,256]{2,1,0:T(8,128)(2,1)}, bf16[5,512,256]{2,1,0:T(8,128)(2,1)}, u32[]{:S(2)}, u32[]{:S(2)}) collective-permute-start(bf16[5,512,256]{2,1,0:T(8,128)(2,1)} %shard_map.97), channel_id=1, source_target_pairs={{0,8},{1,9},{2,10},{3,11},{4,12},{5,13},{6,14},{7,15},{8,0},{9,1},... | collective-permute-start | bytes 3932168 | tf_op jit(solution)/shard_map/ppermute | solution.py:43
  44.7 7.0 %collective-permute-start.8 = (bf16[512,256]{1,0:T(8,128)(2,1)}, bf16[512,256]{1,0:T(8,128)(2,1)S(1)}, u32[]{:S(2)}, u32[]{:S(2)}) collective-permute-start(bf16[512,256]{1,0:T(8,128)(2,1)} %collective-permute-done.7.refs_8_), channel_id=1, source_target_pairs={{0,8},{1,9},{2,10},{3,11},{4,12},{5,13},{6,14},{7,15},{8,0},{9,1},... | collective-permute-start | bytes 786440 | tf_op jit(solution)/shard_map/ppermute | solution.py:43
  44.8 8.2 %collective-permute-start.9 = (bf16[512,256]{1,0:T(8,128)(2,1)}, bf16[512,256]{1,0:T(8,128)(2,1)S(1)}, u32[]{:S(2)}, u32[]{:S(2)}) collective-permute-start(bf16[512,256]{1,0:T(8,128)(2,1)} %collective-permute-done.7.refs_8_), channel_id=1, source_target_pairs={{0,96},{1,97},{2,98},{3,99},{4,100},{5,101},{6,102},{7,103},{8,104... | collective-permute-start | bytes 786440 | tf_op jit(solution)/shard_map/ppermute | solution.py:43
  45.2 8.9 %collective-permute-start.11 = (bf16[512,256]{1,0:T(8,128)(2,1)}, bf16[512,256]{1,0:T(8,128)(2,1)S(1)}, u32[]{:S(2)}, u32[]{:S(2)}) collective-permute-start(bf16[512,256]{1,0:T(8,128)(2,1)} %collective-permute-done.7.refs_8_), channel_id=1, source_target_pairs={{0,32},{1,33},{2,34},{3,35},{4,36},{5,37},{6,38},{7,39},{8,40},{9,... | collective-permute-start | bytes 786440 | tf_op jit(solution)/shard_map/ppermute | solution.py:43
  46.3 9.2 %collective-permute-start.13 = (bf16[512,256]{1,0:T(8,128)(2,1)}, bf16[512,256]{1,0:T(8,128)(2,1)S(1)}, u32[]{:S(2)}, u32[]{:S(2)}) collective-permute-start(bf16[512,256]{1,0:T(8,128)(2,1)} %collective-permute-done.5.refs_6_), channel_id=1, source_target_pairs={{0,16},{1,17},{2,18},{3,19},{4,20},{5,21},{6,22},{7,23},{8,24},{9,... | collective-permute-start | bytes 786440 | tf_op jit(solution)/shard_map/ppermute | solution.py:43
  51.7 18.2 %collective-permute-start.18 = (bf16[3,512,256]{2,1,0:T(8,128)(2,1)}, bf16[3,512,256]{2,1,0:T(8,128)(2,1)S(1)}, u32[]{:S(2)}, u32[]{:S(2)}) collective-permute-start(bf16[3,512,256]{2,1,0:T(8,128)(2,1)} %shard_map.99), channel_id=1, source_target_pairs={{0,8},{1,9},{2,10},{3,11},{4,12},{5,13},{6,14},{7,15},{8,0},{9,1},... | collective-permute-start | bytes 2359304 | tf_op jit(solution)/shard_map/ppermute | solution.py:43
  53.0 4.1 %collective-permute-start.10 = (bf16[512,256]{1,0:T(8,128)(2,1)S(1)}, bf16[512,256]{1,0:T(8,128)(2,1)S(1)}, u32[]{:S(2)}, u32[]{:S(2)}) collective-permute-start(bf16[512,256]{1,0:T(8,128)(2,1)S(1)} %collective-permute-done.9.refs_10_), channel_id=1, source_target_pairs={{0,8},{1,9},{2,10},{3,11},{4,12},{5,13},{6,14},{7,15},{8,0},{9,1},... | collective-permute-start | bytes 786440 | tf_op jit(solution)/shard_map/ppermute | solution.py:43
  54.2 2.9 %collective-permute-start.12 = (bf16[512,256]{1,0:T(8,128)(2,1)S(1)}, bf16[512,256]{1,0:T(8,128)(2,1)S(1)}, u32[]{:S(2)}, u32[]{:S(2)}) collective-permute-start(bf16[512,256]{1,0:T(8,128)(2,1)S(1)} %collective-permute-done.11.refs_12_), channel_id=1, source_target_pairs={{0,8},{1,9},{2,10},{3,11},{4,12},{5,13},{6,14},{7,15},{8,0},{9,1},... | collective-permute-start | bytes 786440 | tf_op jit(solution)/shard_map/ppermute | solution.py:43
  55.5 2.7 %collective-permute-start.14 = (bf16[512,256]{1,0:T(8,128)(2,1)S(1)}, bf16[512,256]{1,0:T(8,128)(2,1)S(1)}, u32[]{:S(2)}, u32[]{:S(2)}) collective-permute-start(bf16[512,256]{1,0:T(8,128)(2,1)S(1)} %collective-permute-done.13.refs_14_), channel_id=1, source_target_pairs={{0,8},{1,9},{2,10},{3,11},{4,12},{5,13},{6,14},{7,15},{8,0},{9,1},... | collective-permute-start | bytes 786440 | tf_op jit(solution)/shard_map/ppermute | solution.py:43
  65.1 28.3 %all-to-all-start = ((bf16[8,128,512]{2,1,0:T(8,128)(2,1)}), bf16[8,128,512]{2,1,0:T(8,128)(2,1)}, u32[]{:S(2)}, u32[]{:S(2)}) async-start(bf16[8,128,512]{2,1,0:T(8,128)(2,1)} %shard_map.95), calls=%async_computation | async-start | bytes 2097152 | tf_op jit(solution)/shard_map/all_to_all | solution.py:209
  69.9 3.4 %copy-start.2 = (bf16[16,1024,256]{2,1,0:T(8,128)(2,1)S(1)}, bf16[16,1024,256]{2,1,0:T(8,128)(2,1)}, u32[]{:S(2)}) copy-start(bf16[16,1024,256]{2,1,0:T(8,128)(2,1)} %copy-done) | copy-start | bytes 25165828
  74.9 27.2 %copy-start.6 = (f32[512,1,1,256]{3,2,1,0:T(1,128)S(1)}, f32[512,1,1,256]{3,2,1,0:T(1,128)}, u32[]{:S(2)}) copy-start(f32[512,1,1,256]{3,2,1,0:T(1,128)} %param.8) | copy-start | bytes 1572868
  74.9 27.2 %copy-start.7 = (f32[512,1,1,256]{3,2,1,0:T(1,128)S(1)}, f32[512,1,1,256]{3,2,1,0:T(1,128)}, u32[]{:S(2)}) copy-start(f32[512,1,1,256]{3,2,1,0:T(1,128)} %param.9) | copy-start | bytes 1572868
  74.9 27.2 %copy-start.8 = (f32[512,1,1,256]{3,2,1,0:T(1,128)S(1)}, f32[512,1,1,256]{3,2,1,0:T(1,128)}, u32[]{:S(2)}) copy-start(f32[512,1,1,256]{3,2,1,0:T(1,128)} %param.10) | copy-start | bytes 1572868
  74.9 13.3 %collective-permute-start.19 = (bf16[512,256]{1,0:T(8,128)(2,1)S(1)}, bf16[512,256]{1,0:T(8,128)(2,1)S(1)}, u32[]{:S(2)}, u32[]{:S(2)}) collective-permute-start(bf16[512,256]{1,0:T(8,128)(2,1)S(1)} %get-tuple-element.19), channel_id=1, source_target_pairs={{0,32},{1,33},{2,34},{3,35},{4,36},{5,37},{6,38},{7,39},{8,40},{9,... | collective-permute-start | bytes 786440 | tf_op jit(solution)/shard_map/ppermute | solution.py:43
  75.1 13.1 %collective-permute-start.20 = (bf16[512,256]{1,0:T(8,128)(2,1)S(1)}, bf16[512,256]{1,0:T(8,128)(2,1)S(1)}, u32[]{:S(2)}, u32[]{:S(2)}) collective-permute-start(bf16[512,256]{1,0:T(8,128)(2,1)S(1)} %get-tuple-element.20), channel_id=1, source_target_pairs={{0,96},{1,97},{2,98},{3,99},{4,100},{5,101},{6,102},{7,103},{8,104... | collective-permute-start | bytes 786440 | tf_op jit(solution)/shard_map/ppermute | solution.py:43
  77.7 14.6 %collective-permute-start.22 = (bf16[512,256]{1,0:T(8,128)(2,1)S(1)}, bf16[512,256]{1,0:T(8,128)(2,1)S(1)}, u32[]{:S(2)}, u32[]{:S(2)}) collective-permute-start(bf16[512,256]{1,0:T(8,128)(2,1)S(1)} %get-tuple-element.22), channel_id=1, source_target_pairs={{0,16},{1,17},{2,18},{3,19},{4,20},{5,21},{6,22},{7,23},{8,24},{9,... | collective-permute-start | bytes 786440 | tf_op jit(solution)/shard_map/ppermute | solution.py:43
  84.7 0.8 copy-start.9
  85.5 9.9 %collective-permute-start.16 = (bf16[512,256]{1,0:T(8,128)(2,1)}, bf16[512,256]{1,0:T(8,128)(2,1)S(1)}, u32[]{:S(2)}, u32[]{:S(2)}) collective-permute-start(bf16[512,256]{1,0:T(8,128)(2,1)} %get-tuple-element.16), channel_id=1, source_target_pairs={{0,32},{1,33},{2,34},{3,35},{4,36},{5,37},{6,38},{7,39},{8,40},{9,... | collective-permute-start | bytes 786440 | tf_op jit(solution)/shard_map/ppermute | solution.py:43
  85.5 9.9 %collective-permute-start.17 = (bf16[512,256]{1,0:T(8,128)(2,1)}, bf16[512,256]{1,0:T(8,128)(2,1)S(1)}, u32[]{:S(2)}, u32[]{:S(2)}) collective-permute-start(bf16[512,256]{1,0:T(8,128)(2,1)} %get-tuple-element.17), channel_id=1, source_target_pairs={{0,96},{1,97},{2,98},{3,99},{4,100},{5,101},{6,102},{7,103},{8,104... | collective-permute-start | bytes 786440 | tf_op jit(solution)/shard_map/ppermute | solution.py:43
  88.3 7.4 %collective-permute-start.21 = (bf16[512,256]{1,0:T(8,128)(2,1)S(1)}, bf16[512,256]{1,0:T(8,128)(2,1)S(1)}, u32[]{:S(2)}, u32[]{:S(2)}) collective-permute-start(bf16[512,256]{1,0:T(8,128)(2,1)S(1)} %shard_map.101), channel_id=1, source_target_pairs={{0,16},{1,17},{2,18},{3,19},{4,20},{5,21},{6,22},{7,23},{8,24},{9,... | collective-permute-start | bytes 786440 | tf_op jit(solution)/shard_map/ppermute | solution.py:43
  93.0 9.1 %collective-permute-start.23 = (bf16[512,256]{1,0:T(8,128)(2,1)}, bf16[512,256]{1,0:T(8,128)(2,1)S(1)}, u32[]{:S(2)}, u32[]{:S(2)}) collective-permute-start(bf16[512,256]{1,0:T(8,128)(2,1)} %shard_map.102), channel_id=1, source_target_pairs={{0,64},{1,65},{2,66},{3,67},{4,68},{5,69},{6,70},{7,71},{8,72},{9,... | collective-permute-start | bytes 786440 | tf_op jit(solution)/shard_map/ppermute | solution.py:43
  102.1 1.0 copy-start.10

commit v2 on v1

v2 whole, which is shorter than its diff:
```python
import math

import jax
import jax.numpy as jnp
import numpy as np
from jax import lax
from jax.experimental import pallas as pl
from jax.experimental.pallas import tpu as pltpu
from jax.sharding import PartitionSpec as P


LATENT = 512
COLS = 256
NX, NZH, NC = 4, 2, 2
NZL, NY = 2, 4
TOK = 1024
TOKENS = 16384
BF = jnp.bfloat16
F32 = jnp.float32
VM = pl.BlockSpec(memory_space=pltpu.VMEM)
AXES = ("dp", "head")


def signs(length):
    i = np.arange(length)
    common = i[:, None] & i[None, :]
    parity = np.zeros_like(common)
    for position in range(length.bit_length()):
        parity += (common >> position) & 1
    return jnp.asarray(1 - 2 * (parity & 1), BF)


def shifted(value, dx=0, dz=0, dc=0, dl=0, dy=0, fan_x=0, fan_y=0):
    sizes = (NX, NZH, NC, NZL, NY)
    pairs = []
    for source, place in enumerate(np.ndindex(*sizes)):
        sign = 1 - 2 * place[2]
        steps = (dx + sign * fan_x, dz, dc, dl, dy + sign * fan_y)
        target = [(p + d) % n for p, d, n in zip(place, steps, sizes)]
        pairs.append((source, int(np.ravel_multi_index(target, sizes))))
    return lax.ppermute(value, AXES, pairs)


def kernel(body, outs, count, in_specs=None, scratch=(), limit=16, home=False):
    shape_of = jax.ShapeDtypeStruct if home else pltpu.VMEM
    return pl.pallas_call(
        body,
        in_specs=in_specs or [VM] * count,
        out_specs=[VM] * len(outs),
        out_shape=[shape_of(shape, dtype) for shape, dtype in outs],
        scratch_shapes=list(scratch),
        compiler_params=pltpu.CompilerParams(vmem_limit_bytes=limit << 20),
    )


def my_core():
    return lax.rem(lax.axis_index("dp"), NC)


def ahead(core):
    return 1 + 2 * core


def group_at(dx, dz, core):
    me = lax.axis_index("dp")
    x, zh = me // (NZH * NC), lax.rem(me // NC, NZH)
    return (lax.rem(x + dx, NX) * NZH + lax.rem(zh + dz, NZH)) * NC + core


def head_at(dl, dy):
    me = lax.axis_index("head")
    return lax.rem(me // NY + dl, NZL) * NY + lax.rem(me + dy, NY)


def front_body(h_hbm, l_hbm, w_hbm, o_ref, turn_ref, h_ref, l_ref, w_ref, sems):
    moves = zip((w_hbm, l_hbm, h_hbm), (w_ref, l_ref, h_ref))
    copies = [pltpu.make_async_copy(a, b, sems.at[i]) for i, (a, b) in enumerate(moves)]
    for copy in copies:
        copy.start()
    copies[0].wait()
    for half in range(2):
        rows = w_ref[pl.ds(half, LATENT, stride=2), :]
        o_ref[:, half * 128 : half * 128 + 128] = rows.astype(BF)
    copies[1].wait()
    copies[2].wait()
    turned = lax.dot_general(
        h_ref[...], l_ref[...], (((1,), (1,)), ((), ())), preferred_element_type=F32
    )
    turn_ref[...] = (turned * (1.0 / math.sqrt(LATENT))).astype(BF)


def swap_body(g_ref, o_ref, held, sems):
    parts = sems.shape[0]
    size = TOK // parts
    copies = [
        pltpu.make_async_copy(
            g_ref.at[pl.ds(part * size, size)], held.at[pl.ds(part * size, size)], sems.at[part]
        )
        for part in range(parts)
    ]
    for copy in copies:
        copy.start()
    for part, copy in enumerate(copies):
        copy.wait()
        rows = held[part * size : part * size + size]
        o_ref[:, part * size : part * size + size] = jnp.swapaxes(rows, 0, 1)


def pack_body(a_ref, b_ref, o_ref):
    o_ref[0] = a_ref[...]
    o_ref[1] = b_ref[...]


def cut_body(pair_ref, o_ref):
    o_ref[...] = pair_ref[0]


def place_body(own, pair, other, far, z_own, z_pair, z_other, z_far, o_ref):
    up, down = ahead(my_core()), ahead(1 - my_core())
    pieces = (
        (0, 0, own[...]), (0, down, pair[0]), (0, up, other[1]), (0, 2, far[...]),
        (1, 0, z_own[...]), (1, down, z_pair[0]), (1, up, z_other[1]), (1, 2, z_far[...]),
    )
    for dl, dy, turned in pieces:
        o_ref[:, pl.ds(pl.multiple_of(head_at(dl, dy) * 128, 128), 128)] = turned


def turned_block(l_ref, g_ref, block):
    value = jnp.dot(l_ref[...], g_ref[block], preferred_element_type=F32)
    spread = 2.0 * jnp.sqrt(jnp.mean(value * value, axis=0, keepdims=True) + 1e-06)
    return jnp.clip(value, -spread, spread).astype(BF)


def early(core):
    step = ahead(core)
    return [(step, 1, 0), (step, 1, 1), (2, 1, core)]


def late(core):
    step = ahead(core)
    return [(step, 0, 0), (step, 0, 1), (2, 0, core), (0, 1, core), (0, 0, core)]


def give_body(places):
    def body(g_ref, l_ref, o_ref):
        for at, place in enumerate(places(1 - my_core())):
            o_ref[at] = turned_block(l_ref, g_ref, group_at(*place))

    return body


def keep_body(places):
    def body(g_ref, l_ref, r_ref, pair, *single):
        for at, place in enumerate(places(my_core())):
            mine = turned_block(l_ref, g_ref, group_at(*place)).astype(F32) + r_ref[at].astype(F32)
            if at < 2:
                pair[at] = mine.astype(pair.dtype)
            else:
                single[at - 2][...] = mine.astype(single[at - 2].dtype)

    return body


def products(g_ref, terms, part):
    total = None
    for w, dx, dz, core in terms:
        rows = g_ref[group_at(dx, dz, core), part * 512 : part * 512 + 512]
        term = lax.dot_general(rows, w, (((1,), (1,)), ((), ())), preferred_element_type=F32)
        total = term if total is None else total + term
    return total


def latent_body(g_ref, p0, x, xs, f, fs, z, zs, zx, zxs, o_ref):
    core = my_core()
    rest = 1 - core
    up, down = ahead(core), ahead(rest)
    terms = [
        (p0[0], 0, 0, core), (p0[1], 0, 0, rest), (x[0], down, 0, core), (x[1], down, 0, rest),
        (xs[0], up, 0, rest), (xs[1], up, 0, core), (f[...], 2, 0, core), (fs[...], 2, 0, rest),
        (z[...], 0, 1, core), (zs[...], 0, 1, rest), (zx[0], down, 1, core), (zx[1], down, 1, rest),
        (zxs[0], up, 1, rest), (zxs[1], up, 1, core),
    ]
    for part in range(2):
        o_ref[part * 512 : part * 512 + 512] = products(g_ref, terms, part)


def finish_body(g_ref, zf, zfs, part_ref, o_ref):
    core = my_core()
    terms = [(zf[...], 2, 1, core), (zfs[...], 2, 1, 1 - core)]
    for part in range(2):
        total = part_ref[part * 512 : part * 512 + 512] + products(g_ref, terms, part)
        o_ref[part * 4 : part * 4 + 4] = total.astype(BF).reshape(4, 128, LATENT)


def total_body(r_ref, o_ref):
    total = r_ref[0].astype(F32)
    for peer in range(1, NZL * NY):
        total = total + r_ref[peer].astype(F32)
    o_ref[...] = total.astype(BF)


def join_pair_body(base, pair, other, o_ref):
    core = my_core()
    total = base[...] + pair[core].astype(F32) + other[core].astype(F32)
    o_ref[...] = total.astype(BF)


def update_body(h_ref, own, pair, other, over, far, w_ref, a_ref, b_ref, nw_ref, na_ref, nb_ref):
    core = my_core()
    summed = own[...] + pair[core].astype(F32) + other[core].astype(F32)
    summed = summed + over[...].astype(F32) + far[...].astype(F32)
    high = summed.astype(BF)
    low = (summed - high.astype(F32)).astype(BF)
    h = h_ref[...]
    grad = jnp.dot(h, high, preferred_element_type=F32) + jnp.dot(h, low, preferred_element_type=F32)
    grad = grad * (TOKENS ** (-0.5) / math.sqrt(LATENT))
    for half in range(2):
        rows = pl.ds(half, LATENT, stride=2)
        g = grad[:, half * 128 : half * 128 + 128]
        one = 0.9 * a_ref[rows, :] + 0.1 * g
        two = 0.95 * b_ref[rows, :] + 0.05 * g * g
        step = one / (1.0 - 0.9**10) / (jnp.sqrt(two / (1.0 - 0.95**10)) + 1e-08)
        w = w_ref[rows, :]
        na_ref[rows, :] = one
        nb_ref[rows, :] = two
        nw_ref[rows, :] = w - 0.001 * (step + 0.1 * w)


def join_body(*refs):
    total = refs[0][...].astype(F32)
    for r in refs[1:-1]:
        total = total + r[...].astype(F32)
    refs[-1][...] = total.astype(BF)


def run(body, outs, *operands, **more):
    return kernel(body, outs, len(operands), **more)(*operands)


def send(value, **steps):
    return shifted(value, **steps)


def step(latent, out_grad, weight, moment_one, moment_two):
    h = signs(LATENT)
    flat = (1024, 128)
    block = (LATENT, COLS)
    one = [(block, BF)]
    peers = NZL * NY

    far_off = [pltpu.with_memory_space_constraint(v, pltpu.HBM) for v in (h, latent, weight.reshape(flat))]
    w, turn = run(
        front_body,
        [(block, BF), ((LATENT, 128), BF)],
        *far_off,
        in_specs=[pl.BlockSpec(memory_space=pltpu.HBM)] * 3,
        scratch=[
            pltpu.VMEM((LATENT, LATENT), BF), pltpu.VMEM((128, LATENT), BF), pltpu.VMEM(flat, F32),
            pltpu.SemaphoreType.DMA((3,)),
        ],
    )
    rows_pair = [((2, LATENT, 128), BF)]
    (l_pair,) = run(pack_body, rows_pair, turn, send(turn, dc=1))
    l_z = send(turn, dl=1)
    l_y = send(l_pair, fan_y=1)
    l_ys = send(l_y, dc=1)
    (lz_pair,) = run(pack_body, rows_pair, l_z, send(l_z, dc=1))
    l_zy = send(lz_pair, fan_y=1)
    l_zys = send(l_zy, dc=1)
    l_2 = send(run(cut_body, [((LATENT, 128), BF)], l_y)[0], fan_y=1)
    l_2z = send(run(cut_body, [((LATENT, 128), BF)], l_zy)[0], fan_y=1)

    pair = [((2, *block), BF)]
    (w_pair,) = run(pack_body, pair, w, send(w, dc=1))
    w_z = send(w, dz=1)
    w_x = send(w_pair, fan_x=1)
    w_zs = send(w_z, dc=1)
    (wz_pair,) = run(pack_body, pair, w_z, w_zs)
    w_zx = send(wz_pair, fan_x=1)
    w_2 = send(run(cut_body, one, w_x)[0], fan_x=1)
    w_2z = send(run(cut_body, one, w_zx)[0], fan_x=1)
    ws = [
        w_pair, w_x, send(w_x, dc=1), w_2, send(w_2, dc=1), w_z, w_zs,
        w_zx, send(w_zx, dc=1),
    ]

    (grads,) = run(
        swap_body,
        [((16, TOK, COLS), BF)],
        pltpu.with_memory_space_constraint(out_grad[:, :, 0, :], pltpu.HBM),
        in_specs=[pl.BlockSpec(memory_space=pltpu.HBM)],
        scratch=[pltpu.VMEM((TOK, 16, COLS), BF), pltpu.SemaphoreType.DMA((8,))],
        limit=24,
    )

    (turn,) = run(place_body, [((LATENT, TOK), BF)], turn, l_y, l_ys, l_2, l_z, l_zy, l_zys, l_2z)
    (give,) = run(give_body(early), [((3, *block), BF)], grads, turn)
    got = send(give, dc=1)
    t_a, t_b = run(keep_body(early), pair + one, grads, turn, got)
    (give,) = run(give_body(late), [((5, *block), BF)], grads, turn)
    got = send(give, dc=1)
    t_d, far, over, own = run(keep_body(late), pair + [(block, F32)] * 3, grads, turn, got)
    t_a = send(t_a, fan_x=1)
    t_b = send(t_b, dz=1)
    t_d = send(t_d, fan_x=1)
    (over,) = run(join_pair_body, one, over, t_a, send(t_a, dc=1))
    over = send(over, dz=1)
    (far,) = run(join_body, one, far, t_b)
    far = send(far, dx=2)

    (partial,) = run(latent_body, [((TOK, LATENT), F32)], grads, *ws)
    (partial,) = run(
        finish_body, [((peers, 128, LATENT), BF)],
        grads, w_2z, send(w_2z, dc=1), partial,
    )
    arrived = lax.all_to_all(partial, "head", 0, 0, tiled=True)
    (latent_grad,) = run(total_body, [(latent.shape, BF)], arrived, home=True)

    states = [s.reshape(flat) for s in (weight, moment_one, moment_two)]
    new = run(
        update_body, [(flat, F32)] * 3, h, own, t_d, send(t_d, dc=1), over, far, *states,
        limit=24, home=True,
    )
    new = [n.reshape(weight.shape) for n in new]
    return (latent_grad, *new)


def solution(mesh):
    state = P(None, "dp", "head", None)
    return jax.shard_map(
        step,
        mesh=mesh,
        in_specs=(P(("dp", "head"), None), P("dp", None, "head", None), state, state, state),
        out_specs=(P(("dp", "head"), None), state, state, state),
        check_vma=False,
    )
```

time: 106 us -> 113 us (1.066); the launches traced: 105 us -> 110 us
  waiting for transfers between devices: 12.3 us -> 37.4 us
  local copies, waits for them, and re-layouts: 18.3 us -> 5.76 us
  starting transfers between devices: 48.6 us -> 41.6 us
  other arithmetic: 2.06 us -> 0 us
  Pallas kernels: 23.1 us -> 25 us
    ppermute x24 -> x29, waiting for transfers between devices: 12.3 us -> 37.4 us  [shifted(): return lax.ppermute(value, AXES, pairs)]
    unnamed x22 -> x16, local copies, waits for them, and re-layouts: 16.3 us -> 5.76 us
    all_to_all x1 -> x0, starting transfers between devices: 6.36 us -> none  [step(): rows = lax.all_to_all(rows, 'head', 0, 0, tiled=True)]
    reduce_sum x1 -> x0, other arithmetic: 2.06 us -> none  [step(): latent_grad = arrived.astype(F32).sum(axis=0).astype(BF)]
    broadcast_in_dim x1 -> x0, local copies, waits for them, and re-layouts: 1.99 us -> none  [step(): rows = jnp.broadcast_to(latent[None], (peers, *latent.shape))]
    pallas_call x11 -> x21, Pallas kernels: 23.1 us -> 25 us  [run(): return kernel(body, outs, len(operands), **more)(*operands)]
    ppermute x24 -> x29, starting transfers between devices: 37.4 us -> 37.5 us  [shifted(): return lax.ppermute(value, AXES, pairs)]
  transfers between devices with their start and end apart: 26 -> 30, of which waited for: 6 -> 10; matrix products, arithmetic and copies ran while one was open for 2% -> 0% of each run, Pallas kernels for 20% -> 18%
where the time goes in v2:
time: 113 us; the launch traced here: 110 us
  starting transfers between devices  41.6 us (37%)
  waiting for transfers between devices  37.4 us (33%)
  Pallas kernels  25 us (22%)
  local copies, waits for them, and re-layouts  5.76 us (5%)
    ppermute x29, starting transfers between devices, shifted(): return lax.ppermute(value, AXES, pairs)  37.5 us
    ppermute x29, waiting for transfers between devices, shifted(): return lax.ppermute(value, AXES, pairs)  37.4 us
    pallas_call x21, Pallas kernels, run(): return kernel(body, outs, len(operands), **more)(*operands)  25 us
    unnamed x16, local copies, waits for them, and re-layouts  5.76 us
    all_to_all x1, starting transfers between devices, step(): arrived = lax.all_to_all(partial, 'head', 0, 0, tiled=True)  4.07 us
  transfers between devices with their start and end apart: 30, of which 10 were waited for; matrix products, arithmetic and copies ran while one was open for 0% of the time, Pallas kernels for 18%

profile of v2, /device:TPU:1, one launch (start us, length us, event | category | flops | bytes accessed | tf_op | source)
XLA Modules:
  0.0 110.5 jit_solution(17669927719172989381)
XLA Ops:
  0.6 1.6 %shard_map.94 = (bf16[512,256]{1,0:T(8,128)(2,1)S(1)}, bf16[512,128]{1,0:T(8,128)(2,1)S(1)}) custom-call(bf16[512,512]{1,0:T(8,128)(2,1)} %constant.2.clone.h_hbm.h_ref, bf16[128,512]{1,0:T(8,128)(2,1)} %l_hbm.1, f32[1024,128]{1,0:T(8,128)} %bitcast.7), custom_call_target="tpu_custom_call" | custom-call | tf_op jit(solution)/shard_map/pallas_call | solution.py:237
  2.2 2.5 %collective-permute-start.15 = (bf16[512,128]{1,0:T(8,128)(2,1)S(1)}, bf16[512,128]{1,0:T(8,128)(2,1)S(1)}, u32[]{:S(2)}, u32[]{:S(2)}) collective-permute-start(bf16[512,128]{1,0:T(8,128)(2,1)S(1)} %get-tuple-element.16.a_ref.own), channel_id=1, source_target_pairs={{0,4},{1,5},{2,6},{3,7},{4,0},{5,1},{6,2},{7,3},{8,12},{9,13},{10,... | collective-permute-start | bytes 393224 | tf_op jit(solution)/shard_map/ppermute | solution.py:41
  4.7 1.0 collective-permute-start.11
  5.7 2.2 %collective-permute-done.15.a_ref.z_own = bf16[512,128]{1,0:T(8,128)(2,1)S(1)} collective-permute-done((bf16[512,128]{1,0:T(8,128)(2,1)S(1)}, bf16[512,128]{1,0:T(8,128)(2,1)S(1)}, u32[]{:S(2)}, u32[]{:S(2)}) %collective-permute-start.15) | collective-permute-done | bytes 131104 | tf_op jit(solution)/shard_map/ppermute | solution.py:41
  7.9 1.3 %collective-permute-start.16 = (bf16[512,128]{1,0:T(8,128)(2,1)S(1)}, bf16[512,128]{1,0:T(8,128)(2,1)S(1)}, u32[]{:S(2)}, u32[]{:S(2)}) collective-permute-start(bf16[512,128]{1,0:T(8,128)(2,1)S(1)} %collective-permute-done.15.a_ref.z_own), channel_id=1, source_target_pairs={{0,8},{1,9},{2,10},{3,11},{4,12},{5,13},{6,14},{7,15},{8,0},{9,1},... | collective-permute-start | bytes 393224 | tf_op jit(solution)/shard_map/ppermute | solution.py:41
  9.2 2.8 %collective-permute-start.12 = (bf16[2,512,128]{2,1,0:T(8,128)(2,1)S(1)}, bf16[2,512,128]{2,1,0:T(8,128)(2,1)S(1)}, u32[]{:S(2)}, u32[]{:S(2)}) collective-permute-start(bf16[2,512,128]{2,1,0:T(8,128)(2,1)S(1)} %shard_map.102), channel_id=1, source_target_pairs={{0,1},{1,2},{2,3},{3,0},{4,5},{5,6},{6,7},{7,4},{8,11},{9,8},{10,9... | collective-permute-start | bytes 786440 | tf_op jit(solution)/shard_map/ppermute | solution.py:41
  12.0 0.0 collective-permute-done.16.b_ref
  12.0 1.0 collective-permute-start.17
  13.0 2.3 %collective-permute-done.12.pair_ref.pair = bf16[2,512,128]{2,1,0:T(8,128)(2,1)S(1)} collective-permute-done((bf16[2,512,128]{2,1,0:T(8,128)(2,1)S(1)}, bf16[2,512,128]{2,1,0:T(8,128)(2,1)S(1)}, u32[]{:S(2)}, u32[]{:S(2)}) %collective-permute-start.12) | collective-permute-done | bytes 262176 | tf_op jit(solution)/shard_map/ppermute | solution.py:41
  15.3 1.5 %collective-permute-start.13 = (bf16[2,512,128]{2,1,0:T(8,128)(2,1)S(1)}, bf16[2,512,128]{2,1,0:T(8,128)(2,1)S(1)}, u32[]{:S(2)}, u32[]{:S(2)}) collective-permute-start(bf16[2,512,128]{2,1,0:T(8,128)(2,1)S(1)} %collective-permute-done.12.pair_ref.pair), channel_id=1, source_target_pairs={{0,8},{1,9},{2,10},{3,11},{4,12},{5,13},{6,14},{7,15},{8,0},{9,1},... | collective-permute-start | bytes 786440 | tf_op jit(solution)/shard_map/ppermute | solution.py:41
  16.9 1.3 %collective-permute-done.17.pair_ref.z_pair = bf16[2,512,128]{2,1,0:T(8,128)(2,1)S(1)} collective-permute-done((bf16[2,512,128]{2,1,0:T(8,128)(2,1)S(1)}, bf16[2,512,128]{2,1,0:T(8,128)(2,1)S(1)}, u32[]{:S(2)}, u32[]{:S(2)}) %collective-permute-start.17) | collective-permute-done | bytes 262176 | tf_op jit(solution)/shard_map/ppermute | solution.py:41
  18.1 1.5 %collective-permute-start.18 = (bf16[2,512,128]{2,1,0:T(8,128)(2,1)S(1)}, bf16[2,512,128]{2,1,0:T(8,128)(2,1)S(1)}, u32[]{:S(2)}, u32[]{:S(2)}) collective-permute-start(bf16[2,512,128]{2,1,0:T(8,128)(2,1)S(1)} %collective-permute-done.17.pair_ref.z_pair), channel_id=1, source_target_pairs={{0,8},{1,9},{2,10},{3,11},{4,12},{5,13},{6,14},{7,15},{8,0},{9,1},... | collective-permute-start | bytes 786440 | tf_op jit(solution)/shard_map/ppermute | solution.py:41
  19.7 1.7 %collective-permute-start.14 = (bf16[512,128]{1,0:T(8,128)(2,1)S(1)}, bf16[512,128]{1,0:T(8,128)(2,1)S(1)}, u32[]{:S(2)}, u32[]{:S(2)}) collective-permute-start(bf16[512,128]{1,0:T(8,128)(2,1)S(1)} %shard_map.103), channel_id=1, source_target_pairs={{0,1},{1,2},{2,3},{3,0},{4,5},{5,6},{6,7},{7,4},{8,11},{9,8},{10,9... | collective-permute-start | bytes 393224 | tf_op jit(solution)/shard_map/ppermute | solution.py:41
  21.4 0.5 collective-permute-start.19
  21.8 3.4 %collective-permute-start = (bf16[512,256]{1,0:T(8,128)(2,1)S(1)}, bf16[512,256]{1,0:T(8,128)(2,1)S(1)}, u32[]{:S(2)}, u32[]{:S(2)}) collective-permute-start(bf16[512,256]{1,0:T(8,128)(2,1)S(1)} %get-tuple-element.15.a_ref), channel_id=1, source_target_pairs={{0,16},{1,17},{2,18},{3,19},{4,20},{5,21},{6,22},{7,23},{8,24},{9,... | collective-permute-start | bytes 786440 | tf_op jit(solution)/shard_map/ppermute | solution.py:41
  25.3 3.7 %shard_map.93.g_ref = bf16[16,1024,256]{2,1,0:T(8,128)(2,1)S(1)} custom-call(bf16[1024,16,256]{2,1,0:T(8,128)(2,1)} %bitcast.11), custom_call_target="tpu_custom_call" | custom-call | tf_op jit(solution)/shard_map/pallas_call | solution.py:237
  29.0 0.0 collective-permute-done.13.other
  29.0 0.0 collective-permute-done.19.z_far
  29.0 0.3 shard_map.106.l_ref
  29.4 2.0 %shard_map.107 = bf16[5,512,256]{2,1,0:T(8,128)(2,1)S(1)} custom-call(bf16[16,1024,256]{2,1,0:T(8,128)(2,1)S(1)} %shard_map.93.g_ref, bf16[512,1024]{1,0:T(8,128)(2,1)S(1)} %shard_map.106.l_ref), custom_call_target="tpu_custom_call" | custom-call | tf_op jit(solution)/shard_map/pallas_call | solution.py:237
  31.3 0.3 collective-permute-start.20
  31.6 0.3 collective-permute-start.5
  31.9 0.1 collective-permute-done.a_ref.z
  32.0 0.5 collective-permute-start.1
  32.5 1.2 %shard_map.109 = bf16[3,512,256]{2,1,0:T(8,128)(2,1)S(1)} custom-call(bf16[16,1024,256]{2,1,0:T(8,128)(2,1)S(1)} %shard_map.93.g_ref, bf16[512,1024]{1,0:T(8,128)(2,1)S(1)} %shard_map.106.l_ref), custom_call_target="tpu_custom_call" | custom-call | tf_op jit(solution)/shard_map/pallas_call | solution.py:237
  33.7 0.1 collective-permute-start.23
  33.8 1.0 collective-permute-done.5.b_ref
  34.9 2.5 %collective-permute-start.6 = (bf16[2,512,256]{2,1,0:T(8,128)(2,1)S(1)}, bf16[2,512,256]{2,1,0:T(8,128)(2,1)S(1)}, u32[]{:S(2)}, u32[]{:S(2)}) collective-permute-start(bf16[2,512,256]{2,1,0:T(8,128)(2,1)S(1)} %shard_map.97.p0), channel_id=1, source_target_pairs={{0,32},{1,33},{2,34},{3,35},{4,36},{5,37},{6,38},{7,39},{8,104},{9... | collective-permute-start | bytes 1572872 | tf_op jit(solution)/shard_map/ppermute | solution.py:41
  37.4 0.0 collective-permute-done.1.b_ref.zs
  37.4 0.6 collective-permute-start.2
  38.1 5.5 %collective-permute-done.6.pair_ref.x = bf16[2,512,256]{2,1,0:T(8,128)(2,1)S(1)} collective-permute-done((bf16[2,512,256]{2,1,0:T(8,128)(2,1)S(1)}, bf16[2,512,256]{2,1,0:T(8,128)(2,1)S(1)}, u32[]{:S(2)}, u32[]{:S(2)}) %collective-permute-start.6) | collective-permute-done | bytes 524320 | tf_op jit(solution)/shard_map/ppermute | solution.py:41
  43.5 3.2 %collective-permute-start.8 = (bf16[512,256]{1,0:T(8,128)(2,1)S(1)}, bf16[512,256]{1,0:T(8,128)(2,1)S(1)}, u32[]{:S(2)}, u32[]{:S(2)}) collective-permute-start(bf16[512,256]{1,0:T(8,128)(2,1)S(1)} %shard_map.98), channel_id=1, source_target_pairs={{0,32},{1,33},{2,34},{3,35},{4,36},{5,37},{6,38},{7,39},{8,104},{9... | collective-permute-start | bytes 786440 | tf_op jit(solution)/shard_map/ppermute | solution.py:41
  46.7 2.4 %collective-permute-done.2.pair_ref.zx = bf16[2,512,256]{2,1,0:T(8,128)(2,1)S(1)} collective-permute-done((bf16[2,512,256]{2,1,0:T(8,128)(2,1)S(1)}, bf16[2,512,256]{2,1,0:T(8,128)(2,1)S(1)}, u32[]{:S(2)}, u32[]{:S(2)}) %collective-permute-start.2) | collective-permute-done | bytes 524320 | tf_op jit(solution)/shard_map/ppermute | solution.py:41
  49.2 3.2 %collective-permute-start.3 = (bf16[512,256]{1,0:T(8,128)(2,1)S(1)}, bf16[512,256]{1,0:T(8,128)(2,1)S(1)}, u32[]{:S(2)}, u32[]{:S(2)}) collective-permute-start(bf16[512,256]{1,0:T(8,128)(2,1)S(1)} %shard_map.96), channel_id=1, source_target_pairs={{0,32},{1,33},{2,34},{3,35},{4,36},{5,37},{6,38},{7,39},{8,104},{9... | collective-permute-start | bytes 786440 | tf_op jit(solution)/shard_map/ppermute | solution.py:41
  52.4 0.0 collective-permute-start.10
  52.4 2.3 %shard_map.110 = (bf16[2,512,256]{2,1,0:T(8,128)(2,1)}, bf16[512,256]{1,0:T(8,128)(2,1)S(1)}) custom-call(bf16[16,1024,256]{2,1,0:T(8,128)(2,1)S(1)} %shard_map.93.g_ref, bf16[512,1024]{1,0:T(8,128)(2,1)S(1)} %shard_map.106.l_ref, bf16[3,512,256]{2,1,0:T(8,128)(2,1)S(1)} %collective-permute-done.23.r_ref), custom_call_target="tpu_custom_call" | custom-call | tf_op jit(solution)/shard_map/pallas_call | solution.py:237
  54.6 1.8 %collective-permute-start.24 = (bf16[2,512,256]{2,1,0:T(8,128)(2,1)}, bf16[2,512,256]{2,1,0:T(8,128)(2,1)S(1)}, u32[]{:S(2)}, u32[]{:S(2)}) collective-permute-start(bf16[2,512,256]{2,1,0:T(8,128)(2,1)} %get-tuple-element.20), channel_id=1, source_target_pairs={{0,32},{1,33},{2,34},{3,35},{4,36},{5,37},{6,38},{7,39},{8,104},{9... | collective-permute-start | bytes 1572872 | tf_op jit(solution)/shard_map/ppermute | solution.py:41
  56.5 2.4 %collective-permute-start.9 = (bf16[512,256]{1,0:T(8,128)(2,1)S(1)}, bf16[512,256]{1,0:T(8,128)(2,1)S(1)}, u32[]{:S(2)}, u32[]{:S(2)}) collective-permute-start(bf16[512,256]{1,0:T(8,128)(2,1)S(1)} %collective-permute-done.8.f), channel_id=1, source_target_pairs={{0,8},{1,9},{2,10},{3,11},{4,12},{5,13},{6,14},{7,15},{8,0},{9,1},... | collective-permute-start | bytes 786440 | tf_op jit(solution)/shard_map/ppermute | solution.py:41
  58.8 0.0 collective-permute-start.4
  58.9 2.5 %shard_map.108 = (bf16[2,512,256]{2,1,0:T(8,128)(2,1)}, f32[512,256]{1,0:T(8,128)S(1)}, f32[512,256]{1,0:T(8,128)S(1)}, f32[512,256]{1,0:T(8,128)S(1)}) custom-call(bf16[16,1024,256]{2,1,0:T(8,128)(2,1)S(1)} %shard_map.93.g_ref, bf16[512,1024]{1,0:T(8,128)(2,1)S(1)} %shard_map.106.l_ref, bf16[5,512,256]{2,1,0:T(8,128)(2,1)S(1)} %collective-permute-done.20.r_ref), custom_call_target="tpu_custom_call" | custom-call | tf_op jit(solution)/shard_map/pallas_call | solution.py:237
  61.4 0.8 copy-done.2
  62.2 0.8 copy-done.6
  63.0 0.4 collective-permute-start.21
  63.4 4.0 %shard_map.99.part_ref = f32[1024,512]{1,0:T(8,128)S(1)} custom-call(bf16[16,1024,256]{2,1,0:T(8,128)(2,1)S(1)} %shard_map.93.g_ref, bf16[2,512,256]{2,1,0:T(8,128)(2,1)S(1)} %shard_map.97.p0, bf16[2,512,256]{2,1,0:T(8,128)(2,1)S(1)} %collective-permute-done.6.pair_ref.x, bf16[2,512,256]{2,1,0:T(8,128)(2,1)S(1)} %collective-permute-done.7.xs, ...), custom_call_target="tpu_custom_call" | custom-call | tf_op jit(solution)/shard_map/pallas_call | solution.py:237
  67.4 1.7 %shard_map.100 = bf16[8,128,512]{2,1,0:T(8,128)(2,1)} custom-call(bf16[16,1024,256]{2,1,0:T(8,128)(2,1)S(1)} %shard_map.93.g_ref, bf16[512,256]{1,0:T(8,128)(2,1)S(1)} %collective-permute-done.3.zf, bf16[512,256]{1,0:T(8,128)(2,1)S(1)} %collective-permute-done.4.zfs, f32[1024,512]{1,0:T(8,128)S(1)} %shard_map.99.part_ref), custom_call_target="tpu_custom_call" | custom-call | tf_op jit(solution)/shard_map/pallas_call | solution.py:237
  69.2 4.1 %all-to-all-start = ((bf16[8,128,512]{2,1,0:T(8,128)(2,1)}), bf16[8,128,512]{2,1,0:T(8,128)(2,1)S(1)}, u32[]{:S(2)}, u32[]{:S(2)}) async-start(bf16[8,128,512]{2,1,0:T(8,128)(2,1)} %shard_map.100), calls=%async_computation | async-start | bytes 2097152 | tf_op jit(solution)/shard_map/all_to_all | solution.py:316
  73.2 0.0 copy-start.1
  73.3 0.6 collective-permute-start.25
  73.8 1.6 %collective-permute-start.27 = (bf16[512,256]{1,0:T(8,128)(2,1)S(1)}, bf16[512,256]{1,0:T(8,128)(2,1)S(1)}, u32[]{:S(2)}, u32[]{:S(2)}) collective-permute-start(bf16[512,256]{1,0:T(8,128)(2,1)S(1)} %get-tuple-element.22), channel_id=1, source_target_pairs={{0,16},{1,17},{2,18},{3,19},{4,20},{5,21},{6,22},{7,23},{8,24},{9,... | collective-permute-start | bytes 786440 | tf_op jit(solution)/shard_map/ppermute | solution.py:41
  75.4 0.4 collective-permute-start.22
  75.8 16.5 %collective-permute-done.27.refs_1_ = bf16[512,256]{1,0:T(8,128)(2,1)S(1)} collective-permute-done((bf16[512,256]{1,0:T(8,128)(2,1)S(1)}, bf16[512,256]{1,0:T(8,128)(2,1)S(1)}, u32[]{:S(2)}, u32[]{:S(2)}) %collective-permute-start.27) | collective-permute-done | bytes 262176 | tf_op jit(solution)/shard_map/ppermute | solution.py:41
  92.3 1.0 copy-done.3
  93.3 0.7 shard_map.112
  94.1 1.0 collective-permute-start.28
  95.1 0.8 shard_map.111
  95.9 1.4 %collective-permute-start.26 = (bf16[512,256]{1,0:T(8,128)(2,1)}, bf16[512,256]{1,0:T(8,128)(2,1)S(1)}, u32[]{:S(2)}, u32[]{:S(2)}) collective-permute-start(bf16[512,256]{1,0:T(8,128)(2,1)} %shard_map.111), channel_id=1, source_target_pairs={{0,16},{1,17},{2,18},{3,19},{4,20},{5,21},{6,22},{7,23},{8,24},{9,... | collective-permute-start | bytes 786440 | tf_op jit(solution)/shard_map/ppermute | solution.py:41
  97.2 0.8 shard_map.101
  98.0 4.4 %collective-permute-done.28.far = bf16[512,256]{1,0:T(8,128)(2,1)S(1)} collective-permute-done((bf16[512,256]{1,0:T(8,128)(2,1)}, bf16[512,256]{1,0:T(8,128)(2,1)S(1)}, u32[]{:S(2)}, u32[]{:S(2)}) %collective-permute-start.28) | collective-permute-done | bytes 262176 | tf_op jit(solution)/shard_map/ppermute | solution.py:41
  102.5 1.7 %collective-permute-done.26.over = bf16[512,256]{1,0:T(8,128)(2,1)S(1)} collective-permute-done((bf16[512,256]{1,0:T(8,128)(2,1)}, bf16[512,256]{1,0:T(8,128)(2,1)S(1)}, u32[]{:S(2)}, u32[]{:S(2)}) %collective-permute-start.26) | collective-permute-done | bytes 262176 | tf_op jit(solution)/shard_map/ppermute | solution.py:41
  104.2 0.0 copy-start.4
  104.2 1.0 copy-done.4
  105.2 1.0 copy-done.5
  106.2 1.0 copy-done.7
  107.3 3.2 %shard_map.113 = (f32[1024,128]{1,0:T(8,128)}, f32[1024,128]{1,0:T(8,128)}, f32[1024,128]{1,0:T(8,128)}) custom-call(bf16[512,512]{1,0:T(8,128)(2,1)S(1)} %copy-done.1, f32[512,256]{1,0:T(8,128)S(1)} %copy-done.7, bf16[2,512,256]{2,1,0:T(8,128)(2,1)} %collective-permute-done.21.pair, bf16[2,512,256]{2,1,0:T(8,128)(2,1)} %collective-permute-done.22.other, ...), custom_call_target="tpu_custom_call" | custom-call | tf_op jit(solution)/shard_map/pallas_call | solution.py:237
  (33 shorter events, 0.2 us)
Async XLA Ops:
  2.2 5.7 %collective-permute-start.15 = (bf16[512,128]{1,0:T(8,128)(2,1)S(1)}, bf16[512,128]{1,0:T(8,128)(2,1)S(1)}, u32[]{:S(2)}, u32[]{:S(2)}) collective-permute-start(bf16[512,128]{1,0:T(8,128)(2,1)S(1)} %get-tuple-element.16.a_ref.own), channel_id=1, source_target_pairs={{0,4},{1,5},{2,6},{3,7},{4,0},{5,1},{6,2},{7,3},{8,12},{9,13},{10,... | collective-permute-start | bytes 393224 | tf_op jit(solution)/shard_map/ppermute | solution.py:41
  4.7 4.5 %collective-permute-start.11 = (bf16[512,128]{1,0:T(8,128)(2,1)S(1)}, bf16[512,128]{1,0:T(8,128)(2,1)S(1)}, u32[]{:S(2)}, u32[]{:S(2)}) collective-permute-start(bf16[512,128]{1,0:T(8,128)(2,1)S(1)} %get-tuple-element.16.a_ref.own), channel_id=1, source_target_pairs={{0,8},{1,9},{2,10},{3,11},{4,12},{5,13},{6,14},{7,15},{8,0},{9,1},... | collective-permute-start | bytes 393224 | tf_op jit(solution)/shard_map/ppermute | solution.py:41
  7.9 4.1 %collective-permute-start.16 = (bf16[512,128]{1,0:T(8,128)(2,1)S(1)}, bf16[512,128]{1,0:T(8,128)(2,1)S(1)}, u32[]{:S(2)}, u32[]{:S(2)}) collective-permute-start(bf16[512,128]{1,0:T(8,128)(2,1)S(1)} %collective-permute-done.15.a_ref.z_own), channel_id=1, source_target_pairs={{0,8},{1,9},{2,10},{3,11},{4,12},{5,13},{6,14},{7,15},{8,0},{9,1},... | collective-permute-start | bytes 393224 | tf_op jit(solution)/shard_map/ppermute | solution.py:41
  9.2 6.1 %collective-permute-start.12 = (bf16[2,512,128]{2,1,0:T(8,128)(2,1)S(1)}, bf16[2,512,128]{2,1,0:T(8,128)(2,1)S(1)}, u32[]{:S(2)}, u32[]{:S(2)}) collective-permute-start(bf16[2,512,128]{2,1,0:T(8,128)(2,1)S(1)} %shard_map.102), channel_id=1, source_target_pairs={{0,1},{1,2},{2,3},{3,0},{4,5},{5,6},{6,7},{7,4},{8,11},{9,8},{10,9... | collective-permute-start | bytes 786440 | tf_op jit(solution)/shard_map/ppermute | solution.py:41
  12.0 6.1 %collective-permute-start.17 = (bf16[2,512,128]{2,1,0:T(8,128)(2,1)S(1)}, bf16[2,512,128]{2,1,0:T(8,128)(2,1)S(1)}, u32[]{:S(2)}, u32[]{:S(2)}) collective-permute-start(bf16[2,512,128]{2,1,0:T(8,128)(2,1)S(1)} %shard_map.104), channel_id=1, source_target_pairs={{0,1},{1,2},{2,3},{3,0},{4,5},{5,6},{6,7},{7,4},{8,11},{9,8},{10,9... | collective-permute-start | bytes 786440 | tf_op jit(solution)/shard_map/ppermute | solution.py:41
  15.3 13.7 %collective-permute-start.13 = (bf16[2,512,128]{2,1,0:T(8,128)(2,1)S(1)}, bf16[2,512,128]{2,1,0:T(8,128)(2,1)S(1)}, u32[]{:S(2)}, u32[]{:S(2)}) collective-permute-start(bf16[2,512,128]{2,1,0:T(8,128)(2,1)S(1)} %collective-permute-done.12.pair_ref.pair), channel_id=1, source_target_pairs={{0,8},{1,9},{2,10},{3,11},{4,12},{5,13},{6,14},{7,15},{8,0},{9,1},... | collective-permute-start | bytes 786440 | tf_op jit(solution)/shard_map/ppermute | solution.py:41
  18.1 10.9 %collective-permute-start.18 = (bf16[2,512,128]{2,1,0:T(8,128)(2,1)S(1)}, bf16[2,512,128]{2,1,0:T(8,128)(2,1)S(1)}, u32[]{:S(2)}, u32[]{:S(2)}) collective-permute-start(bf16[2,512,128]{2,1,0:T(8,128)(2,1)S(1)} %collective-permute-done.17.pair_ref.z_pair), channel_id=1, source_target_pairs={{0,8},{1,9},{2,10},{3,11},{4,12},{5,13},{6,14},{7,15},{8,0},{9,1},... | collective-permute-start | bytes 786440 | tf_op jit(solution)/shard_map/ppermute | solution.py:41
  19.7 9.3 %collective-permute-start.14 = (bf16[512,128]{1,0:T(8,128)(2,1)S(1)}, bf16[512,128]{1,0:T(8,128)(2,1)S(1)}, u32[]{:S(2)}, u32[]{:S(2)}) collective-permute-start(bf16[512,128]{1,0:T(8,128)(2,1)S(1)} %shard_map.103), channel_id=1, source_target_pairs={{0,1},{1,2},{2,3},{3,0},{4,5},{5,6},{6,7},{7,4},{8,11},{9,8},{10,9... | collective-permute-start | bytes 393224 | tf_op jit(solution)/shard_map/ppermute | solution.py:41
  21.4 7.7 %collective-permute-start.19 = (bf16[512,128]{1,0:T(8,128)(2,1)S(1)}, bf16[512,128]{1,0:T(8,128)(2,1)S(1)}, u32[]{:S(2)}, u32[]{:S(2)}) collective-permute-start(bf16[512,128]{1,0:T(8,128)(2,1)S(1)} %shard_map.105), channel_id=1, source_target_pairs={{0,1},{1,2},{2,3},{3,0},{4,5},{5,6},{6,7},{7,4},{8,11},{9,8},{10,9... | collective-permute-start | bytes 393224 | tf_op jit(solution)/shard_map/ppermute | solution.py:41
  21.8 10.1 %collective-permute-start = (bf16[512,256]{1,0:T(8,128)(2,1)S(1)}, bf16[512,256]{1,0:T(8,128)(2,1)S(1)}, u32[]{:S(2)}, u32[]{:S(2)}) collective-permute-start(bf16[512,256]{1,0:T(8,128)(2,1)S(1)} %get-tuple-element.15.a_ref), channel_id=1, source_target_pairs={{0,16},{1,17},{2,18},{3,19},{4,20},{5,21},{6,22},{7,23},{8,24},{9,... | collective-permute-start | bytes 786440 | tf_op jit(solution)/shard_map/ppermute | solution.py:41
  31.3 27.5 %collective-permute-start.20 = (bf16[5,512,256]{2,1,0:T(8,128)(2,1)S(1)}, bf16[5,512,256]{2,1,0:T(8,128)(2,1)S(1)}, u32[]{:S(2)}, u32[]{:S(2)}) collective-permute-start(bf16[5,512,256]{2,1,0:T(8,128)(2,1)S(1)} %shard_map.107), channel_id=1, source_target_pairs={{0,8},{1,9},{2,10},{3,11},{4,12},{5,13},{6,14},{7,15},{8,0},{9,1},... | collective-permute-start | bytes 3932168 | tf_op jit(solution)/shard_map/ppermute | solution.py:41
  31.6 3.2 %collective-permute-start.5 = (bf16[512,256]{1,0:T(8,128)(2,1)S(1)}, bf16[512,256]{1,0:T(8,128)(2,1)S(1)}, u32[]{:S(2)}, u32[]{:S(2)}) collective-permute-start(bf16[512,256]{1,0:T(8,128)(2,1)S(1)} %get-tuple-element.15.a_ref), channel_id=1, source_target_pairs={{0,8},{1,9},{2,10},{3,11},{4,12},{5,13},{6,14},{7,15},{8,0},{9,1},... | collective-permute-start | bytes 786440 | tf_op jit(solution)/shard_map/ppermute | solution.py:41
  32.0 5.4 %collective-permute-start.1 = (bf16[512,256]{1,0:T(8,128)(2,1)S(1)}, bf16[512,256]{1,0:T(8,128)(2,1)S(1)}, u32[]{:S(2)}, u32[]{:S(2)}) collective-permute-start(bf16[512,256]{1,0:T(8,128)(2,1)S(1)} %collective-permute-done.a_ref.z), channel_id=1, source_target_pairs={{0,8},{1,9},{2,10},{3,11},{4,12},{5,13},{6,14},{7,15},{8,0},{9,1},... | collective-permute-start | bytes 786440 | tf_op jit(solution)/shard_map/ppermute | solution.py:41
  33.7 18.6 %collective-permute-start.23 = (bf16[3,512,256]{2,1,0:T(8,128)(2,1)S(1)}, bf16[3,512,256]{2,1,0:T(8,128)(2,1)S(1)}, u32[]{:S(2)}, u32[]{:S(2)}) collective-permute-start(bf16[3,512,256]{2,1,0:T(8,128)(2,1)S(1)} %shard_map.109), channel_id=1, source_target_pairs={{0,8},{1,9},{2,10},{3,11},{4,12},{5,13},{6,14},{7,15},{8,0},{9,1},... | collective-permute-start | bytes 2359304 | tf_op jit(solution)/shard_map/ppermute | solution.py:41
  34.9 8.7 %collective-permute-start.6 = (bf16[2,512,256]{2,1,0:T(8,128)(2,1)S(1)}, bf16[2,512,256]{2,1,0:T(8,128)(2,1)S(1)}, u32[]{:S(2)}, u32[]{:S(2)}) collective-permute-start(bf16[2,512,256]{2,1,0:T(8,128)(2,1)S(1)} %shard_map.97.p0), channel_id=1, source_target_pairs={{0,32},{1,33},{2,34},{3,35},{4,36},{5,37},{6,38},{7,39},{8,104},{9... | collective-permute-start | bytes 1572872 | tf_op jit(solution)/shard_map/ppermute | solution.py:41
  37.4 11.7 %collective-permute-start.2 = (bf16[2,512,256]{2,1,0:T(8,128)(2,1)S(1)}, bf16[2,512,256]{2,1,0:T(8,128)(2,1)S(1)}, u32[]{:S(2)}, u32[]{:S(2)}) collective-permute-start(bf16[2,512,256]{2,1,0:T(8,128)(2,1)S(1)} %shard_map.95), channel_id=1, source_target_pairs={{0,32},{1,33},{2,34},{3,35},{4,36},{5,37},{6,38},{7,39},{8,104},{9... | collective-permute-start | bytes 1572872 | tf_op jit(solution)/shard_map/ppermute | solution.py:41
  43.5 11.1 %collective-permute-start.8 = (bf16[512,256]{1,0:T(8,128)(2,1)S(1)}, bf16[512,256]{1,0:T(8,128)(2,1)S(1)}, u32[]{:S(2)}, u32[]{:S(2)}) collective-permute-start(bf16[512,256]{1,0:T(8,128)(2,1)S(1)} %shard_map.98), channel_id=1, source_target_pairs={{0,32},{1,33},{2,34},{3,35},{4,36},{5,37},{6,38},{7,39},{8,104},{9... | collective-permute-start | bytes 786440 | tf_op jit(solution)/shard_map/ppermute | solution.py:41
  46.7 16.3 %collective-permute-start.7 = (bf16[2,512,256]{2,1,0:T(8,128)(2,1)S(1)}, bf16[2,512,256]{2,1,0:T(8,128)(2,1)S(1)}, u32[]{:S(2)}, u32[]{:S(2)}) collective-permute-start(bf16[2,512,256]{2,1,0:T(8,128)(2,1)S(1)} %collective-permute-done.6.pair_ref.x), channel_id=1, source_target_pairs={{0,8},{1,9},{2,10},{3,11},{4,12},{5,13},{6,14},{7,15},{8,0},{9,1},... | collective-permute-start | bytes 1572872 | tf_op jit(solution)/shard_map/ppermute | solution.py:41
  49.2 7.3 %collective-permute-start.3 = (bf16[512,256]{1,0:T(8,128)(2,1)S(1)}, bf16[512,256]{1,0:T(8,128)(2,1)S(1)}, u32[]{:S(2)}, u32[]{:S(2)}) collective-permute-start(bf16[512,256]{1,0:T(8,128)(2,1)S(1)} %shard_map.96), channel_id=1, source_target_pairs={{0,32},{1,33},{2,34},{3,35},{4,36},{5,37},{6,38},{7,39},{8,104},{9... | collective-permute-start | bytes 786440 | tf_op jit(solution)/shard_map/ppermute | solution.py:41
  52.4 11.1 %collective-permute-start.10 = (bf16[2,512,256]{2,1,0:T(8,128)(2,1)S(1)}, bf16[2,512,256]{2,1,0:T(8,128)(2,1)S(1)}, u32[]{:S(2)}, u32[]{:S(2)}) collective-permute-start(bf16[2,512,256]{2,1,0:T(8,128)(2,1)S(1)} %collective-permute-done.2.pair_ref.zx), channel_id=1, source_target_pairs={{0,8},{1,9},{2,10},{3,11},{4,12},{5,13},{6,14},{7,15},{8,0},{9,1},... | collective-permute-start | bytes 1572872 | tf_op jit(solution)/shard_map/ppermute | solution.py:41
  54.6 18.6 %collective-permute-start.24 = (bf16[2,512,256]{2,1,0:T(8,128)(2,1)}, bf16[2,512,256]{2,1,0:T(8,128)(2,1)S(1)}, u32[]{:S(2)}, u32[]{:S(2)}) collective-permute-start(bf16[2,512,256]{2,1,0:T(8,128)(2,1)} %get-tuple-element.20), channel_id=1, source_target_pairs={{0,32},{1,33},{2,34},{3,35},{4,36},{5,37},{6,38},{7,39},{8,104},{9... | collective-permute-start | bytes 1572872 | tf_op jit(solution)/shard_map/ppermute | solution.py:41
  56.5 7.0 %collective-permute-start.9 = (bf16[512,256]{1,0:T(8,128)(2,1)S(1)}, bf16[512,256]{1,0:T(8,128)(2,1)S(1)}, u32[]{:S(2)}, u32[]{:S(2)}) collective-permute-start(bf16[512,256]{1,0:T(8,128)(2,1)S(1)} %collective-permute-done.8.f), channel_id=1, source_target_pairs={{0,8},{1,9},{2,10},{3,11},{4,12},{5,13},{6,14},{7,15},{8,0},{9,1},... | collective-permute-start | bytes 786440 | tf_op jit(solution)/shard_map/ppermute | solution.py:41
  58.8 8.6 %collective-permute-start.4 = (bf16[512,256]{1,0:T(8,128)(2,1)S(1)}, bf16[512,256]{1,0:T(8,128)(2,1)S(1)}, u32[]{:S(2)}, u32[]{:S(2)}) collective-permute-start(bf16[512,256]{1,0:T(8,128)(2,1)S(1)} %collective-permute-done.3.zf), channel_id=1, source_target_pairs={{0,8},{1,9},{2,10},{3,11},{4,12},{5,13},{6,14},{7,15},{8,0},{9,1},... | collective-permute-start | bytes 786440 | tf_op jit(solution)/shard_map/ppermute | solution.py:41
  61.4 0.8 copy-start.2
  62.2 0.8 copy-start.6
  63.0 12.5 %collective-permute-start.21 = (bf16[2,512,256]{2,1,0:T(8,128)(2,1)}, bf16[2,512,256]{2,1,0:T(8,128)(2,1)}, u32[]{:S(2)}, u32[]{:S(2)}) collective-permute-start(bf16[2,512,256]{2,1,0:T(8,128)(2,1)} %get-tuple-element.18), channel_id=1, source_target_pairs={{0,32},{1,33},{2,34},{3,35},{4,36},{5,37},{6,38},{7,39},{8,104},{9... | collective-permute-start | bytes 1572872 | tf_op jit(solution)/shard_map/ppermute | solution.py:41
  69.2 28.1 %all-to-all-start = ((bf16[8,128,512]{2,1,0:T(8,128)(2,1)}), bf16[8,128,512]{2,1,0:T(8,128)(2,1)S(1)}, u32[]{:S(2)}, u32[]{:S(2)}) async-start(bf16[8,128,512]{2,1,0:T(8,128)(2,1)} %shard_map.100), calls=%async_computation | async-start | bytes 2097152 | tf_op jit(solution)/shard_map/all_to_all | solution.py:316
  73.2 30.9 %copy-start = (f32[512,1,1,256]{3,2,1,0:T(1,128)S(1)}, f32[512,1,1,256]{3,2,1,0:T(1,128)}, u32[]{:S(2)}) copy-start(f32[512,1,1,256]{3,2,1,0:T(1,128)} %param.8) | copy-start | bytes 1572868
  73.2 30.9 %copy-start.1 = (bf16[512,512]{1,0:T(8,128)(2,1)S(1)}, bf16[512,512]{1,0:T(8,128)(2,1)}, u32[]{:S(2)}) copy-start(bf16[512,512]{1,0:T(8,128)(2,1)} %constant.2.clone.h_hbm.h_ref) | copy-start | bytes 1572868
  73.3 21.8 %collective-permute-start.25 = (bf16[2,512,256]{2,1,0:T(8,128)(2,1)S(1)}, bf16[2,512,256]{2,1,0:T(8,128)(2,1)S(1)}, u32[]{:S(2)}, u32[]{:S(2)}) collective-permute-start(bf16[2,512,256]{2,1,0:T(8,128)(2,1)S(1)} %collective-permute-done.24.pair), channel_id=1, source_target_pairs={{0,8},{1,9},{2,10},{3,11},{4,12},{5,13},{6,14},{7,15},{8,0},{9,1},... | collective-permute-start | bytes 1572872 | tf_op jit(solution)/shard_map/ppermute | solution.py:41
  73.8 18.5 %collective-permute-start.27 = (bf16[512,256]{1,0:T(8,128)(2,1)S(1)}, bf16[512,256]{1,0:T(8,128)(2,1)S(1)}, u32[]{:S(2)}, u32[]{:S(2)}) collective-permute-start(bf16[512,256]{1,0:T(8,128)(2,1)S(1)} %get-tuple-element.22), channel_id=1, source_target_pairs={{0,16},{1,17},{2,18},{3,19},{4,20},{5,21},{6,22},{7,23},{8,24},{9,... | collective-permute-start | bytes 786440 | tf_op jit(solution)/shard_map/ppermute | solution.py:41
  75.4 28.7 %collective-permute-start.22 = (bf16[2,512,256]{2,1,0:T(8,128)(2,1)}, bf16[2,512,256]{2,1,0:T(8,128)(2,1)}, u32[]{:S(2)}, u32[]{:S(2)}) collective-permute-start(bf16[2,512,256]{2,1,0:T(8,128)(2,1)} %collective-permute-done.21.pair), channel_id=1, source_target_pairs={{0,8},{1,9},{2,10},{3,11},{4,12},{5,13},{6,14},{7,15},{8,0},{9,1},... | collective-permute-start | bytes 1572872 | tf_op jit(solution)/shard_map/ppermute | solution.py:41
  92.3 1.0 copy-start.3
  94.1 8.4 %collective-permute-start.28 = (bf16[512,256]{1,0:T(8,128)(2,1)}, bf16[512,256]{1,0:T(8,128)(2,1)S(1)}, u32[]{:S(2)}, u32[]{:S(2)}) collective-permute-start(bf16[512,256]{1,0:T(8,128)(2,1)} %shard_map.112), channel_id=1, source_target_pairs={{0,64},{1,65},{2,66},{3,67},{4,68},{5,69},{6,70},{7,71},{8,72},{9,... | collective-permute-start | bytes 786440 | tf_op jit(solution)/shard_map/ppermute | solution.py:41
  95.9 8.3 %collective-permute-start.26 = (bf16[512,256]{1,0:T(8,128)(2,1)}, bf16[512,256]{1,0:T(8,128)(2,1)S(1)}, u32[]{:S(2)}, u32[]{:S(2)}) collective-permute-start(bf16[512,256]{1,0:T(8,128)(2,1)} %shard_map.111), channel_id=1, source_target_pairs={{0,16},{1,17},{2,18},{3,19},{4,20},{5,21},{6,22},{7,23},{8,24},{9,... | collective-permute-start | bytes 786440 | tf_op jit(solution)/shard_map/ppermute | solution.py:41
  104.2 1.0 copy-start.4
  105.2 1.0 copy-start.5
  106.2 1.0 copy-start.7

commit v3 on v2

--- a/solution.py
+++ b/solution.py
@@ -89,20 +89,10 @@
     turn_ref[...] = (turned * (1.0 / math.sqrt(LATENT))).astype(BF)
 
 
-def swap_body(g_ref, o_ref, held, sems):
-    parts = sems.shape[0]
-    size = TOK // parts
-    copies = [
-        pltpu.make_async_copy(
-            g_ref.at[pl.ds(part * size, size)], held.at[pl.ds(part * size, size)], sems.at[part]
-        )
-        for part in range(parts)
-    ]
-    for copy in copies:
-        copy.start()
-    for part, copy in enumerate(copies):
-        copy.wait()
-        rows = held[part * size : part * size + size]
+def swap_body(g_ref, o_ref):
+    size = 128
+    for part in range(TOK // size):
+        rows = g_ref[part * size : part * size + size]
         o_ref[:, part * size : part * size + size] = jnp.swapaxes(rows, 0, 1)
 
 
@@ -111,18 +101,18 @@
     o_ref[1] = b_ref[...]
 
 
+def pack_beside_body(g_hbm, a_ref, b_ref, o_ref):
+    pack_body(a_ref, b_ref, o_ref)
+
+
 def cut_body(pair_ref, o_ref):
     o_ref[...] = pair_ref[0]
 
 
-def place_body(own, pair, other, far, z_own, z_pair, z_other, z_far, o_ref):
-    up, down = ahead(my_core()), ahead(1 - my_core())
-    pieces = (
-        (0, 0, own[...]), (0, down, pair[0]), (0, up, other[1]), (0, 2, far[...]),
-        (1, 0, z_own[...]), (1, down, z_pair[0]), (1, up, z_other[1]), (1, 2, z_far[...]),
-    )
-    for dl, dy, turned in pieces:
-        o_ref[:, pl.ds(pl.multiple_of(head_at(dl, dy) * 128, 128), 128)] = turned
+def place_body(*refs):
+    for place, ref in zip(((0, 0), (0, 3), (0, 1), (0, 2), (1, 0), (1, 3), (1, 1), (1, 2)), refs):
+        at = pl.multiple_of(head_at(*place) * 128, 128)
+        refs[-1][:, pl.ds(at, 128)] = ref[...]
 
 
 def turned_block(l_ref, g_ref, block):
@@ -170,7 +160,7 @@
     return total
 
 
-def latent_body(g_ref, p0, x, xs, f, fs, z, zs, zx, zxs, o_ref):
+def latent_body(g_ref, p0, x, xs, f, fs, z, zs, zx, zxs, zf, zfs, *refs):
     core = my_core()
     rest = 1 - core
     up, down = ahead(core), ahead(rest)
@@ -178,37 +168,34 @@
         (p0[0], 0, 0, core), (p0[1], 0, 0, rest), (x[0], down, 0, core), (x[1], down, 0, rest),
         (xs[0], up, 0, rest), (xs[1], up, 0, core), (f[...], 2, 0, core), (fs[...], 2, 0, rest),
         (z[...], 0, 1, core), (zs[...], 0, 1, rest), (zx[0], down, 1, core), (zx[1], down, 1, rest),
-        (zxs[0], up, 1, rest), (zxs[1], up, 1, core),
+        (zxs[0], up, 1, rest), (zxs[1], up, 1, core), (zf[...], 2, 1, core), (zfs[...], 2, 1, rest),
     ]
     for part in range(2):
-        o_ref[part * 512 : part * 512 + 512] = products(g_ref, terms, part)
-
-
-def finish_body(g_ref, zf, zfs, part_ref, o_ref):
-    core = my_core()
-    terms = [(zf[...], 2, 1, core), (zfs[...], 2, 1, 1 - core)]
-    for part in range(2):
-        total = part_ref[part * 512 : part * 512 + 512] + products(g_ref, terms, part)
-        o_ref[part * 4 : part * 4 + 4] = total.astype(BF).reshape(4, 128, LATENT)
-
-
-def total_body(r_ref, o_ref):
-    total = r_ref[0].astype(F32)
-    for peer in range(1, NZL * NY):
-        total = total + r_ref[peer].astype(F32)
-    o_ref[...] = total.astype(BF)
+        total = products(g_ref, terms, part)
+        refs[-1][part * 4 : part * 4 + 4] = total.astype(BF).reshape(4, 128, LATENT)
+    for dy, o_ref in zip((0, 1, 3, 2), refs):
+        for dl in range(NZL):
+            o_ref[dl] = refs[-1][head_at(dl, dy)]
+
+
+def meet_body(own, up, down, far, near_ref, cross_ref):
+    for dl, o_ref in enumerate((near_ref, cross_ref)):
+        total = own[dl].astype(F32) + up[dl].astype(F32) + down[dl].astype(F32) + far[dl].astype(F32)
+        o_ref[...] = total.astype(o_ref.dtype)
+
+
+def total_body(near, cross, o_ref):
+    o_ref[...] = (near[...] + cross[...].astype(F32)).astype(BF)
 
 
 def join_pair_body(base, pair, other, o_ref):
     core = my_core()
-    total = base[...] + pair[core].astype(F32) + other[core].astype(F32)
-    o_ref[...] = total.astype(BF)
-
-
-def update_body(h_ref, own, pair, other, over, far, w_ref, a_ref, b_ref, nw_ref, na_ref, nb_ref):
-    core = my_core()
-    summed = own[...] + pair[core].astype(F32) + other[core].astype(F32)
-    summed = summed + over[...].astype(F32) + far[...].astype(F32)
+    total = base[...].astype(F32) + pair[core].astype(F32) + other[core].astype(F32)
+    o_ref[...] = total.astype(o_ref.dtype)
+
+
+def update_body(h_ref, base, over, far, w_ref, a_ref, b_ref, nw_ref, na_ref, nb_ref):
+    summed = base[...] + over[...].astype(F32) + far[...].astype(F32)
     high = summed.astype(BF)
     low = (summed - high.astype(F32)).astype(BF)
     h = h_ref[...]
@@ -246,7 +233,6 @@
     flat = (1024, 128)
     block = (LATENT, COLS)
     one = [(block, BF)]
-    peers = NZL * NY
 
     far_off = [pltpu.with_memory_space_constraint(v, pltpu.HBM) for v in (h, latent, weight.reshape(flat))]
     w, turn = run(
@@ -259,47 +245,42 @@
             pltpu.SemaphoreType.DMA((3,)),
         ],
     )
-    rows_pair = [((2, LATENT, 128), BF)]
-    (l_pair,) = run(pack_body, rows_pair, turn, send(turn, dc=1))
     l_z = send(turn, dl=1)
-    l_y = send(l_pair, fan_y=1)
-    l_ys = send(l_y, dc=1)
-    (lz_pair,) = run(pack_body, rows_pair, l_z, send(l_z, dc=1))
-    l_zy = send(lz_pair, fan_y=1)
-    l_zys = send(l_zy, dc=1)
-    l_2 = send(run(cut_body, [((LATENT, 128), BF)], l_y)[0], fan_y=1)
-    l_2z = send(run(cut_body, [((LATENT, 128), BF)], l_zy)[0], fan_y=1)
+    l_up = send(turn, dy=1)
+    l_dn = send(turn, dy=-1)
+    l_2 = send(l_up, dy=1)
+    lz_up = send(l_z, dy=1)
+    lz_dn = send(l_z, dy=-1)
+    lz_2 = send(lz_dn, dy=-1)
+    rows = (turn, l_up, l_dn, l_2, l_z, lz_up, lz_dn, lz_2)
 
     pair = [((2, *block), BF)]
-    (w_pair,) = run(pack_body, pair, w, send(w, dc=1))
+    (w_pair,) = run(
+        pack_beside_body, pair,
+        pltpu.with_memory_space_constraint(out_grad[:, :, 0, :], pltpu.HBM), w, send(w, dc=1),
+        in_specs=[pl.BlockSpec(memory_space=pltpu.HBM), VM, VM],
+    )
     w_z = send(w, dz=1)
     w_x = send(w_pair, fan_x=1)
     w_zs = send(w_z, dc=1)
     (wz_pair,) = run(pack_body, pair, w_z, w_zs)
     w_zx = send(wz_pair, fan_x=1)
     w_2 = send(run(cut_body, one, w_x)[0], fan_x=1)
-    w_2z = send(run(cut_body, one, w_zx)[0], fan_x=1)
+    w_2z = send(w_2, dz=1)
     ws = [
         w_pair, w_x, send(w_x, dc=1), w_2, send(w_2, dc=1), w_z, w_zs,
         w_zx, send(w_zx, dc=1),
     ]
 
-    (grads,) = run(
-        swap_body,
-        [((16, TOK, COLS), BF)],
-        pltpu.with_memory_space_constraint(out_grad[:, :, 0, :], pltpu.HBM),
-        in_specs=[pl.BlockSpec(memory_space=pltpu.HBM)],
-        scratch=[pltpu.VMEM((TOK, 16, COLS), BF), pltpu.SemaphoreType.DMA((8,))],
-        limit=24,
-    )
-
-    (turn,) = run(place_body, [((LATENT, TOK), BF)], turn, l_y, l_ys, l_2, l_z, l_zy, l_zys, l_2z)
+    (grads,) = run(swap_body, [((16, TOK, COLS), BF)], out_grad[:, :, 0, :])
+
+    (turn,) = run(place_body, [((LATENT, TOK), BF)], *rows)
     (give,) = run(give_body(early), [((3, *block), BF)], grads, turn)
     got = send(give, dc=1)
     t_a, t_b = run(keep_body(early), pair + one, grads, turn, got)
     (give,) = run(give_body(late), [((5, *block), BF)], grads, turn)
     got = send(give, dc=1)
-    t_d, far, over, own = run(keep_body(late), pair + [(block, F32)] * 3, grads, turn, got)
+    t_d, far, over, own = run(keep_body(late), pair + one * 3, grads, turn, got)
     t_a = send(t_a, fan_x=1)
     t_b = send(t_b, dz=1)
     t_d = send(t_d, fan_x=1)
@@ -308,17 +289,23 @@
     (far,) = run(join_body, one, far, t_b)
     far = send(far, dx=2)
 
-    (partial,) = run(latent_body, [((TOK, LATENT), F32)], grads, *ws)
-    (partial,) = run(
-        finish_body, [((peers, 128, LATENT), BF)],
-        grads, w_2z, send(w_2z, dc=1), partial,
-    )
-    arrived = lax.all_to_all(partial, "head", 0, 0, tiled=True)
-    (latent_grad,) = run(total_body, [(latent.shape, BF)], arrived, home=True)
-
+    piece = (128, LATENT)
+    s_own, s_up, s_dn, s_2 = run(
+        latent_body, [((NZL, *piece), BF)] * 4,
+        grads, *ws, w_2z, send(w_2z, dc=1),
+        scratch=[pltpu.VMEM((NZL * NY, *piece), BF)],
+    )
+    s_2 = send(s_2, dy=2)
+    s_up = send(s_up, dy=1)
+    s_dn = send(s_dn, dy=-1)
+    near, cross = run(meet_body, [(piece, F32), (piece, BF)], s_own, s_up, s_dn, s_2)
+    cross = send(cross, dl=1)
+    (latent_grad,) = run(total_body, [(piece, BF)], near, cross, home=True)
+
+    (own,) = run(join_pair_body, [(block, F32)], own, t_d, send(t_d, dc=1))
     states = [s.reshape(flat) for s in (weight, moment_one, moment_two)]
     new = run(
-        update_body, [(flat, F32)] * 3, h, own, t_d, send(t_d, dc=1), over, far, *states,
+        update_body, [(flat, F32)] * 3, h, own, over, far, *states,
         limit=24, home=True,
     )
     new = [n.reshape(weight.shape) for n in new]

time: 113 us -> 102 us (0.903); the launches traced: 110 us -> 101 us
  waiting for transfers between devices: 37.4 us -> 27.3 us
  starting transfers between devices: 41.6 us -> 50.5 us
  Pallas kernels: 25 us -> 18.9 us
  local copies, waits for them, and re-layouts: 5.76 us -> 3.4 us
    ppermute x29 -> x31, starting transfers between devices: 37.5 us -> 50.5 us  [shifted(): return lax.ppermute(value, AXES, pairs)]
    ppermute x29 -> x31, waiting for transfers between devices: 37.4 us -> 27.3 us  [shifted(): return lax.ppermute(value, AXES, pairs)]
    pallas_call x21 -> x17, Pallas kernels: 25 us -> 18.9 us  [run(): return kernel(body, outs, len(operands), **more)(*operands)]
    all_to_all x1 -> x0, starting transfers between devices: 4.07 us -> none  [step(): arrived = lax.all_to_all(partial, 'head', 0, 0, tiled=True)]
    unnamed x16 -> x10, local copies, waits for them, and re-layouts: 5.76 us -> 3.4 us
  transfers between devices with their start and end apart: 30 -> 31, of which waited for: 10 -> 9; matrix products, arithmetic and copies ran while one was open for 0% -> 0% of each run, Pallas kernels for 18% -> 13%
where the time goes in v3:
time: 102 us; the launch traced here: 101 us
  starting transfers between devices  50.5 us (50%)
  waiting for transfers between devices  27.3 us (27%)
  Pallas kernels  18.9 us (19%)
  local copies, waits for them, and re-layouts  3.4 us (3%)
    ppermute x31, starting transfers between devices, shifted(): return lax.ppermute(value, AXES, pairs)  50.5 us
    ppermute x31, waiting for transfers between devices, shifted(): return lax.ppermute(value, AXES, pairs)  27.3 us
    pallas_call x17, Pallas kernels, run(): return kernel(body, outs, len(operands), **more)(*operands)  18.9 us
    unnamed x10, local copies, waits for them, and re-layouts  3.4 us
  transfers between devices with their start and end apart: 31, of which 9 were waited for; matrix products, arithmetic and copies ran while one was open for 0% of the time, Pallas kernels for 13%

profile of v3, /device:TPU:1, one launch (start us, length us, event | category | flops | bytes accessed | tf_op | source)
XLA Modules:
  0.0 101.0 jit_solution(5940483775822082322)
XLA Ops:
  0.6 1.6 %shard_map.94 = (bf16[512,256]{1,0:T(8,128)(2,1)S(1)}, bf16[512,128]{1,0:T(8,128)(2,1)S(1)}) custom-call(bf16[512,512]{1,0:T(8,128)(2,1)} %constant.2.clone.h_hbm.h_ref, bf16[128,512]{1,0:T(8,128)(2,1)} %l_hbm.1, f32[1024,128]{1,0:T(8,128)} %bitcast.9), custom_call_target="tpu_custom_call" | custom-call | tf_op jit(solution)/shard_map/pallas_call | solution.py:224
  2.2 2.5 %collective-permute-start.18 = (bf16[512,128]{1,0:T(8,128)(2,1)S(1)}, bf16[512,128]{1,0:T(8,128)(2,1)S(1)}, u32[]{:S(2)}, u32[]{:S(2)}) collective-permute-start(bf16[512,128]{1,0:T(8,128)(2,1)S(1)} %get-tuple-element.28.refs_0_), channel_id=1, source_target_pairs={{0,4},{1,5},{2,6},{3,7},{4,0},{5,1},{6,2},{7,3},{8,12},{9,13},{10,... | collective-permute-start | bytes 393224 | tf_op jit(solution)/shard_map/ppermute | solution.py:41
  4.7 1.3 %collective-permute-start.15 = (bf16[512,128]{1,0:T(8,128)(2,1)S(1)}, bf16[512,128]{1,0:T(8,128)(2,1)S(1)}, u32[]{:S(2)}, u32[]{:S(2)}) collective-permute-start(bf16[512,128]{1,0:T(8,128)(2,1)S(1)} %get-tuple-element.28.refs_0_), channel_id=1, source_target_pairs={{0,1},{1,2},{2,3},{3,0},{4,5},{5,6},{6,7},{7,4},{8,9},{9,10},{10,1... | collective-permute-start | bytes 393224 | tf_op jit(solution)/shard_map/ppermute | solution.py:41
  6.0 1.9 %collective-permute-done.18.refs_4_ = bf16[512,128]{1,0:T(8,128)(2,1)S(1)} collective-permute-done((bf16[512,128]{1,0:T(8,128)(2,1)S(1)}, bf16[512,128]{1,0:T(8,128)(2,1)S(1)}, u32[]{:S(2)}, u32[]{:S(2)}) %collective-permute-start.18) | collective-permute-done | bytes 131104 | tf_op jit(solution)/shard_map/ppermute | solution.py:41
  7.9 2.6 %collective-permute-start.20 = (bf16[512,128]{1,0:T(8,128)(2,1)S(1)}, bf16[512,128]{1,0:T(8,128)(2,1)S(1)}, u32[]{:S(2)}, u32[]{:S(2)}) collective-permute-start(bf16[512,128]{1,0:T(8,128)(2,1)S(1)} %collective-permute-done.18.refs_4_), channel_id=1, source_target_pairs={{0,3},{1,0},{2,1},{3,2},{4,7},{5,4},{6,5},{7,6},{8,11},{9,8},{10,9... | collective-permute-start | bytes 393224 | tf_op jit(solution)/shard_map/ppermute | solution.py:41
  10.6 0.5 collective-permute-start.16
  11.0 1.0 collective-permute-start.19
  12.0 0.0 collective-permute-start.17
  12.0 0.5 collective-permute-done.20.refs_6_
  12.5 3.1 %collective-permute-start.21 = (bf16[512,128]{1,0:T(8,128)(2,1)S(1)}, bf16[512,128]{1,0:T(8,128)(2,1)S(1)}, u32[]{:S(2)}, u32[]{:S(2)}) collective-permute-start(bf16[512,128]{1,0:T(8,128)(2,1)S(1)} %collective-permute-done.20.refs_6_), channel_id=1, source_target_pairs={{0,3},{1,0},{2,1},{3,2},{4,7},{5,4},{6,5},{7,6},{8,11},{9,8},{10,9... | collective-permute-start | bytes 393224 | tf_op jit(solution)/shard_map/ppermute | solution.py:41
  15.6 3.4 %copy-done = bf16[1024,16,1,256]{3,1,2,0:T(8,128)(2,1)S(1)} copy-done((bf16[1024,16,1,256]{3,1,2,0:T(8,128)(2,1)S(1)}, bf16[1024,16,1,256]{3,1,2,0:T(8,128)(2,1)}, u32[]{:S(2)}) %copy-start) | copy-done | bytes 8388632
  19.0 2.1 %shard_map.93.g_ref = bf16[16,1024,256]{2,1,0:T(8,128)(2,1)S(1)} custom-call(bf16[1024,16,256]{2,1,0:T(8,128)(2,1)S(1)} %bitcast.8), custom_call_target="tpu_custom_call" | custom-call | tf_op jit(solution)/shard_map/pallas_call | solution.py:224
  21.1 0.0 collective-permute-done.16.refs_2_
  21.1 0.0 collective-permute-done.19.refs_5_
  21.1 0.0 collective-permute-done.21.refs_7_
  21.1 0.3 shard_map.101.l_ref
  21.4 2.0 %shard_map.102 = bf16[5,512,256]{2,1,0:T(8,128)(2,1)S(1)} custom-call(bf16[16,1024,256]{2,1,0:T(8,128)(2,1)S(1)} %shard_map.93.g_ref, bf16[512,1024]{1,0:T(8,128)(2,1)S(1)} %shard_map.101.l_ref), custom_call_target="tpu_custom_call" | custom-call | tf_op jit(solution)/shard_map/pallas_call | solution.py:224
  23.4 3.9 %collective-permute-start.22 = (bf16[5,512,256]{2,1,0:T(8,128)(2,1)S(1)}, bf16[5,512,256]{2,1,0:T(8,128)(2,1)S(1)}, u32[]{:S(2)}, u32[]{:S(2)}) collective-permute-start(bf16[5,512,256]{2,1,0:T(8,128)(2,1)S(1)} %shard_map.102), channel_id=1, source_target_pairs={{0,8},{1,9},{2,10},{3,11},{4,12},{5,13},{6,14},{7,15},{8,0},{9,1},... | collective-permute-start | bytes 3932168 | tf_op jit(solution)/shard_map/ppermute | solution.py:41
  27.2 0.1 collective-permute-start
  27.3 3.2 %collective-permute-start.5 = (bf16[512,256]{1,0:T(8,128)(2,1)S(1)}, bf16[512,256]{1,0:T(8,128)(2,1)S(1)}, u32[]{:S(2)}, u32[]{:S(2)}) collective-permute-start(bf16[512,256]{1,0:T(8,128)(2,1)S(1)} %get-tuple-element.21.a_ref), channel_id=1, source_target_pairs={{0,16},{1,17},{2,18},{3,19},{4,20},{5,21},{6,22},{7,23},{8,24},{9,... | collective-permute-start | bytes 786440 | tf_op jit(solution)/shard_map/ppermute | solution.py:41
  30.6 1.2 %shard_map.105 = bf16[3,512,256]{2,1,0:T(8,128)(2,1)S(1)} custom-call(bf16[16,1024,256]{2,1,0:T(8,128)(2,1)S(1)} %shard_map.93.g_ref, bf16[512,1024]{1,0:T(8,128)(2,1)S(1)} %shard_map.101.l_ref), custom_call_target="tpu_custom_call" | custom-call | tf_op jit(solution)/shard_map/pallas_call | solution.py:224
  31.8 0.8 collective-permute-start.25
  32.6 0.0 collective-permute-done.b_ref
  32.6 2.5 %collective-permute-start.1 = (bf16[2,512,256]{2,1,0:T(8,128)(2,1)S(1)}, bf16[2,512,256]{2,1,0:T(8,128)(2,1)S(1)}, u32[]{:S(2)}, u32[]{:S(2)}) collective-permute-start(bf16[2,512,256]{2,1,0:T(8,128)(2,1)S(1)} %shard_map.95.p0), channel_id=1, source_target_pairs={{0,32},{1,33},{2,34},{3,35},{4,36},{5,37},{6,38},{7,39},{8,104},{9... | collective-permute-start | bytes 1572872 | tf_op jit(solution)/shard_map/ppermute | solution.py:41
  35.2 1.7 %collective-permute-done.5.a_ref.z = bf16[512,256]{1,0:T(8,128)(2,1)S(1)} collective-permute-done((bf16[512,256]{1,0:T(8,128)(2,1)S(1)}, bf16[512,256]{1,0:T(8,128)(2,1)S(1)}, u32[]{:S(2)}, u32[]{:S(2)}) %collective-permute-start.5) | collective-permute-done | bytes 262176 | tf_op jit(solution)/shard_map/ppermute | solution.py:41
  36.8 1.0 collective-permute-start.6
  37.8 1.2 %collective-permute-done.6.b_ref.zs = bf16[512,256]{1,0:T(8,128)(2,1)S(1)} collective-permute-done((bf16[512,256]{1,0:T(8,128)(2,1)S(1)}, bf16[512,256]{1,0:T(8,128)(2,1)S(1)}, u32[]{:S(2)}, u32[]{:S(2)}) %collective-permute-start.6) | collective-permute-done | bytes 262176 | tf_op jit(solution)/shard_map/ppermute | solution.py:41
  39.0 2.5 %collective-permute-start.7 = (bf16[2,512,256]{2,1,0:T(8,128)(2,1)S(1)}, bf16[2,512,256]{2,1,0:T(8,128)(2,1)S(1)}, u32[]{:S(2)}, u32[]{:S(2)}) collective-permute-start(bf16[2,512,256]{2,1,0:T(8,128)(2,1)S(1)} %shard_map.97), channel_id=1, source_target_pairs={{0,32},{1,33},{2,34},{3,35},{4,36},{5,37},{6,38},{7,39},{8,104},{9... | collective-permute-start | bytes 1572872 | tf_op jit(solution)/shard_map/ppermute | solution.py:41
  41.6 0.0 collective-permute-done.1.pair_ref.x
  41.6 1.5 %collective-permute-start.2 = (bf16[2,512,256]{2,1,0:T(8,128)(2,1)S(1)}, bf16[2,512,256]{2,1,0:T(8,128)(2,1)S(1)}, u32[]{:S(2)}, u32[]{:S(2)}) collective-permute-start(bf16[2,512,256]{2,1,0:T(8,128)(2,1)S(1)} %collective-permute-done.1.pair_ref.x), channel_id=1, source_target_pairs={{0,8},{1,9},{2,10},{3,11},{4,12},{5,13},{6,14},{7,15},{8,0},{9,1},... | collective-permute-start | bytes 1572872 | tf_op jit(solution)/shard_map/ppermute | solution.py:41
  43.1 0.0 collective-permute-done.25.r_ref
  43.1 1.6 %shard_map.106 = (bf16[2,512,256]{2,1,0:T(8,128)(2,1)S(1)}, bf16[512,256]{1,0:T(8,128)(2,1)S(1)}) custom-call(bf16[16,1024,256]{2,1,0:T(8,128)(2,1)S(1)} %shard_map.93.g_ref, bf16[512,1024]{1,0:T(8,128)(2,1)S(1)} %shard_map.101.l_ref, bf16[3,512,256]{2,1,0:T(8,128)(2,1)S(1)} %collective-permute-done.25.r_ref), custom_call_target="tpu_custom_call" | custom-call | tf_op jit(solution)/shard_map/pallas_call | solution.py:224
  44.7 1.4 %collective-permute-start.26 = (bf16[2,512,256]{2,1,0:T(8,128)(2,1)S(1)}, bf16[2,512,256]{2,1,0:T(8,128)(2,1)S(1)}, u32[]{:S(2)}, u32[]{:S(2)}) collective-permute-start(bf16[2,512,256]{2,1,0:T(8,128)(2,1)S(1)} %get-tuple-element.32), channel_id=1, source_target_pairs={{0,32},{1,33},{2,34},{3,35},{4,36},{5,37},{6,38},{7,39},{8,104},{9... | collective-permute-start | bytes 1572872 | tf_op jit(solution)/shard_map/ppermute | solution.py:41
  46.1 0.5 collective-permute-start.3
  46.6 1.1 %collective-permute-done.7.zx = bf16[2,512,256]{2,1,0:T(8,128)(2,1)S(1)} collective-permute-done((bf16[2,512,256]{2,1,0:T(8,128)(2,1)S(1)}, bf16[2,512,256]{2,1,0:T(8,128)(2,1)S(1)}, u32[]{:S(2)}, u32[]{:S(2)}) %collective-permute-start.7) | collective-permute-done | bytes 524320 | tf_op jit(solution)/shard_map/ppermute | solution.py:41
  47.7 2.2 %collective-permute-start.8 = (bf16[2,512,256]{2,1,0:T(8,128)(2,1)S(1)}, bf16[2,512,256]{2,1,0:T(8,128)(2,1)S(1)}, u32[]{:S(2)}, u32[]{:S(2)}) collective-permute-start(bf16[2,512,256]{2,1,0:T(8,128)(2,1)S(1)} %collective-permute-done.7.zx), channel_id=1, source_target_pairs={{0,8},{1,9},{2,10},{3,11},{4,12},{5,13},{6,14},{7,15},{8,0},{9,1},... | collective-permute-start | bytes 1572872 | tf_op jit(solution)/shard_map/ppermute | solution.py:41
  49.9 0.0 collective-permute-done.22.r_ref
  49.9 2.5 %shard_map.103 = (bf16[2,512,256]{2,1,0:T(8,128)(2,1)S(1)}, bf16[512,256]{1,0:T(8,128)(2,1)S(1)}, bf16[512,256]{1,0:T(8,128)(2,1)S(1)}, bf16[512,256]{1,0:T(8,128)(2,1)S(1)}) custom-call(bf16[16,1024,256]{2,1,0:T(8,128)(2,1)S(1)} %shard_map.93.g_ref, bf16[512,1024]{1,0:T(8,128)(2,1)S(1)} %shard_map.101.l_ref, ...), custom_call_target="tpu_custom_call" | custom-call | tf_op jit(solution)/shard_map/pallas_call | solution.py:224
  52.4 1.3 %collective-permute-start.23 = (bf16[2,512,256]{2,1,0:T(8,128)(2,1)S(1)}, bf16[2,512,256]{2,1,0:T(8,128)(2,1)S(1)}, u32[]{:S(2)}, u32[]{:S(2)}) collective-permute-start(bf16[2,512,256]{2,1,0:T(8,128)(2,1)S(1)} %get-tuple-element.30), channel_id=1, source_target_pairs={{0,32},{1,33},{2,34},{3,35},{4,36},{5,37},{6,38},{7,39},{8,104},{9... | collective-permute-start | bytes 1572872 | tf_op jit(solution)/shard_map/ppermute | solution.py:41
  53.7 2.4 %collective-permute-done.3.f = bf16[512,256]{1,0:T(8,128)(2,1)S(1)} collective-permute-done((bf16[512,256]{1,0:T(8,128)(2,1)S(1)}, bf16[512,256]{1,0:T(8,128)(2,1)S(1)}, u32[]{:S(2)}, u32[]{:S(2)}) %collective-permute-start.3) | collective-permute-done | bytes 262176 | tf_op jit(solution)/shard_map/ppermute | solution.py:41
  56.1 3.0 %collective-permute-start.9 = (bf16[512,256]{1,0:T(8,128)(2,1)S(1)}, bf16[512,256]{1,0:T(8,128)(2,1)S(1)}, u32[]{:S(2)}, u32[]{:S(2)}) collective-permute-start(bf16[512,256]{1,0:T(8,128)(2,1)S(1)} %collective-permute-done.3.f), channel_id=1, source_target_pairs={{0,16},{1,17},{2,18},{3,19},{4,20},{5,21},{6,22},{7,23},{8,24},{9,... | collective-permute-start | bytes 786440 | tf_op jit(solution)/shard_map/ppermute | solution.py:41
  59.1 0.0 collective-permute-done.2.xs
  59.1 2.4 %collective-permute-start.4 = (bf16[512,256]{1,0:T(8,128)(2,1)S(1)}, bf16[512,256]{1,0:T(8,128)(2,1)S(1)}, u32[]{:S(2)}, u32[]{:S(2)}) collective-permute-start(bf16[512,256]{1,0:T(8,128)(2,1)S(1)} %collective-permute-done.3.f), channel_id=1, source_target_pairs={{0,8},{1,9},{2,10},{3,11},{4,12},{5,13},{6,14},{7,15},{8,0},{9,1},... | collective-permute-start | bytes 786440 | tf_op jit(solution)/shard_map/ppermute | solution.py:41
  61.6 0.0 collective-permute-done.26.pair
  61.6 0.1 collective-permute-start.27
  61.6 1.7 %collective-permute-done.9.zf = bf16[512,256]{1,0:T(8,128)(2,1)S(1)} collective-permute-done((bf16[512,256]{1,0:T(8,128)(2,1)S(1)}, bf16[512,256]{1,0:T(8,128)(2,1)S(1)}, u32[]{:S(2)}, u32[]{:S(2)}) %collective-permute-start.9) | collective-permute-done | bytes 262176 | tf_op jit(solution)/shard_map/ppermute | solution.py:41
  63.4 3.0 %collective-permute-start.10 = (bf16[512,256]{1,0:T(8,128)(2,1)S(1)}, bf16[512,256]{1,0:T(8,128)(2,1)S(1)}, u32[]{:S(2)}, u32[]{:S(2)}) collective-permute-start(bf16[512,256]{1,0:T(8,128)(2,1)S(1)} %collective-permute-done.9.zf), channel_id=1, source_target_pairs={{0,8},{1,9},{2,10},{3,11},{4,12},{5,13},{6,14},{7,15},{8,0},{9,1},... | collective-permute-start | bytes 786440 | tf_op jit(solution)/shard_map/ppermute | solution.py:41
  66.4 0.0 copy-start.4
  66.4 3.0 %collective-permute-start.29 = (bf16[512,256]{1,0:T(8,128)(2,1)S(1)}, bf16[512,256]{1,0:T(8,128)(2,1)S(1)}, u32[]{:S(2)}, u32[]{:S(2)}) collective-permute-start(bf16[512,256]{1,0:T(8,128)(2,1)S(1)} %get-tuple-element.34), channel_id=1, source_target_pairs={{0,16},{1,17},{2,18},{3,19},{4,20},{5,21},{6,22},{7,23},{8,24},{9,... | collective-permute-start | bytes 786440 | tf_op jit(solution)/shard_map/ppermute | solution.py:41
  69.5 0.3 collective-permute-start.24
  69.8 4.6 %shard_map.98 = (bf16[2,128,512]{2,1,0:T(8,128)(2,1)S(1)}, bf16[2,128,512]{2,1,0:T(8,128)(2,1)S(1)}, bf16[2,128,512]{2,1,0:T(8,128)(2,1)S(1)}, bf16[2,128,512]{2,1,0:T(8,128)(2,1)S(1)}) custom-call(bf16[16,1024,256]{2,1,0:T(8,128)(2,1)S(1)} %shard_map.93.g_ref, bf16[2,512,256]{2,1,0:T(8,128)(2,1)S(1)} %shard_map.95.p0, ...), custom_call_target="tpu_custom_call" | custom-call | tf_op jit(solution)/shard_map/pallas_call | solution.py:224
  74.4 0.1 collective-permute-start.11
  74.4 2.7 %collective-permute-start.12 = (bf16[2,128,512]{2,1,0:T(8,128)(2,1)S(1)}, bf16[2,128,512]{2,1,0:T(8,128)(2,1)S(1)}, u32[]{:S(2)}, u32[]{:S(2)}) collective-permute-start(bf16[2,128,512]{2,1,0:T(8,128)(2,1)S(1)} %get-tuple-element.24), channel_id=1, source_target_pairs={{0,3},{1,0},{2,1},{3,2},{4,7},{5,4},{6,5},{7,6},{8,11},{9,8},{10,9... | collective-permute-start | bytes 786440 | tf_op jit(solution)/shard_map/ppermute | solution.py:41
  77.1 0.1 shard_map.108
  77.2 2.6 %collective-permute-start.30 = (bf16[512,256]{1,0:T(8,128)(2,1)S(1)}, bf16[512,256]{1,0:T(8,128)(2,1)S(1)}, u32[]{:S(2)}, u32[]{:S(2)}) collective-permute-start(bf16[512,256]{1,0:T(8,128)(2,1)S(1)} %shard_map.108), channel_id=1, source_target_pairs={{0,64},{1,65},{2,66},{3,67},{4,68},{5,69},{6,70},{7,71},{8,72},{9,... | collective-permute-start | bytes 786440 | tf_op jit(solution)/shard_map/ppermute | solution.py:41
  79.7 0.1 shard_map.107
  79.9 9.1 %collective-permute-done.11.up = bf16[2,128,512]{2,1,0:T(8,128)(2,1)S(1)} collective-permute-done((bf16[2,128,512]{2,1,0:T(8,128)(2,1)S(1)}, bf16[2,128,512]{2,1,0:T(8,128)(2,1)S(1)}, u32[]{:S(2)}, u32[]{:S(2)}) %collective-permute-start.11) | collective-permute-done | bytes 262176 | tf_op jit(solution)/shard_map/ppermute | solution.py:41
  88.9 0.6 collective-permute-start.28
  89.5 0.1 shard_map.99
  89.6 0.8 collective-permute-start.14
  90.4 7.8 %collective-permute-done.14.cross = bf16[128,512]{1,0:T(8,128)(2,1)S(1)} collective-permute-done((bf16[128,512]{1,0:T(8,128)(2,1)S(1)}, bf16[128,512]{1,0:T(8,128)(2,1)S(1)}, u32[]{:S(2)}, u32[]{:S(2)}) %collective-permute-start.14) | collective-permute-done | bytes 131104 | tf_op jit(solution)/shard_map/ppermute | solution.py:41
  98.2 0.7 shard_map.100
  98.9 0.1 shard_map.104.base
  99.1 2.0 %shard_map.109 = (f32[1024,128]{1,0:T(8,128)}, f32[1024,128]{1,0:T(8,128)}, f32[1024,128]{1,0:T(8,128)}) custom-call(bf16[512,512]{1,0:T(8,128)(2,1)S(1)} %copy-done.2, f32[512,256]{1,0:T(8,128)S(1)} %shard_map.104.base, bf16[512,256]{1,0:T(8,128)(2,1)S(1)} %collective-permute-done.28.over, bf16[512,256]{1,0:T(8,128)(2,1)S(1)} %collective-permute-done.30.far, ...), custom_call_target="tpu_custom_call" | custom-call | tf_op jit(solution)/shard_map/pallas_call | solution.py:224
  (25 shorter events, 0.1 us)
Async XLA Ops:
  2.2 5.7 %collective-permute-start.18 = (bf16[512,128]{1,0:T(8,128)(2,1)S(1)}, bf16[512,128]{1,0:T(8,128)(2,1)S(1)}, u32[]{:S(2)}, u32[]{:S(2)}) collective-permute-start(bf16[512,128]{1,0:T(8,128)(2,1)S(1)} %get-tuple-element.28.refs_0_), channel_id=1, source_target_pairs={{0,4},{1,5},{2,6},{3,7},{4,0},{5,1},{6,2},{7,3},{8,12},{9,13},{10,... | collective-permute-start | bytes 393224 | tf_op jit(solution)/shard_map/ppermute | solution.py:41
  4.7 7.3 %collective-permute-start.15 = (bf16[512,128]{1,0:T(8,128)(2,1)S(1)}, bf16[512,128]{1,0:T(8,128)(2,1)S(1)}, u32[]{:S(2)}, u32[]{:S(2)}) collective-permute-start(bf16[512,128]{1,0:T(8,128)(2,1)S(1)} %get-tuple-element.28.refs_0_), channel_id=1, source_target_pairs={{0,1},{1,2},{2,3},{3,0},{4,5},{5,6},{6,7},{7,4},{8,9},{9,10},{10,1... | collective-permute-start | bytes 393224 | tf_op jit(solution)/shard_map/ppermute | solution.py:41
  7.9 4.6 %collective-permute-start.20 = (bf16[512,128]{1,0:T(8,128)(2,1)S(1)}, bf16[512,128]{1,0:T(8,128)(2,1)S(1)}, u32[]{:S(2)}, u32[]{:S(2)}) collective-permute-start(bf16[512,128]{1,0:T(8,128)(2,1)S(1)} %collective-permute-done.18.refs_4_), channel_id=1, source_target_pairs={{0,3},{1,0},{2,1},{3,2},{4,7},{5,4},{6,5},{7,6},{8,11},{9,8},{10,9... | collective-permute-start | bytes 393224 | tf_op jit(solution)/shard_map/ppermute | solution.py:41
  10.6 10.5 %collective-permute-start.16 = (bf16[512,128]{1,0:T(8,128)(2,1)S(1)}, bf16[512,128]{1,0:T(8,128)(2,1)S(1)}, u32[]{:S(2)}, u32[]{:S(2)}) collective-permute-start(bf16[512,128]{1,0:T(8,128)(2,1)S(1)} %get-tuple-element.28.refs_0_), channel_id=1, source_target_pairs={{0,3},{1,0},{2,1},{3,2},{4,7},{5,4},{6,5},{7,6},{8,11},{9,8},{10,9... | collective-permute-start | bytes 393224 | tf_op jit(solution)/shard_map/ppermute | solution.py:41
  11.0 10.1 %collective-permute-start.19 = (bf16[512,128]{1,0:T(8,128)(2,1)S(1)}, bf16[512,128]{1,0:T(8,128)(2,1)S(1)}, u32[]{:S(2)}, u32[]{:S(2)}) collective-permute-start(bf16[512,128]{1,0:T(8,128)(2,1)S(1)} %collective-permute-done.18.refs_4_), channel_id=1, source_target_pairs={{0,1},{1,2},{2,3},{3,0},{4,5},{5,6},{6,7},{7,4},{8,9},{9,10},{10,1... | collective-permute-start | bytes 393224 | tf_op jit(solution)/shard_map/ppermute | solution.py:41
  12.0 9.1 %collective-permute-start.17 = (bf16[512,128]{1,0:T(8,128)(2,1)S(1)}, bf16[512,128]{1,0:T(8,128)(2,1)S(1)}, u32[]{:S(2)}, u32[]{:S(2)}) collective-permute-start(bf16[512,128]{1,0:T(8,128)(2,1)S(1)} %collective-permute-done.15.refs_1_), channel_id=1, source_target_pairs={{0,1},{1,2},{2,3},{3,0},{4,5},{5,6},{6,7},{7,4},{8,9},{9,10},{10,1... | collective-permute-start | bytes 393224 | tf_op jit(solution)/shard_map/ppermute | solution.py:41
  12.5 8.6 %collective-permute-start.21 = (bf16[512,128]{1,0:T(8,128)(2,1)S(1)}, bf16[512,128]{1,0:T(8,128)(2,1)S(1)}, u32[]{:S(2)}, u32[]{:S(2)}) collective-permute-start(bf16[512,128]{1,0:T(8,128)(2,1)S(1)} %collective-permute-done.20.refs_6_), channel_id=1, source_target_pairs={{0,3},{1,0},{2,1},{3,2},{4,7},{5,4},{6,5},{7,6},{8,11},{9,8},{10,9... | collective-permute-start | bytes 393224 | tf_op jit(solution)/shard_map/ppermute | solution.py:41
  15.6 3.4 %copy-start = (bf16[1024,16,1,256]{3,1,2,0:T(8,128)(2,1)S(1)}, bf16[1024,16,1,256]{3,1,2,0:T(8,128)(2,1)}, u32[]{:S(2)}) copy-start(bf16[1024,16,1,256]{3,1,2,0:T(8,128)(2,1)} %param.7) | copy-start | bytes 25165828
  23.4 26.5 %collective-permute-start.22 = (bf16[5,512,256]{2,1,0:T(8,128)(2,1)S(1)}, bf16[5,512,256]{2,1,0:T(8,128)(2,1)S(1)}, u32[]{:S(2)}, u32[]{:S(2)}) collective-permute-start(bf16[5,512,256]{2,1,0:T(8,128)(2,1)S(1)} %shard_map.102), channel_id=1, source_target_pairs={{0,8},{1,9},{2,10},{3,11},{4,12},{5,13},{6,14},{7,15},{8,0},{9,1},... | collective-permute-start | bytes 3932168 | tf_op jit(solution)/shard_map/ppermute | solution.py:41
  27.2 5.3 %collective-permute-start = (bf16[512,256]{1,0:T(8,128)(2,1)S(1)}, bf16[512,256]{1,0:T(8,128)(2,1)S(1)}, u32[]{:S(2)}, u32[]{:S(2)}) collective-permute-start(bf16[512,256]{1,0:T(8,128)(2,1)S(1)} %get-tuple-element.21.a_ref), channel_id=1, source_target_pairs={{0,8},{1,9},{2,10},{3,11},{4,12},{5,13},{6,14},{7,15},{8,0},{9,1},... | collective-permute-start | bytes 786440 | tf_op jit(solution)/shard_map/ppermute | solution.py:41
  27.3 9.5 %collective-permute-start.5 = (bf16[512,256]{1,0:T(8,128)(2,1)S(1)}, bf16[512,256]{1,0:T(8,128)(2,1)S(1)}, u32[]{:S(2)}, u32[]{:S(2)}) collective-permute-start(bf16[512,256]{1,0:T(8,128)(2,1)S(1)} %get-tuple-element.21.a_ref), channel_id=1, source_target_pairs={{0,16},{1,17},{2,18},{3,19},{4,20},{5,21},{6,22},{7,23},{8,24},{9,... | collective-permute-start | bytes 786440 | tf_op jit(solution)/shard_map/ppermute | solution.py:41
  31.8 11.3 %collective-permute-start.25 = (bf16[3,512,256]{2,1,0:T(8,128)(2,1)S(1)}, bf16[3,512,256]{2,1,0:T(8,128)(2,1)S(1)}, u32[]{:S(2)}, u32[]{:S(2)}) collective-permute-start(bf16[3,512,256]{2,1,0:T(8,128)(2,1)S(1)} %shard_map.105), channel_id=1, source_target_pairs={{0,8},{1,9},{2,10},{3,11},{4,12},{5,13},{6,14},{7,15},{8,0},{9,1},... | collective-permute-start | bytes 2359304 | tf_op jit(solution)/shard_map/ppermute | solution.py:41
  32.6 9.0 %collective-permute-start.1 = (bf16[2,512,256]{2,1,0:T(8,128)(2,1)S(1)}, bf16[2,512,256]{2,1,0:T(8,128)(2,1)S(1)}, u32[]{:S(2)}, u32[]{:S(2)}) collective-permute-start(bf16[2,512,256]{2,1,0:T(8,128)(2,1)S(1)} %shard_map.95.p0), channel_id=1, source_target_pairs={{0,32},{1,33},{2,34},{3,35},{4,36},{5,37},{6,38},{7,39},{8,104},{9... | collective-permute-start | bytes 1572872 | tf_op jit(solution)/shard_map/ppermute | solution.py:41
  36.8 2.2 %collective-permute-start.6 = (bf16[512,256]{1,0:T(8,128)(2,1)S(1)}, bf16[512,256]{1,0:T(8,128)(2,1)S(1)}, u32[]{:S(2)}, u32[]{:S(2)}) collective-permute-start(bf16[512,256]{1,0:T(8,128)(2,1)S(1)} %collective-permute-done.5.a_ref.z), channel_id=1, source_target_pairs={{0,8},{1,9},{2,10},{3,11},{4,12},{5,13},{6,14},{7,15},{8,0},{9,1},... | collective-permute-start | bytes 786440 | tf_op jit(solution)/shard_map/ppermute | solution.py:41
  39.0 8.7 %collective-permute-start.7 = (bf16[2,512,256]{2,1,0:T(8,128)(2,1)S(1)}, bf16[2,512,256]{2,1,0:T(8,128)(2,1)S(1)}, u32[]{:S(2)}, u32[]{:S(2)}) collective-permute-start(bf16[2,512,256]{2,1,0:T(8,128)(2,1)S(1)} %shard_map.97), channel_id=1, source_target_pairs={{0,32},{1,33},{2,34},{3,35},{4,36},{5,37},{6,38},{7,39},{8,104},{9... | collective-permute-start | bytes 1572872 | tf_op jit(solution)/shard_map/ppermute | solution.py:41
  41.6 17.5 %collective-permute-start.2 = (bf16[2,512,256]{2,1,0:T(8,128)(2,1)S(1)}, bf16[2,512,256]{2,1,0:T(8,128)(2,1)S(1)}, u32[]{:S(2)}, u32[]{:S(2)}) collective-permute-start(bf16[2,512,256]{2,1,0:T(8,128)(2,1)S(1)} %collective-permute-done.1.pair_ref.x), channel_id=1, source_target_pairs={{0,8},{1,9},{2,10},{3,11},{4,12},{5,13},{6,14},{7,15},{8,0},{9,1},... | collective-permute-start | bytes 1572872 | tf_op jit(solution)/shard_map/ppermute | solution.py:41
  44.7 16.9 %collective-permute-start.26 = (bf16[2,512,256]{2,1,0:T(8,128)(2,1)S(1)}, bf16[2,512,256]{2,1,0:T(8,128)(2,1)S(1)}, u32[]{:S(2)}, u32[]{:S(2)}) collective-permute-start(bf16[2,512,256]{2,1,0:T(8,128)(2,1)S(1)} %get-tuple-element.32), channel_id=1, source_target_pairs={{0,32},{1,33},{2,34},{3,35},{4,36},{5,37},{6,38},{7,39},{8,104},{9... | collective-permute-start | bytes 1572872 | tf_op jit(solution)/shard_map/ppermute | solution.py:41
  46.1 10.1 %collective-permute-start.3 = (bf16[512,256]{1,0:T(8,128)(2,1)S(1)}, bf16[512,256]{1,0:T(8,128)(2,1)S(1)}, u32[]{:S(2)}, u32[]{:S(2)}) collective-permute-start(bf16[512,256]{1,0:T(8,128)(2,1)S(1)} %shard_map.96), channel_id=1, source_target_pairs={{0,32},{1,33},{2,34},{3,35},{4,36},{5,37},{6,38},{7,39},{8,104},{9... | collective-permute-start | bytes 786440 | tf_op jit(solution)/shard_map/ppermute | solution.py:41
  47.7 22.0 %collective-permute-start.8 = (bf16[2,512,256]{2,1,0:T(8,128)(2,1)S(1)}, bf16[2,512,256]{2,1,0:T(8,128)(2,1)S(1)}, u32[]{:S(2)}, u32[]{:S(2)}) collective-permute-start(bf16[2,512,256]{2,1,0:T(8,128)(2,1)S(1)} %collective-permute-done.7.zx), channel_id=1, source_target_pairs={{0,8},{1,9},{2,10},{3,11},{4,12},{5,13},{6,14},{7,15},{8,0},{9,1},... | collective-permute-start | bytes 1572872 | tf_op jit(solution)/shard_map/ppermute | solution.py:41
  52.4 17.1 %collective-permute-start.23 = (bf16[2,512,256]{2,1,0:T(8,128)(2,1)S(1)}, bf16[2,512,256]{2,1,0:T(8,128)(2,1)S(1)}, u32[]{:S(2)}, u32[]{:S(2)}) collective-permute-start(bf16[2,512,256]{2,1,0:T(8,128)(2,1)S(1)} %get-tuple-element.30), channel_id=1, source_target_pairs={{0,32},{1,33},{2,34},{3,35},{4,36},{5,37},{6,38},{7,39},{8,104},{9... | collective-permute-start | bytes 1572872 | tf_op jit(solution)/shard_map/ppermute | solution.py:41
  56.1 7.2 %collective-permute-start.9 = (bf16[512,256]{1,0:T(8,128)(2,1)S(1)}, bf16[512,256]{1,0:T(8,128)(2,1)S(1)}, u32[]{:S(2)}, u32[]{:S(2)}) collective-permute-start(bf16[512,256]{1,0:T(8,128)(2,1)S(1)} %collective-permute-done.3.f), channel_id=1, source_target_pairs={{0,16},{1,17},{2,18},{3,19},{4,20},{5,21},{6,22},{7,23},{8,24},{9,... | collective-permute-start | bytes 786440 | tf_op jit(solution)/shard_map/ppermute | solution.py:41
  59.1 7.3 %collective-permute-start.4 = (bf16[512,256]{1,0:T(8,128)(2,1)S(1)}, bf16[512,256]{1,0:T(8,128)(2,1)S(1)}, u32[]{:S(2)}, u32[]{:S(2)}) collective-permute-start(bf16[512,256]{1,0:T(8,128)(2,1)S(1)} %collective-permute-done.3.f), channel_id=1, source_target_pairs={{0,8},{1,9},{2,10},{3,11},{4,12},{5,13},{6,14},{7,15},{8,0},{9,1},... | collective-permute-start | bytes 786440 | tf_op jit(solution)/shard_map/ppermute | solution.py:41
  61.6 15.6 %collective-permute-start.27 = (bf16[2,512,256]{2,1,0:T(8,128)(2,1)S(1)}, bf16[2,512,256]{2,1,0:T(8,128)(2,1)S(1)}, u32[]{:S(2)}, u32[]{:S(2)}) collective-permute-start(bf16[2,512,256]{2,1,0:T(8,128)(2,1)S(1)} %collective-permute-done.26.pair), channel_id=1, source_target_pairs={{0,8},{1,9},{2,10},{3,11},{4,12},{5,13},{6,14},{7,15},{8,0},{9,1},... | collective-permute-start | bytes 1572872 | tf_op jit(solution)/shard_map/ppermute | solution.py:41
  63.4 6.4 %collective-permute-start.10 = (bf16[512,256]{1,0:T(8,128)(2,1)S(1)}, bf16[512,256]{1,0:T(8,128)(2,1)S(1)}, u32[]{:S(2)}, u32[]{:S(2)}) collective-permute-start(bf16[512,256]{1,0:T(8,128)(2,1)S(1)} %collective-permute-done.9.zf), channel_id=1, source_target_pairs={{0,8},{1,9},{2,10},{3,11},{4,12},{5,13},{6,14},{7,15},{8,0},{9,1},... | collective-permute-start | bytes 786440 | tf_op jit(solution)/shard_map/ppermute | solution.py:41
  66.4 32.6 %copy-start.1 = (f32[512,1,1,256]{3,2,1,0:T(1,128)S(1)}, f32[512,1,1,256]{3,2,1,0:T(1,128)}, u32[]{:S(2)}) copy-start(f32[512,1,1,256]{3,2,1,0:T(1,128)} %param.8) | copy-start | bytes 1572868
  66.4 32.6 %copy-start.2 = (bf16[512,512]{1,0:T(8,128)(2,1)S(1)}, bf16[512,512]{1,0:T(8,128)(2,1)}, u32[]{:S(2)}) copy-start(bf16[512,512]{1,0:T(8,128)(2,1)} %constant.2.clone.h_hbm.h_ref) | copy-start | bytes 1572868
  66.4 32.7 %copy-start.3 = (f32[512,1,1,256]{3,2,1,0:T(1,128)S(1)}, f32[512,1,1,256]{3,2,1,0:T(1,128)}, u32[]{:S(2)}) copy-start(f32[512,1,1,256]{3,2,1,0:T(1,128)} %param.9) | copy-start | bytes 1572868
  66.4 32.7 %copy-start.4 = (f32[512,1,1,256]{3,2,1,0:T(1,128)S(1)}, f32[512,1,1,256]{3,2,1,0:T(1,128)}, u32[]{:S(2)}) copy-start(f32[512,1,1,256]{3,2,1,0:T(1,128)} %param.10) | copy-start | bytes 1572868
  66.4 10.7 %collective-permute-start.29 = (bf16[512,256]{1,0:T(8,128)(2,1)S(1)}, bf16[512,256]{1,0:T(8,128)(2,1)S(1)}, u32[]{:S(2)}, u32[]{:S(2)}) collective-permute-start(bf16[512,256]{1,0:T(8,128)(2,1)S(1)} %get-tuple-element.34), channel_id=1, source_target_pairs={{0,16},{1,17},{2,18},{3,19},{4,20},{5,21},{6,22},{7,23},{8,24},{9,... | collective-permute-start | bytes 786440 | tf_op jit(solution)/shard_map/ppermute | solution.py:41
  69.5 29.4 %collective-permute-start.24 = (bf16[2,512,256]{2,1,0:T(8,128)(2,1)S(1)}, bf16[2,512,256]{2,1,0:T(8,128)(2,1)S(1)}, u32[]{:S(2)}, u32[]{:S(2)}) collective-permute-start(bf16[2,512,256]{2,1,0:T(8,128)(2,1)S(1)} %collective-permute-done.23.pair), channel_id=1, source_target_pairs={{0,8},{1,9},{2,10},{3,11},{4,12},{5,13},{6,14},{7,15},{8,0},{9,1},... | collective-permute-start | bytes 1572872 | tf_op jit(solution)/shard_map/ppermute | solution.py:41
  74.4 14.6 %collective-permute-start.11 = (bf16[2,128,512]{2,1,0:T(8,128)(2,1)S(1)}, bf16[2,128,512]{2,1,0:T(8,128)(2,1)S(1)}, u32[]{:S(2)}, u32[]{:S(2)}) collective-permute-start(bf16[2,128,512]{2,1,0:T(8,128)(2,1)S(1)} %get-tuple-element.23), channel_id=1, source_target_pairs={{0,1},{1,2},{2,3},{3,0},{4,5},{5,6},{6,7},{7,4},{8,9},{9,10},{10,1... | collective-permute-start | bytes 786440 | tf_op jit(solution)/shard_map/ppermute | solution.py:41
  74.4 15.1 %collective-permute-start.12 = (bf16[2,128,512]{2,1,0:T(8,128)(2,1)S(1)}, bf16[2,128,512]{2,1,0:T(8,128)(2,1)S(1)}, u32[]{:S(2)}, u32[]{:S(2)}) collective-permute-start(bf16[2,128,512]{2,1,0:T(8,128)(2,1)S(1)} %get-tuple-element.24), channel_id=1, source_target_pairs={{0,3},{1,0},{2,1},{3,2},{4,7},{5,4},{6,5},{7,6},{8,11},{9,8},{10,9... | collective-permute-start | bytes 786440 | tf_op jit(solution)/shard_map/ppermute | solution.py:41
  77.1 12.4 %collective-permute-start.13 = (bf16[2,128,512]{2,1,0:T(8,128)(2,1)S(1)}, bf16[2,128,512]{2,1,0:T(8,128)(2,1)S(1)}, u32[]{:S(2)}, u32[]{:S(2)}) collective-permute-start(bf16[2,128,512]{2,1,0:T(8,128)(2,1)S(1)} %get-tuple-element.25), channel_id=1, source_target_pairs={{0,2},{1,3},{2,0},{3,1},{4,6},{5,7},{6,4},{7,5},{8,10},{9,11},{10,... | collective-permute-start | bytes 786440 | tf_op jit(solution)/shard_map/ppermute | solution.py:41
  77.2 21.8 %collective-permute-start.30 = (bf16[512,256]{1,0:T(8,128)(2,1)S(1)}, bf16[512,256]{1,0:T(8,128)(2,1)S(1)}, u32[]{:S(2)}, u32[]{:S(2)}) collective-permute-start(bf16[512,256]{1,0:T(8,128)(2,1)S(1)} %shard_map.108), channel_id=1, source_target_pairs={{0,64},{1,65},{2,66},{3,67},{4,68},{5,69},{6,70},{7,71},{8,72},{9,... | collective-permute-start | bytes 786440 | tf_op jit(solution)/shard_map/ppermute | solution.py:41
  88.9 10.1 %collective-permute-start.28 = (bf16[512,256]{1,0:T(8,128)(2,1)S(1)}, bf16[512,256]{1,0:T(8,128)(2,1)S(1)}, u32[]{:S(2)}, u32[]{:S(2)}) collective-permute-start(bf16[512,256]{1,0:T(8,128)(2,1)S(1)} %shard_map.107), channel_id=1, source_target_pairs={{0,16},{1,17},{2,18},{3,19},{4,20},{5,21},{6,22},{7,23},{8,24},{9,... | collective-permute-start | bytes 786440 | tf_op jit(solution)/shard_map/ppermute | solution.py:41
  89.6 8.6 %collective-permute-start.14 = (bf16[128,512]{1,0:T(8,128)(2,1)S(1)}, bf16[128,512]{1,0:T(8,128)(2,1)S(1)}, u32[]{:S(2)}, u32[]{:S(2)}) collective-permute-start(bf16[128,512]{1,0:T(8,128)(2,1)S(1)} %get-tuple-element.27), channel_id=1, source_target_pairs={{0,4},{1,5},{2,6},{3,7},{4,0},{5,1},{6,2},{7,3},{8,12},{9,13},{10,... | collective-permute-start | bytes 393224 | tf_op jit(solution)/shard_map/ppermute | solution.py:41

commit v4 on v3

--- a/solution.py
+++ b/solution.py
@@ -105,14 +105,20 @@
     pack_body(a_ref, b_ref, o_ref)
 
 
+def pack_more_body(pair_ref, b_ref, o_ref):
+    o_ref[:2] = pair_ref[...]
+    o_ref[2] = b_ref[...]
+
+
 def cut_body(pair_ref, o_ref):
     o_ref[...] = pair_ref[0]
 
 
 def place_body(*refs):
-    for place, ref in zip(((0, 0), (0, 3), (0, 1), (0, 2), (1, 0), (1, 3), (1, 1), (1, 2)), refs):
-        at = pl.multiple_of(head_at(*place) * 128, 128)
-        refs[-1][:, pl.ds(at, 128)] = ref[...]
+    for dy, ref in zip((0, 3, 2, 1), refs):
+        for dl in range(NZL):
+            at = pl.multiple_of(head_at(dl, dy) * 128, 128)
+            refs[-1][:, pl.ds(at, 128)] = ref[dl]
 
 
 def turned_block(l_ref, g_ref, block):
@@ -160,13 +166,13 @@
     return total
 
 
-def latent_body(g_ref, p0, x, xs, f, fs, z, zs, zx, zxs, zf, zfs, *refs):
+def latent_body(g_ref, p0, x, xs, z, zs, zx, zxs, zf, zfs, *refs):
     core = my_core()
     rest = 1 - core
     up, down = ahead(core), ahead(rest)
     terms = [
         (p0[0], 0, 0, core), (p0[1], 0, 0, rest), (x[0], down, 0, core), (x[1], down, 0, rest),
-        (xs[0], up, 0, rest), (xs[1], up, 0, core), (f[...], 2, 0, core), (fs[...], 2, 0, rest),
+        (xs[0], up, 0, rest), (xs[1], up, 0, core), (x[2], 2, 0, core), (xs[2], 2, 0, rest),
         (z[...], 0, 1, core), (zs[...], 0, 1, rest), (zx[0], down, 1, core), (zx[1], down, 1, rest),
         (zxs[0], up, 1, rest), (zxs[1], up, 1, core), (zf[...], 2, 1, core), (zfs[...], 2, 1, rest),
     ]
@@ -246,13 +252,10 @@
         ],
     )
     l_z = send(turn, dl=1)
-    l_up = send(turn, dy=1)
-    l_dn = send(turn, dy=-1)
-    l_2 = send(l_up, dy=1)
-    lz_up = send(l_z, dy=1)
-    lz_dn = send(l_z, dy=-1)
-    lz_2 = send(lz_dn, dy=-1)
-    rows = (turn, l_up, l_dn, l_2, l_z, lz_up, lz_dn, lz_2)
+    (both,) = run(pack_body, [((2, LATENT, 128), BF)], turn, l_z)
+    l_up = send(both, dy=1)
+    l_dn = send(both, dy=-1)
+    l_2 = send(both, dy=2)
 
     pair = [((2, *block), BF)]
     (w_pair,) = run(
@@ -267,14 +270,12 @@
     w_zx = send(wz_pair, fan_x=1)
     w_2 = send(run(cut_body, one, w_x)[0], fan_x=1)
     w_2z = send(w_2, dz=1)
-    ws = [
-        w_pair, w_x, send(w_x, dc=1), w_2, send(w_2, dc=1), w_z, w_zs,
-        w_zx, send(w_zx, dc=1),
-    ]
+    (w_row,) = run(pack_more_body, [((3, *block), BF)], w_x, w_2)
+    ws = [w_pair, w_row, send(w_row, dc=1), w_z, w_zs, w_zx, send(w_zx, dc=1)]
 
     (grads,) = run(swap_body, [((16, TOK, COLS), BF)], out_grad[:, :, 0, :])
 
-    (turn,) = run(place_body, [((LATENT, TOK), BF)], *rows)
+    (turn,) = run(place_body, [((LATENT, TOK), BF)], both, l_up, l_2, l_dn)
     (give,) = run(give_body(early), [((3, *block), BF)], grads, turn)
     got = send(give, dc=1)
     t_a, t_b = run(keep_body(early), pair + one, grads, turn, got)

time: 102 us -> 96.7 us (0.948)
  starting transfers between devices: 50.5 us -> 43 us
  waiting for transfers between devices: 27.3 us -> 30 us
    ppermute x31 -> x27, starting transfers between devices: 50.5 us -> 43 us  [shifted(): return lax.ppermute(value, AXES, pairs)]
    ppermute x31 -> x27, waiting for transfers between devices: 27.3 us -> 30 us  [shifted(): return lax.ppermute(value, AXES, pairs)]
    pallas_call x17 -> x19, Pallas kernels: 18.9 us -> 18.9 us  [run(): return kernel(body, outs, len(operands), **more)(*operands)]
  transfers between devices with their start and end apart: 31 -> 27, of which waited for: 9 -> 10; matrix products, arithmetic and copies ran while one was open for 0% -> 0% of each run, Pallas kernels for 13% -> 16%
where the time goes in v4:
time: 96.7 us; the launch traced here: 96.2 us
  starting transfers between devices  43 us (44%)
  waiting for transfers between devices  30 us (31%)
  Pallas kernels  18.9 us (20%)
  local copies, waits for them, and re-layouts  3.41 us (4%)
    ppermute x27, starting transfers between devices, shifted(): return lax.ppermute(value, AXES, pairs)  43 us
    ppermute x27, waiting for transfers between devices, shifted(): return lax.ppermute(value, AXES, pairs)  30 us
    pallas_call x19, Pallas kernels, run(): return kernel(body, outs, len(operands), **more)(*operands)  18.9 us
    unnamed x10, local copies, waits for them, and re-layouts  3.41 us
  transfers between devices with their start and end apart: 27, of which 10 were waited for; matrix products, arithmetic and copies ran while one was open for 0% of the time, Pallas kernels for 16%

profile of v4, /device:TPU:1, one launch (start us, length us, event | category | flops | bytes accessed | tf_op | source)
XLA Modules:
  0.0 96.2 jit_solution(10913203261790474045)
XLA Ops:
  0.6 1.6 %shard_map.94 = (bf16[512,256]{1,0:T(8,128)(2,1)S(1)}, bf16[512,128]{1,0:T(8,128)(2,1)S(1)}) custom-call(bf16[512,512]{1,0:T(8,128)(2,1)} %constant.2.clone.h_hbm.h_ref, bf16[128,512]{1,0:T(8,128)(2,1)} %l_hbm.1, f32[1024,128]{1,0:T(8,128)} %bitcast.9), custom_call_target="tpu_custom_call" | custom-call | tf_op jit(solution)/shard_map/pallas_call | solution.py:230
  2.2 2.5 %collective-permute-start.14 = (bf16[512,128]{1,0:T(8,128)(2,1)S(1)}, bf16[512,128]{1,0:T(8,128)(2,1)S(1)}, u32[]{:S(2)}, u32[]{:S(2)}) collective-permute-start(bf16[512,128]{1,0:T(8,128)(2,1)S(1)} %get-tuple-element.28.a_ref), channel_id=1, source_target_pairs={{0,4},{1,5},{2,6},{3,7},{4,0},{5,1},{6,2},{7,3},{8,12},{9,13},{10,... | collective-permute-start | bytes 393224 | tf_op jit(solution)/shard_map/ppermute | solution.py:41
  4.7 3.2 %collective-permute-done.14.b_ref = bf16[512,128]{1,0:T(8,128)(2,1)S(1)} collective-permute-done((bf16[512,128]{1,0:T(8,128)(2,1)S(1)}, bf16[512,128]{1,0:T(8,128)(2,1)S(1)}, u32[]{:S(2)}, u32[]{:S(2)}) %collective-permute-start.14) | collective-permute-done | bytes 131104 | tf_op jit(solution)/shard_map/ppermute | solution.py:41
  8.0 1.3 %collective-permute-start.15 = (bf16[2,512,128]{2,1,0:T(8,128)(2,1)S(1)}, bf16[2,512,128]{2,1,0:T(8,128)(2,1)S(1)}, u32[]{:S(2)}, u32[]{:S(2)}) collective-permute-start(bf16[2,512,128]{2,1,0:T(8,128)(2,1)S(1)} %shard_map.102.refs_0_), channel_id=1, source_target_pairs={{0,1},{1,2},{2,3},{3,0},{4,5},{5,6},{6,7},{7,4},{8,9},{9,10},{10,1... | collective-permute-start | bytes 786440 | tf_op jit(solution)/shard_map/ppermute | solution.py:41
  9.2 2.6 %collective-permute-start.16 = (bf16[2,512,128]{2,1,0:T(8,128)(2,1)S(1)}, bf16[2,512,128]{2,1,0:T(8,128)(2,1)S(1)}, u32[]{:S(2)}, u32[]{:S(2)}) collective-permute-start(bf16[2,512,128]{2,1,0:T(8,128)(2,1)S(1)} %shard_map.102.refs_0_), channel_id=1, source_target_pairs={{0,2},{1,3},{2,0},{3,1},{4,6},{5,7},{6,4},{7,5},{8,10},{9,11},{10,... | collective-permute-start | bytes 786440 | tf_op jit(solution)/shard_map/ppermute | solution.py:41
  11.8 1.1 %collective-permute-start.17 = (bf16[2,512,128]{2,1,0:T(8,128)(2,1)S(1)}, bf16[2,512,128]{2,1,0:T(8,128)(2,1)S(1)}, u32[]{:S(2)}, u32[]{:S(2)}) collective-permute-start(bf16[2,512,128]{2,1,0:T(8,128)(2,1)S(1)} %shard_map.102.refs_0_), channel_id=1, source_target_pairs={{0,3},{1,0},{2,1},{3,2},{4,7},{5,4},{6,5},{7,6},{8,11},{9,8},{10,9... | collective-permute-start | bytes 786440 | tf_op jit(solution)/shard_map/ppermute | solution.py:41
  12.9 2.2 %collective-permute-start = (bf16[512,256]{1,0:T(8,128)(2,1)S(1)}, bf16[512,256]{1,0:T(8,128)(2,1)S(1)}, u32[]{:S(2)}, u32[]{:S(2)}) collective-permute-start(bf16[512,256]{1,0:T(8,128)(2,1)S(1)} %get-tuple-element.21.a_ref), channel_id=1, source_target_pairs={{0,8},{1,9},{2,10},{3,11},{4,12},{5,13},{6,14},{7,15},{8,0},{9,1},... | collective-permute-start | bytes 786440 | tf_op jit(solution)/shard_map/ppermute | solution.py:41
  15.1 3.4 %copy-done = bf16[1024,16,1,256]{3,1,2,0:T(8,128)(2,1)S(1)} copy-done((bf16[1024,16,1,256]{3,1,2,0:T(8,128)(2,1)S(1)}, bf16[1024,16,1,256]{3,1,2,0:T(8,128)(2,1)}, u32[]{:S(2)}) %copy-start) | copy-done | bytes 8388632
  18.5 2.1 %shard_map.93.g_ref = bf16[16,1024,256]{2,1,0:T(8,128)(2,1)S(1)} custom-call(bf16[1024,16,256]{2,1,0:T(8,128)(2,1)S(1)} %bitcast.8), custom_call_target="tpu_custom_call" | custom-call | tf_op jit(solution)/shard_map/pallas_call | solution.py:230
  20.6 0.0 collective-permute-done.15.refs_1_
  20.6 1.9 %collective-permute-done.16.refs_2_ = bf16[2,512,128]{2,1,0:T(8,128)(2,1)S(1)} collective-permute-done((bf16[2,512,128]{2,1,0:T(8,128)(2,1)S(1)}, bf16[2,512,128]{2,1,0:T(8,128)(2,1)S(1)}, u32[]{:S(2)}, u32[]{:S(2)}) %collective-permute-start.16) | collective-permute-done | bytes 262176 | tf_op jit(solution)/shard_map/ppermute | solution.py:41
  22.5 0.0 collective-permute-done.17.refs_3_
  22.5 0.3 shard_map.103.l_ref
  22.8 2.0 %shard_map.104 = bf16[5,512,256]{2,1,0:T(8,128)(2,1)S(1)} custom-call(bf16[16,1024,256]{2,1,0:T(8,128)(2,1)S(1)} %shard_map.93.g_ref, bf16[512,1024]{1,0:T(8,128)(2,1)S(1)} %shard_map.103.l_ref), custom_call_target="tpu_custom_call" | custom-call | tf_op jit(solution)/shard_map/pallas_call | solution.py:230
  24.8 2.3 %collective-permute-start.18 = (bf16[5,512,256]{2,1,0:T(8,128)(2,1)S(1)}, bf16[5,512,256]{2,1,0:T(8,128)(2,1)S(1)}, u32[]{:S(2)}, u32[]{:S(2)}) collective-permute-start(bf16[5,512,256]{2,1,0:T(8,128)(2,1)S(1)} %shard_map.104), channel_id=1, source_target_pairs={{0,8},{1,9},{2,10},{3,11},{4,12},{5,13},{6,14},{7,15},{8,0},{9,1},... | collective-permute-start | bytes 3932168 | tf_op jit(solution)/shard_map/ppermute | solution.py:41
  27.1 3.2 %collective-permute-start.4 = (bf16[512,256]{1,0:T(8,128)(2,1)S(1)}, bf16[512,256]{1,0:T(8,128)(2,1)S(1)}, u32[]{:S(2)}, u32[]{:S(2)}) collective-permute-start(bf16[512,256]{1,0:T(8,128)(2,1)S(1)} %get-tuple-element.21.a_ref), channel_id=1, source_target_pairs={{0,16},{1,17},{2,18},{3,19},{4,20},{5,21},{6,22},{7,23},{8,24},{9,... | collective-permute-start | bytes 786440 | tf_op jit(solution)/shard_map/ppermute | solution.py:41
  30.3 1.2 %shard_map.107 = bf16[3,512,256]{2,1,0:T(8,128)(2,1)S(1)} custom-call(bf16[16,1024,256]{2,1,0:T(8,128)(2,1)S(1)} %shard_map.93.g_ref, bf16[512,1024]{1,0:T(8,128)(2,1)S(1)} %shard_map.103.l_ref), custom_call_target="tpu_custom_call" | custom-call | tf_op jit(solution)/shard_map/pallas_call | solution.py:230
  31.5 0.5 collective-permute-start.21
  32.0 0.0 collective-permute-done.b_ref
  32.0 2.5 %collective-permute-start.1 = (bf16[2,512,256]{2,1,0:T(8,128)(2,1)S(1)}, bf16[2,512,256]{2,1,0:T(8,128)(2,1)S(1)}, u32[]{:S(2)}, u32[]{:S(2)}) collective-permute-start(bf16[2,512,256]{2,1,0:T(8,128)(2,1)S(1)} %shard_map.95.p0), channel_id=1, source_target_pairs={{0,32},{1,33},{2,34},{3,35},{4,36},{5,37},{6,38},{7,39},{8,104},{9... | collective-permute-start | bytes 1572872 | tf_op jit(solution)/shard_map/ppermute | solution.py:41
  34.6 2.3 %collective-permute-done.4.a_ref.z = bf16[512,256]{1,0:T(8,128)(2,1)S(1)} collective-permute-done((bf16[512,256]{1,0:T(8,128)(2,1)S(1)}, bf16[512,256]{1,0:T(8,128)(2,1)S(1)}, u32[]{:S(2)}, u32[]{:S(2)}) %collective-permute-start.4) | collective-permute-done | bytes 262176 | tf_op jit(solution)/shard_map/ppermute | solution.py:41
  36.9 0.7 collective-permute-start.5
  37.6 1.2 %collective-permute-done.5.b_ref.zs = bf16[512,256]{1,0:T(8,128)(2,1)S(1)} collective-permute-done((bf16[512,256]{1,0:T(8,128)(2,1)S(1)}, bf16[512,256]{1,0:T(8,128)(2,1)S(1)}, u32[]{:S(2)}, u32[]{:S(2)}) %collective-permute-start.5) | collective-permute-done | bytes 262176 | tf_op jit(solution)/shard_map/ppermute | solution.py:41
  38.8 2.5 %collective-permute-start.6 = (bf16[2,512,256]{2,1,0:T(8,128)(2,1)S(1)}, bf16[2,512,256]{2,1,0:T(8,128)(2,1)S(1)}, u32[]{:S(2)}, u32[]{:S(2)}) collective-permute-start(bf16[2,512,256]{2,1,0:T(8,128)(2,1)S(1)} %shard_map.98), channel_id=1, source_target_pairs={{0,32},{1,33},{2,34},{3,35},{4,36},{5,37},{6,38},{7,39},{8,104},{9... | collective-permute-start | bytes 1572872 | tf_op jit(solution)/shard_map/ppermute | solution.py:41
  41.3 0.0 collective-permute-done.1.pair_ref
  41.3 2.6 %collective-permute-start.2 = (bf16[512,256]{1,0:T(8,128)(2,1)S(1)}, bf16[512,256]{1,0:T(8,128)(2,1)S(1)}, u32[]{:S(2)}, u32[]{:S(2)}) collective-permute-start(bf16[512,256]{1,0:T(8,128)(2,1)S(1)} %shard_map.96), channel_id=1, source_target_pairs={{0,32},{1,33},{2,34},{3,35},{4,36},{5,37},{6,38},{7,39},{8,104},{9... | collective-permute-start | bytes 786440 | tf_op jit(solution)/shard_map/ppermute | solution.py:41
  43.9 1.5 %shard_map.108 = (bf16[2,512,256]{2,1,0:T(8,128)(2,1)S(1)}, bf16[512,256]{1,0:T(8,128)(2,1)S(1)}) custom-call(bf16[16,1024,256]{2,1,0:T(8,128)(2,1)S(1)} %shard_map.93.g_ref, bf16[512,1024]{1,0:T(8,128)(2,1)S(1)} %shard_map.103.l_ref, bf16[3,512,256]{2,1,0:T(8,128)(2,1)S(1)} %collective-permute-done.21.r_ref), custom_call_target="tpu_custom_call" | custom-call | tf_op jit(solution)/shard_map/pallas_call | solution.py:230
  45.4 0.1 collective-permute-start.22
  45.5 4.7 %collective-permute-done.2.b_ref = bf16[512,256]{1,0:T(8,128)(2,1)S(1)} collective-permute-done((bf16[512,256]{1,0:T(8,128)(2,1)S(1)}, bf16[512,256]{1,0:T(8,128)(2,1)S(1)}, u32[]{:S(2)}, u32[]{:S(2)}) %collective-permute-start.2) | collective-permute-done | bytes 262176 | tf_op jit(solution)/shard_map/ppermute | solution.py:41
  50.2 0.1 shard_map.97.x
  50.3 2.2 %collective-permute-start.3 = (bf16[3,512,256]{2,1,0:T(8,128)(2,1)S(1)}, bf16[3,512,256]{2,1,0:T(8,128)(2,1)S(1)}, u32[]{:S(2)}, u32[]{:S(2)}) collective-permute-start(bf16[3,512,256]{2,1,0:T(8,128)(2,1)S(1)} %shard_map.97.x), channel_id=1, source_target_pairs={{0,8},{1,9},{2,10},{3,11},{4,12},{5,13},{6,14},{7,15},{8,0},{9,1},... | collective-permute-start | bytes 2359304 | tf_op jit(solution)/shard_map/ppermute | solution.py:41
  52.5 0.0 collective-permute-done.6.zx
  52.5 0.1 collective-permute-start.7
  52.6 3.0 %collective-permute-start.8 = (bf16[512,256]{1,0:T(8,128)(2,1)S(1)}, bf16[512,256]{1,0:T(8,128)(2,1)S(1)}, u32[]{:S(2)}, u32[]{:S(2)}) collective-permute-start(bf16[512,256]{1,0:T(8,128)(2,1)S(1)} %collective-permute-done.2.b_ref), channel_id=1, source_target_pairs={{0,16},{1,17},{2,18},{3,19},{4,20},{5,21},{6,22},{7,23},{8,24},{9,... | collective-permute-start | bytes 786440 | tf_op jit(solution)/shard_map/ppermute | solution.py:41
  55.6 0.0 collective-permute-done.18.r_ref
  55.6 2.5 %shard_map.105 = (bf16[2,512,256]{2,1,0:T(8,128)(2,1)S(1)}, bf16[512,256]{1,0:T(8,128)(2,1)S(1)}, bf16[512,256]{1,0:T(8,128)(2,1)S(1)}, bf16[512,256]{1,0:T(8,128)(2,1)S(1)}) custom-call(bf16[16,1024,256]{2,1,0:T(8,128)(2,1)S(1)} %shard_map.93.g_ref, bf16[512,1024]{1,0:T(8,128)(2,1)S(1)} %shard_map.103.l_ref, ...), custom_call_target="tpu_custom_call" | custom-call | tf_op jit(solution)/shard_map/pallas_call | solution.py:230
  58.1 1.4 %collective-permute-start.19 = (bf16[2,512,256]{2,1,0:T(8,128)(2,1)S(1)}, bf16[2,512,256]{2,1,0:T(8,128)(2,1)S(1)}, u32[]{:S(2)}, u32[]{:S(2)}) collective-permute-start(bf16[2,512,256]{2,1,0:T(8,128)(2,1)S(1)} %get-tuple-element.30), channel_id=1, source_target_pairs={{0,32},{1,33},{2,34},{3,35},{4,36},{5,37},{6,38},{7,39},{8,104},{9... | collective-permute-start | bytes 1572872 | tf_op jit(solution)/shard_map/ppermute | solution.py:41
  59.5 2.1 %collective-permute-done.8.zf = bf16[512,256]{1,0:T(8,128)(2,1)S(1)} collective-permute-done((bf16[512,256]{1,0:T(8,128)(2,1)S(1)}, bf16[512,256]{1,0:T(8,128)(2,1)S(1)}, u32[]{:S(2)}, u32[]{:S(2)}) %collective-permute-start.8) | collective-permute-done | bytes 262176 | tf_op jit(solution)/shard_map/ppermute | solution.py:41
  61.6 1.3 %collective-permute-start.9 = (bf16[512,256]{1,0:T(8,128)(2,1)S(1)}, bf16[512,256]{1,0:T(8,128)(2,1)S(1)}, u32[]{:S(2)}, u32[]{:S(2)}) collective-permute-start(bf16[512,256]{1,0:T(8,128)(2,1)S(1)} %collective-permute-done.8.zf), channel_id=1, source_target_pairs={{0,8},{1,9},{2,10},{3,11},{4,12},{5,13},{6,14},{7,15},{8,0},{9,1},... | collective-permute-start | bytes 786440 | tf_op jit(solution)/shard_map/ppermute | solution.py:41
  62.9 0.0 collective-permute-done.22.pair
  62.9 0.0 collective-permute-start.23
  62.9 0.0 collective-permute-done.7.zxs
  62.9 0.0 copy-start.1
  62.9 0.0 copy-start.2
  62.9 0.0 copy-start.3
  62.9 0.0 copy-start.4
  62.9 3.0 %collective-permute-start.25 = (bf16[512,256]{1,0:T(8,128)(2,1)S(1)}, bf16[512,256]{1,0:T(8,128)(2,1)S(1)}, u32[]{:S(2)}, u32[]{:S(2)}) collective-permute-start(bf16[512,256]{1,0:T(8,128)(2,1)S(1)} %get-tuple-element.34), channel_id=1, source_target_pairs={{0,16},{1,17},{2,18},{3,19},{4,20},{5,21},{6,22},{7,23},{8,24},{9,... | collective-permute-start | bytes 786440 | tf_op jit(solution)/shard_map/ppermute | solution.py:41
  66.0 0.5 collective-permute-done.19.pair
  66.5 2.8 %collective-permute-start.20 = (bf16[2,512,256]{2,1,0:T(8,128)(2,1)S(1)}, bf16[2,512,256]{2,1,0:T(8,128)(2,1)S(1)}, u32[]{:S(2)}, u32[]{:S(2)}) collective-permute-start(bf16[2,512,256]{2,1,0:T(8,128)(2,1)S(1)} %collective-permute-done.19.pair), channel_id=1, source_target_pairs={{0,8},{1,9},{2,10},{3,11},{4,12},{5,13},{6,14},{7,15},{8,0},{9,1},... | collective-permute-start | bytes 1572872 | tf_op jit(solution)/shard_map/ppermute | solution.py:41
  69.3 4.6 %shard_map.99 = (bf16[2,128,512]{2,1,0:T(8,128)(2,1)S(1)}, bf16[2,128,512]{2,1,0:T(8,128)(2,1)S(1)}, bf16[2,128,512]{2,1,0:T(8,128)(2,1)S(1)}, bf16[2,128,512]{2,1,0:T(8,128)(2,1)S(1)}) custom-call(bf16[16,1024,256]{2,1,0:T(8,128)(2,1)S(1)} %shard_map.93.g_ref, bf16[2,512,256]{2,1,0:T(8,128)(2,1)S(1)} %shard_map.95.p0, ...), custom_call_target="tpu_custom_call" | custom-call | tf_op jit(solution)/shard_map/pallas_call | solution.py:230
  73.9 1.0 %collective-permute-start.10 = (bf16[2,128,512]{2,1,0:T(8,128)(2,1)S(1)}, bf16[2,128,512]{2,1,0:T(8,128)(2,1)S(1)}, u32[]{:S(2)}, u32[]{:S(2)}) collective-permute-start(bf16[2,128,512]{2,1,0:T(8,128)(2,1)S(1)} %get-tuple-element.23), channel_id=1, source_target_pairs={{0,1},{1,2},{2,3},{3,0},{4,5},{5,6},{6,7},{7,4},{8,9},{9,10},{10,1... | collective-permute-start | bytes 786440 | tf_op jit(solution)/shard_map/ppermute | solution.py:41
  74.9 1.7 %collective-permute-start.11 = (bf16[2,128,512]{2,1,0:T(8,128)(2,1)S(1)}, bf16[2,128,512]{2,1,0:T(8,128)(2,1)S(1)}, u32[]{:S(2)}, u32[]{:S(2)}) collective-permute-start(bf16[2,128,512]{2,1,0:T(8,128)(2,1)S(1)} %get-tuple-element.24), channel_id=1, source_target_pairs={{0,3},{1,0},{2,1},{3,2},{4,7},{5,4},{6,5},{7,6},{8,11},{9,8},{10,9... | collective-permute-start | bytes 786440 | tf_op jit(solution)/shard_map/ppermute | solution.py:41
  76.6 1.1 %collective-permute-start.12 = (bf16[2,128,512]{2,1,0:T(8,128)(2,1)S(1)}, bf16[2,128,512]{2,1,0:T(8,128)(2,1)S(1)}, u32[]{:S(2)}, u32[]{:S(2)}) collective-permute-start(bf16[2,128,512]{2,1,0:T(8,128)(2,1)S(1)} %get-tuple-element.25), channel_id=1, source_target_pairs={{0,2},{1,3},{2,0},{3,1},{4,6},{5,7},{6,4},{7,5},{8,10},{9,11},{10,... | collective-permute-start | bytes 786440 | tf_op jit(solution)/shard_map/ppermute | solution.py:41
  77.7 0.1 shard_map.110
  77.8 0.4 collective-permute-start.26
  78.2 0.1 shard_map.109
  78.3 4.7 %collective-permute-done.10.up = bf16[2,128,512]{2,1,0:T(8,128)(2,1)S(1)} collective-permute-done((bf16[2,128,512]{2,1,0:T(8,128)(2,1)S(1)}, bf16[2,128,512]{2,1,0:T(8,128)(2,1)S(1)}, u32[]{:S(2)}, u32[]{:S(2)}) %collective-permute-start.10) | collective-permute-done | bytes 262176 | tf_op jit(solution)/shard_map/ppermute | solution.py:41
  83.0 6.0 %collective-permute-done.12.far = bf16[2,128,512]{2,1,0:T(8,128)(2,1)S(1)} collective-permute-done((bf16[2,128,512]{2,1,0:T(8,128)(2,1)S(1)}, bf16[2,128,512]{2,1,0:T(8,128)(2,1)S(1)}, u32[]{:S(2)}, u32[]{:S(2)}) %collective-permute-start.12) | collective-permute-done | bytes 262176 | tf_op jit(solution)/shard_map/ppermute | solution.py:41
  89.0 0.1 shard_map.100
  89.1 0.8 collective-permute-start.13
  90.0 3.4 %collective-permute-done.13.cross = bf16[128,512]{1,0:T(8,128)(2,1)S(1)} collective-permute-done((bf16[128,512]{1,0:T(8,128)(2,1)S(1)}, bf16[128,512]{1,0:T(8,128)(2,1)S(1)}, u32[]{:S(2)}, u32[]{:S(2)}) %collective-permute-start.13) | collective-permute-done | bytes 131104 | tf_op jit(solution)/shard_map/ppermute | solution.py:41
  93.4 0.7 shard_map.101
  94.1 0.1 shard_map.106.base
  94.2 2.0 %shard_map.111 = (f32[1024,128]{1,0:T(8,128)}, f32[1024,128]{1,0:T(8,128)}, f32[1024,128]{1,0:T(8,128)}) custom-call(bf16[512,512]{1,0:T(8,128)(2,1)S(1)} %copy-done.2, f32[512,256]{1,0:T(8,128)S(1)} %shard_map.106.base, bf16[512,256]{1,0:T(8,128)(2,1)S(1)} %collective-permute-done.24.over, bf16[512,256]{1,0:T(8,128)(2,1)S(1)} %collective-permute-done.26.far, ...), custom_call_target="tpu_custom_call" | custom-call | tf_op jit(solution)/shard_map/pallas_call | solution.py:230
  (19 shorter events, 0.1 us)
Async XLA Ops:
  2.2 5.7 %collective-permute-start.14 = (bf16[512,128]{1,0:T(8,128)(2,1)S(1)}, bf16[512,128]{1,0:T(8,128)(2,1)S(1)}, u32[]{:S(2)}, u32[]{:S(2)}) collective-permute-start(bf16[512,128]{1,0:T(8,128)(2,1)S(1)} %get-tuple-element.28.a_ref), channel_id=1, source_target_pairs={{0,4},{1,5},{2,6},{3,7},{4,0},{5,1},{6,2},{7,3},{8,12},{9,13},{10,... | collective-permute-start | bytes 393224 | tf_op jit(solution)/shard_map/ppermute | solution.py:41
  8.0 12.6 %collective-permute-start.15 = (bf16[2,512,128]{2,1,0:T(8,128)(2,1)S(1)}, bf16[2,512,128]{2,1,0:T(8,128)(2,1)S(1)}, u32[]{:S(2)}, u32[]{:S(2)}) collective-permute-start(bf16[2,512,128]{2,1,0:T(8,128)(2,1)S(1)} %shard_map.102.refs_0_), channel_id=1, source_target_pairs={{0,1},{1,2},{2,3},{3,0},{4,5},{5,6},{6,7},{7,4},{8,9},{9,10},{10,1... | collective-permute-start | bytes 786440 | tf_op jit(solution)/shard_map/ppermute | solution.py:41
  9.2 13.3 %collective-permute-start.16 = (bf16[2,512,128]{2,1,0:T(8,128)(2,1)S(1)}, bf16[2,512,128]{2,1,0:T(8,128)(2,1)S(1)}, u32[]{:S(2)}, u32[]{:S(2)}) collective-permute-start(bf16[2,512,128]{2,1,0:T(8,128)(2,1)S(1)} %shard_map.102.refs_0_), channel_id=1, source_target_pairs={{0,2},{1,3},{2,0},{3,1},{4,6},{5,7},{6,4},{7,5},{8,10},{9,11},{10,... | collective-permute-start | bytes 786440 | tf_op jit(solution)/shard_map/ppermute | solution.py:41
  11.8 10.7 %collective-permute-start.17 = (bf16[2,512,128]{2,1,0:T(8,128)(2,1)S(1)}, bf16[2,512,128]{2,1,0:T(8,128)(2,1)S(1)}, u32[]{:S(2)}, u32[]{:S(2)}) collective-permute-start(bf16[2,512,128]{2,1,0:T(8,128)(2,1)S(1)} %shard_map.102.refs_0_), channel_id=1, source_target_pairs={{0,3},{1,0},{2,1},{3,2},{4,7},{5,4},{6,5},{7,6},{8,11},{9,8},{10,9... | collective-permute-start | bytes 786440 | tf_op jit(solution)/shard_map/ppermute | solution.py:41
  12.9 19.1 %collective-permute-start = (bf16[512,256]{1,0:T(8,128)(2,1)S(1)}, bf16[512,256]{1,0:T(8,128)(2,1)S(1)}, u32[]{:S(2)}, u32[]{:S(2)}) collective-permute-start(bf16[512,256]{1,0:T(8,128)(2,1)S(1)} %get-tuple-element.21.a_ref), channel_id=1, source_target_pairs={{0,8},{1,9},{2,10},{3,11},{4,12},{5,13},{6,14},{7,15},{8,0},{9,1},... | collective-permute-start | bytes 786440 | tf_op jit(solution)/shard_map/ppermute | solution.py:41
  15.1 3.4 %copy-start = (bf16[1024,16,1,256]{3,1,2,0:T(8,128)(2,1)S(1)}, bf16[1024,16,1,256]{3,1,2,0:T(8,128)(2,1)}, u32[]{:S(2)}) copy-start(bf16[1024,16,1,256]{3,1,2,0:T(8,128)(2,1)} %param.7) | copy-start | bytes 25165828
  24.8 30.9 %collective-permute-start.18 = (bf16[5,512,256]{2,1,0:T(8,128)(2,1)S(1)}, bf16[5,512,256]{2,1,0:T(8,128)(2,1)S(1)}, u32[]{:S(2)}, u32[]{:S(2)}) collective-permute-start(bf16[5,512,256]{2,1,0:T(8,128)(2,1)S(1)} %shard_map.104), channel_id=1, source_target_pairs={{0,8},{1,9},{2,10},{3,11},{4,12},{5,13},{6,14},{7,15},{8,0},{9,1},... | collective-permute-start | bytes 3932168 | tf_op jit(solution)/shard_map/ppermute | solution.py:41
  27.1 9.8 %collective-permute-start.4 = (bf16[512,256]{1,0:T(8,128)(2,1)S(1)}, bf16[512,256]{1,0:T(8,128)(2,1)S(1)}, u32[]{:S(2)}, u32[]{:S(2)}) collective-permute-start(bf16[512,256]{1,0:T(8,128)(2,1)S(1)} %get-tuple-element.21.a_ref), channel_id=1, source_target_pairs={{0,16},{1,17},{2,18},{3,19},{4,20},{5,21},{6,22},{7,23},{8,24},{9,... | collective-permute-start | bytes 786440 | tf_op jit(solution)/shard_map/ppermute | solution.py:41
  31.5 12.4 %collective-permute-start.21 = (bf16[3,512,256]{2,1,0:T(8,128)(2,1)S(1)}, bf16[3,512,256]{2,1,0:T(8,128)(2,1)S(1)}, u32[]{:S(2)}, u32[]{:S(2)}) collective-permute-start(bf16[3,512,256]{2,1,0:T(8,128)(2,1)S(1)} %shard_map.107), channel_id=1, source_target_pairs={{0,8},{1,9},{2,10},{3,11},{4,12},{5,13},{6,14},{7,15},{8,0},{9,1},... | collective-permute-start | bytes 2359304 | tf_op jit(solution)/shard_map/ppermute | solution.py:41
  32.0 9.3 %collective-permute-start.1 = (bf16[2,512,256]{2,1,0:T(8,128)(2,1)S(1)}, bf16[2,512,256]{2,1,0:T(8,128)(2,1)S(1)}, u32[]{:S(2)}, u32[]{:S(2)}) collective-permute-start(bf16[2,512,256]{2,1,0:T(8,128)(2,1)S(1)} %shard_map.95.p0), channel_id=1, source_target_pairs={{0,32},{1,33},{2,34},{3,35},{4,36},{5,37},{6,38},{7,39},{8,104},{9... | collective-permute-start | bytes 1572872 | tf_op jit(solution)/shard_map/ppermute | solution.py:41
  36.9 1.8 %collective-permute-start.5 = (bf16[512,256]{1,0:T(8,128)(2,1)S(1)}, bf16[512,256]{1,0:T(8,128)(2,1)S(1)}, u32[]{:S(2)}, u32[]{:S(2)}) collective-permute-start(bf16[512,256]{1,0:T(8,128)(2,1)S(1)} %collective-permute-done.4.a_ref.z), channel_id=1, source_target_pairs={{0,8},{1,9},{2,10},{3,11},{4,12},{5,13},{6,14},{7,15},{8,0},{9,1},... | collective-permute-start | bytes 786440 | tf_op jit(solution)/shard_map/ppermute | solution.py:41
  38.8 13.8 %collective-permute-start.6 = (bf16[2,512,256]{2,1,0:T(8,128)(2,1)S(1)}, bf16[2,512,256]{2,1,0:T(8,128)(2,1)S(1)}, u32[]{:S(2)}, u32[]{:S(2)}) collective-permute-start(bf16[2,512,256]{2,1,0:T(8,128)(2,1)S(1)} %shard_map.98), channel_id=1, source_target_pairs={{0,32},{1,33},{2,34},{3,35},{4,36},{5,37},{6,38},{7,39},{8,104},{9... | collective-permute-start | bytes 1572872 | tf_op jit(solution)/shard_map/ppermute | solution.py:41
  41.3 8.9 %collective-permute-start.2 = (bf16[512,256]{1,0:T(8,128)(2,1)S(1)}, bf16[512,256]{1,0:T(8,128)(2,1)S(1)}, u32[]{:S(2)}, u32[]{:S(2)}) collective-permute-start(bf16[512,256]{1,0:T(8,128)(2,1)S(1)} %shard_map.96), channel_id=1, source_target_pairs={{0,32},{1,33},{2,34},{3,35},{4,36},{5,37},{6,38},{7,39},{8,104},{9... | collective-permute-start | bytes 786440 | tf_op jit(solution)/shard_map/ppermute | solution.py:41
  45.4 17.4 %collective-permute-start.22 = (bf16[2,512,256]{2,1,0:T(8,128)(2,1)S(1)}, bf16[2,512,256]{2,1,0:T(8,128)(2,1)S(1)}, u32[]{:S(2)}, u32[]{:S(2)}) collective-permute-start(bf16[2,512,256]{2,1,0:T(8,128)(2,1)S(1)} %get-tuple-element.32), channel_id=1, source_target_pairs={{0,32},{1,33},{2,34},{3,35},{4,36},{5,37},{6,38},{7,39},{8,104},{9... | collective-permute-start | bytes 1572872 | tf_op jit(solution)/shard_map/ppermute | solution.py:41
  50.3 19.0 %collective-permute-start.3 = (bf16[3,512,256]{2,1,0:T(8,128)(2,1)S(1)}, bf16[3,512,256]{2,1,0:T(8,128)(2,1)S(1)}, u32[]{:S(2)}, u32[]{:S(2)}) collective-permute-start(bf16[3,512,256]{2,1,0:T(8,128)(2,1)S(1)} %shard_map.97.x), channel_id=1, source_target_pairs={{0,8},{1,9},{2,10},{3,11},{4,12},{5,13},{6,14},{7,15},{8,0},{9,1},... | collective-permute-start | bytes 2359304 | tf_op jit(solution)/shard_map/ppermute | solution.py:41
  52.5 10.3 %collective-permute-start.7 = (bf16[2,512,256]{2,1,0:T(8,128)(2,1)S(1)}, bf16[2,512,256]{2,1,0:T(8,128)(2,1)S(1)}, u32[]{:S(2)}, u32[]{:S(2)}) collective-permute-start(bf16[2,512,256]{2,1,0:T(8,128)(2,1)S(1)} %collective-permute-done.6.zx), channel_id=1, source_target_pairs={{0,8},{1,9},{2,10},{3,11},{4,12},{5,13},{6,14},{7,15},{8,0},{9,1},... | collective-permute-start | bytes 1572872 | tf_op jit(solution)/shard_map/ppermute | solution.py:41
  52.6 9.0 %collective-permute-start.8 = (bf16[512,256]{1,0:T(8,128)(2,1)S(1)}, bf16[512,256]{1,0:T(8,128)(2,1)S(1)}, u32[]{:S(2)}, u32[]{:S(2)}) collective-permute-start(bf16[512,256]{1,0:T(8,128)(2,1)S(1)} %collective-permute-done.2.b_ref), channel_id=1, source_target_pairs={{0,16},{1,17},{2,18},{3,19},{4,20},{5,21},{6,22},{7,23},{8,24},{9,... | collective-permute-start | bytes 786440 | tf_op jit(solution)/shard_map/ppermute | solution.py:41
  58.1 8.4 %collective-permute-start.19 = (bf16[2,512,256]{2,1,0:T(8,128)(2,1)S(1)}, bf16[2,512,256]{2,1,0:T(8,128)(2,1)S(1)}, u32[]{:S(2)}, u32[]{:S(2)}) collective-permute-start(bf16[2,512,256]{2,1,0:T(8,128)(2,1)S(1)} %get-tuple-element.30), channel_id=1, source_target_pairs={{0,32},{1,33},{2,34},{3,35},{4,36},{5,37},{6,38},{7,39},{8,104},{9... | collective-permute-start | bytes 1572872 | tf_op jit(solution)/shard_map/ppermute | solution.py:41
  61.6 7.7 %collective-permute-start.9 = (bf16[512,256]{1,0:T(8,128)(2,1)S(1)}, bf16[512,256]{1,0:T(8,128)(2,1)S(1)}, u32[]{:S(2)}, u32[]{:S(2)}) collective-permute-start(bf16[512,256]{1,0:T(8,128)(2,1)S(1)} %collective-permute-done.8.zf), channel_id=1, source_target_pairs={{0,8},{1,9},{2,10},{3,11},{4,12},{5,13},{6,14},{7,15},{8,0},{9,1},... | collective-permute-start | bytes 786440 | tf_op jit(solution)/shard_map/ppermute | solution.py:41
  62.9 14.9 %collective-permute-start.23 = (bf16[2,512,256]{2,1,0:T(8,128)(2,1)S(1)}, bf16[2,512,256]{2,1,0:T(8,128)(2,1)S(1)}, u32[]{:S(2)}, u32[]{:S(2)}) collective-permute-start(bf16[2,512,256]{2,1,0:T(8,128)(2,1)S(1)} %collective-permute-done.22.pair), channel_id=1, source_target_pairs={{0,8},{1,9},{2,10},{3,11},{4,12},{5,13},{6,14},{7,15},{8,0},{9,1},... | collective-permute-start | bytes 1572872 | tf_op jit(solution)/shard_map/ppermute | solution.py:41
  62.9 31.3 %copy-start.1 = (f32[512,1,1,256]{3,2,1,0:T(1,128)S(1)}, f32[512,1,1,256]{3,2,1,0:T(1,128)}, u32[]{:S(2)}) copy-start(f32[512,1,1,256]{3,2,1,0:T(1,128)} %param.8) | copy-start | bytes 1572868
  62.9 31.3 %copy-start.2 = (bf16[512,512]{1,0:T(8,128)(2,1)S(1)}, bf16[512,512]{1,0:T(8,128)(2,1)}, u32[]{:S(2)}) copy-start(bf16[512,512]{1,0:T(8,128)(2,1)} %constant.2.clone.h_hbm.h_ref) | copy-start | bytes 1572868
  62.9 31.3 %copy-start.3 = (f32[512,1,1,256]{3,2,1,0:T(1,128)S(1)}, f32[512,1,1,256]{3,2,1,0:T(1,128)}, u32[]{:S(2)}) copy-start(f32[512,1,1,256]{3,2,1,0:T(1,128)} %param.9) | copy-start | bytes 1572868
  62.9 31.3 %copy-start.4 = (f32[512,1,1,256]{3,2,1,0:T(1,128)S(1)}, f32[512,1,1,256]{3,2,1,0:T(1,128)}, u32[]{:S(2)}) copy-start(f32[512,1,1,256]{3,2,1,0:T(1,128)} %param.10) | copy-start | bytes 1572868
  62.9 13.7 %collective-permute-start.25 = (bf16[512,256]{1,0:T(8,128)(2,1)S(1)}, bf16[512,256]{1,0:T(8,128)(2,1)S(1)}, u32[]{:S(2)}, u32[]{:S(2)}) collective-permute-start(bf16[512,256]{1,0:T(8,128)(2,1)S(1)} %get-tuple-element.34), channel_id=1, source_target_pairs={{0,16},{1,17},{2,18},{3,19},{4,20},{5,21},{6,22},{7,23},{8,24},{9,... | collective-permute-start | bytes 786440 | tf_op jit(solution)/shard_map/ppermute | solution.py:41
  66.5 27.6 %collective-permute-start.20 = (bf16[2,512,256]{2,1,0:T(8,128)(2,1)S(1)}, bf16[2,512,256]{2,1,0:T(8,128)(2,1)S(1)}, u32[]{:S(2)}, u32[]{:S(2)}) collective-permute-start(bf16[2,512,256]{2,1,0:T(8,128)(2,1)S(1)} %collective-permute-done.19.pair), channel_id=1, source_target_pairs={{0,8},{1,9},{2,10},{3,11},{4,12},{5,13},{6,14},{7,15},{8,0},{9,1},... | collective-permute-start | bytes 1572872 | tf_op jit(solution)/shard_map/ppermute | solution.py:41
  73.9 9.1 %collective-permute-start.10 = (bf16[2,128,512]{2,1,0:T(8,128)(2,1)S(1)}, bf16[2,128,512]{2,1,0:T(8,128)(2,1)S(1)}, u32[]{:S(2)}, u32[]{:S(2)}) collective-permute-start(bf16[2,128,512]{2,1,0:T(8,128)(2,1)S(1)} %get-tuple-element.23), channel_id=1, source_target_pairs={{0,1},{1,2},{2,3},{3,0},{4,5},{5,6},{6,7},{7,4},{8,9},{9,10},{10,1... | collective-permute-start | bytes 786440 | tf_op jit(solution)/shard_map/ppermute | solution.py:41
  74.9 8.1 %collective-permute-start.11 = (bf16[2,128,512]{2,1,0:T(8,128)(2,1)S(1)}, bf16[2,128,512]{2,1,0:T(8,128)(2,1)S(1)}, u32[]{:S(2)}, u32[]{:S(2)}) collective-permute-start(bf16[2,128,512]{2,1,0:T(8,128)(2,1)S(1)} %get-tuple-element.24), channel_id=1, source_target_pairs={{0,3},{1,0},{2,1},{3,2},{4,7},{5,4},{6,5},{7,6},{8,11},{9,8},{10,9... | collective-permute-start | bytes 786440 | tf_op jit(solution)/shard_map/ppermute | solution.py:41
  76.6 12.4 %collective-permute-start.12 = (bf16[2,128,512]{2,1,0:T(8,128)(2,1)S(1)}, bf16[2,128,512]{2,1,0:T(8,128)(2,1)S(1)}, u32[]{:S(2)}, u32[]{:S(2)}) collective-permute-start(bf16[2,128,512]{2,1,0:T(8,128)(2,1)S(1)} %get-tuple-element.25), channel_id=1, source_target_pairs={{0,2},{1,3},{2,0},{3,1},{4,6},{5,7},{6,4},{7,5},{8,10},{9,11},{10,... | collective-permute-start | bytes 786440 | tf_op jit(solution)/shard_map/ppermute | solution.py:41
  77.8 16.4 %collective-permute-start.26 = (bf16[512,256]{1,0:T(8,128)(2,1)S(1)}, bf16[512,256]{1,0:T(8,128)(2,1)S(1)}, u32[]{:S(2)}, u32[]{:S(2)}) collective-permute-start(bf16[512,256]{1,0:T(8,128)(2,1)S(1)} %shard_map.110), channel_id=1, source_target_pairs={{0,64},{1,65},{2,66},{3,67},{4,68},{5,69},{6,70},{7,71},{8,72},{9,... | collective-permute-start | bytes 786440 | tf_op jit(solution)/shard_map/ppermute | solution.py:41
  83.0 11.2 %collective-permute-start.24 = (bf16[512,256]{1,0:T(8,128)(2,1)S(1)}, bf16[512,256]{1,0:T(8,128)(2,1)S(1)}, u32[]{:S(2)}, u32[]{:S(2)}) collective-permute-start(bf16[512,256]{1,0:T(8,128)(2,1)S(1)} %shard_map.109), channel_id=1, source_target_pairs={{0,16},{1,17},{2,18},{3,19},{4,20},{5,21},{6,22},{7,23},{8,24},{9,... | collective-permute-start | bytes 786440 | tf_op jit(solution)/shard_map/ppermute | solution.py:41
  89.1 4.3 %collective-permute-start.13 = (bf16[128,512]{1,0:T(8,128)(2,1)S(1)}, bf16[128,512]{1,0:T(8,128)(2,1)S(1)}, u32[]{:S(2)}, u32[]{:S(2)}) collective-permute-start(bf16[128,512]{1,0:T(8,128)(2,1)S(1)} %get-tuple-element.27), channel_id=1, source_target_pairs={{0,4},{1,5},{2,6},{3,7},{4,0},{5,1},{6,2},{7,3},{8,12},{9,13},{10,... | collective-permute-start | bytes 393224 | tf_op jit(solution)/shard_map/ppermute | solution.py:41
